TPU v7x, 512 devices: a whole 4x8x8 slice. The times are simulated.
512 devices in a mesh: seq: 128 (over y, z, core), head: 4 (over x).
Axes of the slice: x: 4, y: 8, z: 8, core: 2. Of those that a mesh axis runs over, the one named last changes fastest.
Arguments:
- queries: bfloat16 [16384, 4096], P('seq', 'head'), may hold values from -6 to 6
- keys: bfloat16 [16384, 4096], P('seq', 'head'), may hold values from -6 to 6
- values: bfloat16 [16384, 4096], P('seq', 'head'), may hold values from -6 to 6
- hidden: bfloat16 [16384, 2048], P('seq', 'head'), may hold values from -6 to 6
- gate_weight: bfloat16 [2048, 256], P('head'), may hold values from -0.125 to 0.125
- level_slot: int32 [8], replicated, may hold values from 0 to 7, each once
- out_grad: bfloat16 [16384, 4096], P('seq', 'head'), may hold values from -6 to 6
Outputs:
- mixed: bfloat16 [16384, 4096], P('seq', 'head')
- grad_queries: bfloat16 [16384, 4096], P('seq', 'head')
- grad_keys: bfloat16 [16384, 4096], P('seq', 'head')
- grad_values: bfloat16 [16384, 4096], P('seq', 'head')
- grad_hidden: bfloat16 [16384, 2048], P('seq', 'head')
Inputs may be any that keep to these rules, and one draw needn't show every extreme that they name: `level_slot`: each column index of a head's block appears once.
All inputs are finite; a program needn't handle non-finite values.
Results may differ from a plain program's by a relative error of at most 0.01.
Values may be sent and summed in bfloat16 or wider, within the bound.
No kernel may reach another device: no remote copies, remote signals or barrier semaphores. Data moves between devices by JAX's collectives and lax.ppermute only.
A program may use at most 64 MiB of HBM per device.

v0:
```python
import jax
import jax.numpy as jnp
from jax import lax
from jax.sharding import PartitionSpec as P

DK = 128
SPAN = 128


HIGH = lax.Precision.HIGHEST


def from_partner(block, axis, stride):
    count = lax.axis_size(axis)
    route = []
    for low in range(count):
        high = low | 1 << stride
        if high != low and high < count:
            route += [(low, high), (high, low)]
    return lax.ppermute(block, axis, route)


def local(queries, keys, values, hidden, gate_weight, level_slot, out_grad):
    tok_rows = queries.shape[0]
    heads_here = queries.shape[1] // DK
    levels = level_slot.shape[0]
    rows_here = heads_here * levels
    span_count = tok_rows // SPAN
    local_bits = span_count.bit_length() - 1
    device_bits = lax.axis_size("seq").bit_length() - 1
    seq_index = lax.axis_index("seq")
    weight_cols = lax.all_to_all(gate_weight, "head", split_axis=1, concat_axis=0, tiled=True)
    logits = lax.dot_general(
        weight_cols,
        lax.all_gather(hidden, "head", axis=1, tiled=True),
        (((0,), (1,)), ((), ())),
        preferred_element_type=jnp.float32,
    )
    slot_table = (level_slot[:, None] == jnp.arange(levels, dtype=jnp.int32)[None, :]).astype(
        jnp.float32
    )
    chosen = jnp.einsum(
        "lm,hmt->hlt", slot_table, logits.reshape(heads_here, levels, tok_rows), precision=HIGH
    )
    weights = jnp.transpose(jax.nn.softplus(chosen), (2, 0, 1))
    query_heads = queries.reshape(tok_rows, heads_here, DK)
    grad_heads = out_grad.reshape(tok_rows, heads_here, DK)
    query_blocks = queries.reshape(span_count, SPAN, heads_here, DK)
    key_blocks = keys.reshape(span_count, SPAN, heads_here, DK)
    value_blocks = values.reshape(span_count, SPAN, heads_here, DK)
    position = jnp.arange(SPAN)
    causal = (position[:, None] >= position[None, :]).astype(jnp.float32)
    scores = jnp.einsum(
        "nchd,nshd->nhcs", query_blocks, key_blocks, preferred_element_type=jnp.float32
    )
    attend = (scores * causal / SPAN).astype(jnp.bfloat16)
    intra = jnp.einsum(
        "nhcs,nshe->nche", attend, value_blocks, preferred_element_type=jnp.float32
    ).reshape(tok_rows, heads_here, DK)
    weighted = (weights[..., None] * grad_heads[:, :, None, :]).astype(jnp.bfloat16)
    device_grads = jnp.einsum(
        "thd,thje->hjde",
        query_heads,
        weighted[:, :, 1 + local_bits :],
        preferred_element_type=jnp.float32,
    )
    span_states = jnp.einsum(
        "nchd,nche->nhde", key_blocks, value_blocks, preferred_element_type=jnp.float32
    )
    device_state = span_states.sum(0)
    group = device_state
    lower_states = []
    for bit_pos in range(device_bits):
        partner = from_partner(group.astype(jnp.bfloat16), "seq", bit_pos).astype(group.dtype)
        upper_half = seq_index >> bit_pos & 1
        lower_states.append(
            jnp.where(upper_half == 1, partner, 0.0) / float((1 << bit_pos) * tok_rows)
        )
        group = group + partner
    pending = device_grads
    carried = jnp.zeros_like(device_state)
    for bit_pos in range(device_bits):
        partner_pending = from_partner(pending.astype(jnp.bfloat16), "seq", bit_pos).astype(
            pending.dtype
        )
        upper_half = seq_index >> bit_pos & 1
        scale_here = float((1 << bit_pos) * tok_rows)
        carried = carried + jnp.where(upper_half == 0, partner_pending[:, 0], 0.0) / scale_here
        pending = pending[:, 1:] + partner_pending[:, 1:]
    device_level = jnp.stack(lower_states, 1).astype(jnp.bfloat16)
    device_outs = jnp.einsum(
        "thd,hjde->tjhe", query_heads, device_level, preferred_element_type=jnp.float32
    )
    mixed = weights[:, :, 0:1] * intra + jnp.einsum(
        "thj,tjhe->the", weights[:, :, 1:], device_outs, precision=HIGH
    )
    first_grad = jnp.sum(grad_heads * intra, -1)
    later_grad = jnp.einsum(
        "the,tjhe->thj", grad_heads.astype(jnp.float32), device_outs, precision=HIGH
    )
    weight_grad = jnp.concatenate([first_grad[:, :, None], later_grad], 2)
    first_blocks = weighted[:, :, 0].reshape(span_count, SPAN, heads_here, DK)
    grad_score = (
        jnp.einsum(
            "nche,nshe->nhcs", first_blocks, value_blocks, preferred_element_type=jnp.float32
        )
        * causal
        / SPAN
    ).astype(jnp.bfloat16)
    grad_query = jnp.einsum(
        "nhcs,nshd->nchd", grad_score, key_blocks, preferred_element_type=jnp.float32
    ).reshape(tok_rows, heads_here, DK)
    grad_key = jnp.einsum(
        "nhcs,nchd->nshd", grad_score, query_blocks, preferred_element_type=jnp.float32
    ).reshape(tok_rows, heads_here, DK)
    grad_value = jnp.einsum(
        "nhcs,nche->nshe", attend, first_blocks, preferred_element_type=jnp.float32
    ).reshape(tok_rows, heads_here, DK)
    device_back = jnp.einsum(
        "the,hjde->tjhd", grad_heads, device_level, preferred_element_type=jnp.float32
    )
    grad_query = grad_query + jnp.einsum(
        "thj,tjhd->thd", weights[:, :, 1 + local_bits :], device_back, precision=HIGH
    )
    state_total = carried[None].astype(jnp.bfloat16)
    grad_key = grad_key + jnp.einsum(
        "nche,nhde->nchd", value_blocks, state_total, preferred_element_type=jnp.float32
    ).reshape(tok_rows, heads_here, DK)
    grad_value = grad_value + jnp.einsum(
        "nchd,nhde->nche", key_blocks, state_total, preferred_element_type=jnp.float32
    ).reshape(tok_rows, heads_here, DK)
    chosen_grad = jnp.transpose(weight_grad, (1, 2, 0)) * jax.nn.sigmoid(chosen)
    logit_grad = (
        jnp.einsum("lm,hlt->hmt", slot_table, chosen_grad, precision=HIGH)
        .reshape(rows_here, tok_rows)
        .astype(jnp.bfloat16)
    )
    partial_grad = lax.dot_general(
        logit_grad, weight_cols, (((0,), (1,)), ((), ())), preferred_element_type=jnp.float32
    )
    grad_hidden = lax.psum_scatter(partial_grad, "head", scatter_dimension=1, tiled=True)
    width_all = heads_here * DK
    return (
        mixed.reshape(tok_rows, width_all).astype(jnp.bfloat16),
        grad_query.reshape(tok_rows, width_all).astype(jnp.bfloat16),
        grad_key.reshape(tok_rows, width_all).astype(jnp.bfloat16),
        grad_value.reshape(tok_rows, width_all).astype(jnp.bfloat16),
        grad_hidden.astype(jnp.bfloat16),
    )


def solution(mesh):
    placed = (
        P("seq", "head"),
        P("seq", "head"),
        P("seq", "head"),
        P("seq", "head"),
        P("head", None),
        P(),
        P("seq", "head"),
    )
    return jax.shard_map(
        local,
        mesh=mesh,
        in_specs=placed,
        out_specs=(
            P("seq", "head"),
            P("seq", "head"),
            P("seq", "head"),
            P("seq", "head"),
            P("seq", "head"),
        ),
        check_vma=False,
    )
```

profile of v0, /device:TPU:1, one launch (start us, length us, event | category | flops | bytes accessed | tf_op | source)
XLA Modules:
  0.0 322.8 jit_solution(2008449599605130262)
XLA Ops:
  7.2 1.9 copy.36
  9.1 4.8 %all-to-all-start = ((bf16[512,4,64]{0,2,1:T(8,128)(2,1)}), bf16[512,4,64]{0,2,1:T(8,128)(2,1)S(1)}, u32[]{:S(2)}, u32[]{:S(2)}) async-start(bf16[512,4,64]{0,2,1:T(8,128)(2,1)} %bitcast.3), calls=%async_computation | async-start | bytes 524288 | tf_op jit(solution)/shard_map/all_to_all | solution.py:32
  13.9 1.1 copy.47
  15.0 1.1 copy.101
  16.4 12.0 %all_gather.3 = bf16[128,2048]{1,0:T(8,128)(2,1)S(1)} all-gather(bf16[128,512]{1,0:T(8,128)(2,1)S(1)} %copy-done.34), channel_id=1, replica_groups=mesh['seq'=128,'head'=4] {'head'}, dimensions={1}, use_global_device_ids=true | all-gather | bytes 655360 | tf_op jit(solution)/shard_map/all_gather | solution.py:35
  28.4 0.3 fusion.44
  29.0 1.3 multiply_convert_fusion
  30.3 3.2 fusion.114
  33.5 9.3 %collective-permute-start.7 = (bf16[8,7,128,128]{2,3,1,0:T(8,128)(2,1)}, bf16[8,7,128,128]{2,3,1,0:T(8,128)(2,1)}, u32[]{:S(2)}, u32[]{:S(2)}) collective-permute-start(bf16[8,7,128,128]{2,3,1,0:T(8,128)(2,1)} %get-tuple-element.35), channel_id=1, source_target_pairs={{0,4},{4,0},{8,12},{12,8},{16,20},{20,16},{24,28},{28,24},{32,36},... | collective-permute-start | bytes 5505032 | tf_op jit(solution)/shard_map/ppermute | solution.py:20
  43.3 0.5 copy-done.17
  43.8 1.9 collective-permute-start
  45.7 1.5 collective-permute-done
  47.3 2.2 collective-permute-start.1
  49.5 1.9 convert_element_type.195
  51.5 3.3 %fusion.111 = (bf16[8,6,128,128]{2,3,1,0:T(8,128)(2,1)}, f32[8,6,128,128]{2,3,1,0:T(8,128)}) fusion(f32[8,7,128,128]{2,3,1,0:T(8,128)S(1)} %convert_element_type.195, f32[8,7,128,128]{2,3,1,0:T(8,128)S(1)} %copy-done.2), kind=kLoop, calls=%fused_computation.155 | loop fusion | flops 1572864 | bytes 11010048 | tf_op jit(solution)/shard_map/convert_element_type | solution.py:83
  54.7 3.4 %collective-permute-start.8 = (bf16[8,6,128,128]{2,3,1,0:T(8,128)(2,1)}, bf16[8,6,128,128]{2,3,1,0:T(8,128)(2,1)}, u32[]{:S(2)}, u32[]{:S(2)}) collective-permute-start(bf16[8,6,128,128]{2,3,1,0:T(8,128)(2,1)} %get-tuple-element.23), channel_id=1, source_target_pairs={{0,8},{8,0},{4,12},{12,4},{16,24},{24,16},{20,28},{28,20},{32,40},... | collective-permute-start | bytes 4718600 | tf_op jit(solution)/shard_map/ppermute | solution.py:20
  58.2 1.9 collective-permute-start.2
  60.4 0.3 fusion.11
  60.8 36.5 %collective-permute-done.2 = bf16[8,128,128]{2,1,0:T(8,128)(2,1)S(1)} collective-permute-done((bf16[8,128,128]{2,1,0:T(8,128)(2,1)S(1)}, bf16[8,128,128]{2,1,0:T(8,128)(2,1)S(1)}, u32[]{:S(2)}, u32[]{:S(2)}) %collective-permute-start.2) | collective-permute-done | bytes 262176 | tf_op jit(solution)/shard_map/ppermute | solution.py:20
  97.4 5.9 %collective-permute-start.3 = (bf16[8,128,128]{2,1,0:T(8,128)(2,1)S(1)}, bf16[8,128,128]{2,1,0:T(8,128)(2,1)S(1)}, u32[]{:S(2)}, u32[]{:S(2)}) collective-permute-start(bf16[8,128,128]{2,1,0:T(8,128)(2,1)S(1)} %fusion.47), channel_id=1, source_target_pairs={{0,32},{32,0},{4,36},{36,4},{8,40},{40,8},{12,44},{44,12},{16,48},... | collective-permute-start | bytes 786440 | tf_op jit(solution)/shard_map/ppermute | solution.py:20
  103.5 6.3 %collective-permute-done.3 = bf16[8,128,128]{2,1,0:T(8,128)(2,1)S(1)} collective-permute-done((bf16[8,128,128]{2,1,0:T(8,128)(2,1)S(1)}, bf16[8,128,128]{2,1,0:T(8,128)(2,1)S(1)}, u32[]{:S(2)}, u32[]{:S(2)}) %collective-permute-start.3) | collective-permute-done | bytes 262176 | tf_op jit(solution)/shard_map/ppermute | solution.py:20
  110.0 2.4 collective-permute-start.4
  112.4 1.8 convert_element_type.197
  114.2 0.5 fusion.110
  114.7 11.1 %collective-permute-start.9 = (bf16[8,5,128,128]{2,3,1,0:T(8,128)(2,1)S(1)}, bf16[8,5,128,128]{2,3,1,0:T(8,128)(2,1)S(1)}, u32[]{:S(2)}, u32[]{:S(2)}) collective-permute-start(bf16[8,5,128,128]{2,3,1,0:T(8,128)(2,1)S(1)} %get-tuple-element.21), channel_id=1, source_target_pairs={{0,16},{16,0},{4,20},{20,4},{8,24},{24,8},{12,28},{28,12},{32,48},... | collective-permute-start | bytes 3932168 | tf_op jit(solution)/shard_map/ppermute | solution.py:20
  125.9 4.1 %collective-permute-start.5 = (bf16[8,128,128]{2,1,0:T(8,128)(2,1)S(1)}, bf16[8,128,128]{2,1,0:T(8,128)(2,1)S(1)}, u32[]{:S(2)}, u32[]{:S(2)}) collective-permute-start(bf16[8,128,128]{2,1,0:T(8,128)(2,1)S(1)} %fusion.48), channel_id=1, source_target_pairs={{0,128},{128,0},{4,132},{132,4},{8,136},{136,8},{12,140},{140,12},... | collective-permute-start | bytes 786440 | tf_op jit(solution)/shard_map/ppermute | solution.py:20
  130.3 11.1 %collective-permute-done.5 = bf16[8,128,128]{2,1,0:T(8,128)(2,1)S(1)} collective-permute-done((bf16[8,128,128]{2,1,0:T(8,128)(2,1)S(1)}, bf16[8,128,128]{2,1,0:T(8,128)(2,1)S(1)}, u32[]{:S(2)}, u32[]{:S(2)}) %collective-permute-start.5) | collective-permute-done | bytes 262176 | tf_op jit(solution)/shard_map/ppermute | solution.py:20
  141.5 6.8 %collective-permute-start.6 = (bf16[8,128,128]{2,1,0:T(8,128)(2,1)S(1)}, bf16[8,128,128]{2,1,0:T(8,128)(2,1)S(1)}, u32[]{:S(2)}, u32[]{:S(2)}) collective-permute-start(bf16[8,128,128]{2,1,0:T(8,128)(2,1)S(1)} %fusion.29), channel_id=1, source_target_pairs={{0,256},{256,0},{4,260},{260,4},{8,264},{264,8},{12,268},{268,12},... | collective-permute-start | bytes 786440 | tf_op jit(solution)/shard_map/ppermute | solution.py:20
  148.5 33.7 %collective-permute-done.9 = bf16[8,5,128,128]{2,3,1,0:T(8,128)(2,1)S(1)} collective-permute-done((bf16[8,5,128,128]{2,3,1,0:T(8,128)(2,1)S(1)}, bf16[8,5,128,128]{2,3,1,0:T(8,128)(2,1)S(1)}, u32[]{:S(2)}, u32[]{:S(2)}) %collective-permute-start.9) | collective-permute-done | bytes 1310752 | tf_op jit(solution)/shard_map/ppermute | solution.py:20
  182.5 0.4 fusion.109
  182.9 1.1 copy-done.4
  184.0 6.3 %collective-permute-start.10 = (bf16[8,4,128,128]{2,3,1,0:T(8,128)(2,1)S(1)}, bf16[8,4,128,128]{2,3,1,0:T(8,128)(2,1)S(1)}, u32[]{:S(2)}, u32[]{:S(2)}) collective-permute-start(bf16[8,4,128,128]{2,3,1,0:T(8,128)(2,1)S(1)} %get-tuple-element.19), channel_id=1, source_target_pairs={{0,32},{32,0},{4,36},{36,4},{8,40},{40,8},{12,44},{44,12},{16,48},... | collective-permute-start | bytes 3145736 | tf_op jit(solution)/shard_map/ppermute | solution.py:20
  190.5 0.8 fusion.2
  191.3 0.4 copy-done.14
  191.8 1.0 multiply_reduce_fusion
  192.8 0.6 fusion
  193.4 42.9 %collective-permute-done.10 = bf16[8,4,128,128]{2,3,1,0:T(8,128)(2,1)S(1)} collective-permute-done((bf16[8,4,128,128]{2,3,1,0:T(8,128)(2,1)S(1)}, bf16[8,4,128,128]{2,3,1,0:T(8,128)(2,1)S(1)}, u32[]{:S(2)}, u32[]{:S(2)}) %collective-permute-start.10) | collective-permute-done | bytes 1048608 | tf_op jit(solution)/shard_map/ppermute | solution.py:20
  236.5 1.8 fusion.108
  238.6 3.7 %collective-permute-start.11 = (bf16[8,3,128,128]{2,3,1,0:T(8,128)(2,1)}, bf16[8,3,128,128]{2,3,1,0:T(8,128)(2,1)}, u32[]{:S(2)}, u32[]{:S(2)}) collective-permute-start(bf16[8,3,128,128]{2,3,1,0:T(8,128)(2,1)} %get-tuple-element.17), channel_id=1, source_target_pairs={{0,64},{64,0},{4,68},{68,4},{8,72},{72,8},{12,76},{76,12},{16,80},... | collective-permute-start | bytes 2359304 | tf_op jit(solution)/shard_map/ppermute | solution.py:20
  242.5 1.3 fusion.115
  243.8 14.9 %collective-permute-done.11 = bf16[8,3,128,128]{2,3,1,0:T(8,128)(2,1)} collective-permute-done((bf16[8,3,128,128]{2,3,1,0:T(8,128)(2,1)}, bf16[8,3,128,128]{2,3,1,0:T(8,128)(2,1)}, u32[]{:S(2)}, u32[]{:S(2)}) %collective-permute-start.11) | collective-permute-done | bytes 786464 | tf_op jit(solution)/shard_map/ppermute | solution.py:20
  258.7 1.3 convert_element_type.203
  260.1 1.1 copy-done.7
  261.2 1.3 fusion.107
  262.5 3.0 collective-permute-start.12
  265.6 1.3 fusion.12
  267.0 2.3 fusion.74
  269.2 20.1 %collective-permute-done.12 = bf16[8,2,128,128]{2,3,1,0:T(8,128)(2,1)} collective-permute-done((bf16[8,2,128,128]{2,3,1,0:T(8,128)(2,1)}, bf16[8,2,128,128]{2,3,1,0:T(8,128)(2,1)}, u32[]{:S(2)}, u32[]{:S(2)}) %collective-permute-start.12) | collective-permute-done | bytes 524320 | tf_op jit(solution)/shard_map/ppermute | solution.py:20
  289.3 1.1 convert_element_type.205
  290.5 1.0 copy-done.11
  291.5 0.8 fusion.30
  292.3 6.1 %collective-permute-start.13 = (bf16[8,1,128,128]{2,3,1,0:T(8,128)(2,1)}, bf16[8,1,128,128]{2,3,1,0:T(8,128)(2,1)}, u32[]{:S(2)}, u32[]{:S(2)}) collective-permute-start(bf16[8,1,128,128]{2,3,1,0:T(8,128)(2,1)} %fusion.30), channel_id=1, source_target_pairs={{0,256},{256,0},{4,260},{260,4},{8,264},{264,8},{12,268},{268,12},... | collective-permute-start | bytes 786440 | tf_op jit(solution)/shard_map/ppermute | solution.py:20
  298.4 0.6 fusion.1
  299.1 0.3 copy-done.18
  299.4 1.0 fusion.15
  300.4 1.8 copy.59
  302.2 1.8 copy.58
  304.0 1.6 convert_element_type.220
  305.6 5.6 %collective-permute-done.13 = bf16[8,1,128,128]{2,3,1,0:T(8,128)(2,1)} collective-permute-done((bf16[8,1,128,128]{2,3,1,0:T(8,128)(2,1)}, bf16[8,1,128,128]{2,3,1,0:T(8,128)(2,1)}, u32[]{:S(2)}, u32[]{:S(2)}) %collective-permute-start.13) | collective-permute-done | bytes 262176 | tf_op jit(solution)/shard_map/ppermute | solution.py:20
  311.2 2.1 fusion.34
  313.3 0.3 fusion.64
  313.7 0.3 fusion.13
  314.0 0.9 copy.61
  315.1 0.9 copy.60
  (104 shorter events, 3.8 us)
Async XLA Ops:
  7.2 35.9 %copy-start = (bf16[128,1024]{1,0:T(8,128)(2,1)S(1)}, bf16[128,1024]{1,0:T(8,128)(2,1)}, u32[]{:S(2)}) copy-start(bf16[128,1024]{1,0:T(8,128)(2,1)} %param.9) | copy-start | bytes 786436
  7.2 9.2 %copy-start.34 = (bf16[128,512]{1,0:T(8,128)(2,1)S(1)}, bf16[128,512]{1,0:T(8,128)(2,1)}, u32[]{:S(2)}) copy-start(bf16[128,512]{1,0:T(8,128)(2,1)} %param.10) | copy-start | bytes 393220
  9.1 19.4 %all-to-all-start = ((bf16[512,4,64]{0,2,1:T(8,128)(2,1)}), bf16[512,4,64]{0,2,1:T(8,128)(2,1)S(1)}, u32[]{:S(2)}, u32[]{:S(2)}) async-start(bf16[512,4,64]{0,2,1:T(8,128)(2,1)} %bitcast.3), calls=%async_computation | async-start | bytes 524288 | tf_op jit(solution)/shard_map/all_to_all | solution.py:32
  13.9 290.1 %reduce-scatter.2.cloned.1.call-start = ((), (), s32[]{:S(2)}) async-start(), calls=%async_computation.2 | async-start | bytes 1310720 | tf_op jit(solution)/shard_map/reduce_scatter | solution.py:141
  15.0 13.7 %copy-start.25 = (bf16[128,1024]{0,1:T(8,128)(2,1)}, bf16[128,1024]{0,1:T(8,128)(2,1)S(1)}, u32[]{:S(2)}) copy-start(bf16[128,1024]{0,1:T(8,128)(2,1)S(1)} %copy.47) | copy-start | bytes 786436
  15.0 13.7 %copy-start.35 = (s32[8]{0:T(128)S(1)}, s32[8]{0:T(128)}, u32[]{:S(2)}) copy-start(s32[8]{0:T(128)} %param.12) | copy-start | bytes 100
  16.1 44.0 %copy-start.12 = (bf16[16,8,8,128]{3,2,1,0:T(8,128)(2,1)}, bf16[16,8,8,128]{3,2,1,0:T(8,128)(2,1)S(1)}, u32[]{:S(2)}) copy-start(bf16[16,8,8,128]{3,2,1,0:T(8,128)(2,1)S(1)} %copy.101) | copy-start | bytes 786436
  16.2 14.1 %copy-start.8 = (f32[128,8,128]{0,2,1:T(8,128)}, f32[128,8,128]{0,2,1:T(8,128)S(1)}, u32[]{:S(2)}) copy-start(f32[128,8,128]{0,2,1:T(8,128)S(1)} %bitcast_convert_fusion) | copy-start | bytes 1572868
  28.4 5.1 %copy-start.28 = (bf16[4,8,8,512]{3,2,0,1:T(8,128)(2,1)}, bf16[4,8,8,512]{3,2,0,1:T(8,128)(2,1)S(1)}, u32[]{:S(2)}) copy-start(bf16[4,8,8,512]{3,2,0,1:T(8,128)(2,1)S(1)} %copy.100) | copy-start | bytes 786436
  30.3 3.2 copy-start.6
  30.3 12.5 %copy-start.19 = (bf16[128,1024]{1,0:T(8,128)(2,1)S(1)}, bf16[128,1024]{1,0:T(8,128)(2,1)}, u32[]{:S(2)}) copy-start(bf16[128,1024]{1,0:T(8,128)(2,1)} %param.8) | copy-start | bytes 786436
  33.5 16.0 %collective-permute-start.7 = (bf16[8,7,128,128]{2,3,1,0:T(8,128)(2,1)}, bf16[8,7,128,128]{2,3,1,0:T(8,128)(2,1)}, u32[]{:S(2)}, u32[]{:S(2)}) collective-permute-start(bf16[8,7,128,128]{2,3,1,0:T(8,128)(2,1)} %get-tuple-element.35), channel_id=1, source_target_pairs={{0,4},{4,0},{8,12},{12,8},{16,20},{20,16},{24,28},{28,24},{32,36},... | collective-permute-start | bytes 5505032 | tf_op jit(solution)/shard_map/ppermute | solution.py:20
  43.1 0.7 copy-start.17
  43.8 3.4 %collective-permute-start = (bf16[8,128,128]{2,1,0:T(8,128)(2,1)S(1)}, bf16[8,128,128]{2,1,0:T(8,128)(2,1)S(1)}, u32[]{:S(2)}, u32[]{:S(2)}) collective-permute-start(bf16[8,128,128]{2,1,0:T(8,128)(2,1)S(1)} %get-tuple-element.29), channel_id=1, source_target_pairs={{0,4},{4,0},{8,12},{12,8},{16,20},{20,16},{24,28},{28,24},{32,36},... | collective-permute-start | bytes 786440 | tf_op jit(solution)/shard_map/ppermute | solution.py:20
  47.3 4.2 %copy-start.2 = (f32[8,7,128,128]{2,3,1,0:T(8,128)S(1)}, f32[8,7,128,128]{2,3,1,0:T(8,128)}, u32[]{:S(2)}) copy-start(f32[8,7,128,128]{2,3,1,0:T(8,128)} %get-tuple-element.36) | copy-start | bytes 11010052
  47.3 10.8 %collective-permute-start.1 = (bf16[8,128,128]{2,1,0:T(8,128)(2,1)S(1)}, bf16[8,128,128]{2,1,0:T(8,128)(2,1)S(1)}, u32[]{:S(2)}, u32[]{:S(2)}) collective-permute-start(bf16[8,128,128]{2,1,0:T(8,128)(2,1)S(1)} %fusion.46), channel_id=1, source_target_pairs={{0,8},{8,0},{4,12},{12,4},{16,24},{24,16},{20,28},{28,20},{32,40},... | collective-permute-start | bytes 786440 | tf_op jit(solution)/shard_map/ppermute | solution.py:20
  51.5 3.3 %copy-start.1 = (f32[8,7,128,128]{2,3,1,0:T(8,128)}, f32[8,7,128,128]{2,3,1,0:T(8,128)S(1)}, u32[]{:S(2)}) copy-start(f32[8,7,128,128]{2,3,1,0:T(8,128)S(1)} %convert_element_type.195) | copy-start | bytes 11010052
  54.7 57.6 %collective-permute-start.8 = (bf16[8,6,128,128]{2,3,1,0:T(8,128)(2,1)}, bf16[8,6,128,128]{2,3,1,0:T(8,128)(2,1)}, u32[]{:S(2)}, u32[]{:S(2)}) collective-permute-start(bf16[8,6,128,128]{2,3,1,0:T(8,128)(2,1)} %get-tuple-element.23), channel_id=1, source_target_pairs={{0,8},{8,0},{4,12},{12,4},{16,24},{24,16},{20,28},{28,20},{32,40},... | collective-permute-start | bytes 4718600 | tf_op jit(solution)/shard_map/ppermute | solution.py:20
  58.2 39.0 %collective-permute-start.2 = (bf16[8,128,128]{2,1,0:T(8,128)(2,1)S(1)}, bf16[8,128,128]{2,1,0:T(8,128)(2,1)S(1)}, u32[]{:S(2)}, u32[]{:S(2)}) collective-permute-start(bf16[8,128,128]{2,1,0:T(8,128)(2,1)S(1)} %fusion.106), channel_id=1, source_target_pairs={{0,16},{16,0},{4,20},{20,4},{8,24},{24,8},{12,28},{28,12},{32,48},... | collective-permute-start | bytes 786440 | tf_op jit(solution)/shard_map/ppermute | solution.py:20
  60.4 49.5 %copy-start.21 = (bf16[128,8,128]{0,2,1:T(8,128)(2,1)}, bf16[128,8,128]{0,2,1:T(8,128)(2,1)S(1)}, u32[]{:S(2)}) copy-start(bf16[128,8,128]{0,2,1:T(8,128)(2,1)S(1)} %copy.51) | copy-start | bytes 786436
  60.8 131.0 %copy-start.30 = (bf16[8,128,128]{2,1,0:T(8,128)(2,1)}, bf16[8,128,128]{2,1,0:T(8,128)(2,1)S(1)}, u32[]{:S(2)}) copy-start(bf16[8,128,128]{2,1,0:T(8,128)(2,1)S(1)} %fusion.11) | copy-start | bytes 786436
  97.2 12.7 %copy-start.23 = (bf16[8,128,128]{2,1,0:T(8,128)(2,1)}, bf16[8,128,128]{2,1,0:T(8,128)(2,1)S(1)}, u32[]{:S(2)}) copy-start(bf16[8,128,128]{2,1,0:T(8,128)(2,1)S(1)} %collective-permute-done.2) | copy-start | bytes 786436
  97.4 12.4 %collective-permute-start.3 = (bf16[8,128,128]{2,1,0:T(8,128)(2,1)S(1)}, bf16[8,128,128]{2,1,0:T(8,128)(2,1)S(1)}, u32[]{:S(2)}, u32[]{:S(2)}) collective-permute-start(bf16[8,128,128]{2,1,0:T(8,128)(2,1)S(1)} %fusion.47), channel_id=1, source_target_pairs={{0,32},{32,0},{4,36},{36,4},{8,40},{40,8},{12,44},{44,12},{16,48},... | collective-permute-start | bytes 786440 | tf_op jit(solution)/shard_map/ppermute | solution.py:20
  110.0 4.2 %copy-start.3 = (f32[8,6,128,128]{2,3,1,0:T(8,128)S(1)}, f32[8,6,128,128]{2,3,1,0:T(8,128)}, u32[]{:S(2)}) copy-start(f32[8,6,128,128]{2,3,1,0:T(8,128)} %get-tuple-element.24) | copy-start | bytes 9437188
  110.0 15.9 %collective-permute-start.4 = (bf16[8,128,128]{2,1,0:T(8,128)(2,1)S(1)}, bf16[8,128,128]{2,1,0:T(8,128)(2,1)S(1)}, u32[]{:S(2)}, u32[]{:S(2)}) collective-permute-start(bf16[8,128,128]{2,1,0:T(8,128)(2,1)S(1)} %get-tuple-element.25), channel_id=1, source_target_pairs={{0,64},{64,0},{4,68},{68,4},{8,72},{72,8},{12,76},{76,12},{16,80},... | collective-permute-start | bytes 786440 | tf_op jit(solution)/shard_map/ppermute | solution.py:20
  114.1 11.6 %copy-start.24 = (bf16[8,128,128]{2,1,0:T(8,128)(2,1)S(1)}, bf16[8,128,128]{2,1,0:T(8,128)(2,1)}, u32[]{:S(2)}) copy-start(bf16[8,128,128]{2,1,0:T(8,128)(2,1)} %copy-done.23) | copy-start | bytes 786436
  114.7 67.5 %collective-permute-start.9 = (bf16[8,5,128,128]{2,3,1,0:T(8,128)(2,1)S(1)}, bf16[8,5,128,128]{2,3,1,0:T(8,128)(2,1)S(1)}, u32[]{:S(2)}, u32[]{:S(2)}) collective-permute-start(bf16[8,5,128,128]{2,3,1,0:T(8,128)(2,1)S(1)} %get-tuple-element.21), channel_id=1, source_target_pairs={{0,16},{16,0},{4,20},{20,4},{8,24},{24,8},{12,28},{28,12},{32,48},... | collective-permute-start | bytes 3932168 | tf_op jit(solution)/shard_map/ppermute | solution.py:20
  125.9 15.5 %collective-permute-start.5 = (bf16[8,128,128]{2,1,0:T(8,128)(2,1)S(1)}, bf16[8,128,128]{2,1,0:T(8,128)(2,1)S(1)}, u32[]{:S(2)}, u32[]{:S(2)}) collective-permute-start(bf16[8,128,128]{2,1,0:T(8,128)(2,1)S(1)} %fusion.48), channel_id=1, source_target_pairs={{0,128},{128,0},{4,132},{132,4},{8,136},{136,8},{12,140},{140,12},... | collective-permute-start | bytes 786440 | tf_op jit(solution)/shard_map/ppermute | solution.py:20
  141.5 48.8 %collective-permute-start.6 = (bf16[8,128,128]{2,1,0:T(8,128)(2,1)S(1)}, bf16[8,128,128]{2,1,0:T(8,128)(2,1)S(1)}, u32[]{:S(2)}, u32[]{:S(2)}) collective-permute-start(bf16[8,128,128]{2,1,0:T(8,128)(2,1)S(1)} %fusion.29), channel_id=1, source_target_pairs={{0,256},{256,0},{4,260},{260,4},{8,264},{264,8},{12,268},{268,12},... | collective-permute-start | bytes 786440 | tf_op jit(solution)/shard_map/ppermute | solution.py:20
  182.5 1.5 copy-start.4
  182.5 7.9 %copy-start.13 = (bf16[16,8,8,128]{3,2,1,0:T(8,128)(2,1)S(1)}, bf16[16,8,8,128]{3,2,1,0:T(8,128)(2,1)}, u32[]{:S(2)}) copy-start(bf16[16,8,8,128]{3,2,1,0:T(8,128)(2,1)} %copy-done.12) | copy-start | bytes 786436
  184.0 52.3 %collective-permute-start.10 = (bf16[8,4,128,128]{2,3,1,0:T(8,128)(2,1)S(1)}, bf16[8,4,128,128]{2,3,1,0:T(8,128)(2,1)S(1)}, u32[]{:S(2)}, u32[]{:S(2)}) collective-permute-start(bf16[8,4,128,128]{2,3,1,0:T(8,128)(2,1)S(1)} %get-tuple-element.19), channel_id=1, source_target_pairs={{0,32},{32,0},{4,36},{36,4},{8,40},{40,8},{12,44},{44,12},{16,48},... | collective-permute-start | bytes 3145736 | tf_op jit(solution)/shard_map/ppermute | solution.py:20
  190.4 1.3 copy-start.14
  190.5 1.3 copy-start.26
  190.5 2.3 copy-start.9
  236.5 2.1 copy-start.5
  236.5 5.9 %copy-start.29 = (bf16[4,8,8,512]{3,2,0,1:T(8,128)(2,1)S(1)}, bf16[4,8,8,512]{3,2,0,1:T(8,128)(2,1)}, u32[]{:S(2)}) copy-start(bf16[4,8,8,512]{3,2,0,1:T(8,128)(2,1)} %copy-done.28) | copy-start | bytes 786436
  238.6 20.1 %collective-permute-start.11 = (bf16[8,3,128,128]{2,3,1,0:T(8,128)(2,1)}, bf16[8,3,128,128]{2,3,1,0:T(8,128)(2,1)}, u32[]{:S(2)}, u32[]{:S(2)}) collective-permute-start(bf16[8,3,128,128]{2,3,1,0:T(8,128)(2,1)} %get-tuple-element.17), channel_id=1, source_target_pairs={{0,64},{64,0},{4,68},{68,4},{8,72},{72,8},{12,76},{76,12},{16,80},... | collective-permute-start | bytes 2359304 | tf_op jit(solution)/shard_map/ppermute | solution.py:20
  243.8 17.4 %copy-start.10 = (f32[8,3,128,128]{2,3,1,0:T(8,128)S(1)}, f32[8,3,128,128]{2,3,1,0:T(8,128)}, u32[]{:S(2)}) copy-start(f32[8,3,128,128]{2,3,1,0:T(8,128)} %get-tuple-element.18) | copy-start | bytes 4718596
  260.0 1.2 copy-start.7
  262.5 26.8 %collective-permute-start.12 = (bf16[8,2,128,128]{2,3,1,0:T(8,128)(2,1)}, bf16[8,2,128,128]{2,3,1,0:T(8,128)(2,1)}, u32[]{:S(2)}, u32[]{:S(2)}) collective-permute-start(bf16[8,2,128,128]{2,3,1,0:T(8,128)(2,1)} %get-tuple-element.15), channel_id=1, source_target_pairs={{0,128},{128,0},{4,132},{132,4},{8,136},{136,8},{12,140},{140,12},... | collective-permute-start | bytes 1572872 | tf_op jit(solution)/shard_map/ppermute | solution.py:20
  265.6 25.9 %copy-start.16 = (f32[8,2,128,128]{2,3,1,0:T(8,128)S(1)}, f32[8,2,128,128]{2,3,1,0:T(8,128)}, u32[]{:S(2)}) copy-start(f32[8,2,128,128]{2,3,1,0:T(8,128)} %get-tuple-element.16) | copy-start | bytes 3145732
  266.9 32.1 %copy-start.32 = (bf16[8,128,128]{2,1,0:T(8,128)(2,1)}, bf16[8,128,128]{2,1,0:T(8,128)(2,1)S(1)}, u32[]{:S(2)}) copy-start(bf16[8,128,128]{2,1,0:T(8,128)(2,1)S(1)} %fusion.12) | copy-start | bytes 786436
  266.9 31.5 %copy-start.15 = (bf16[8,7,128,128]{3,2,0,1:T(8,128)(2,1)S(1)}, bf16[8,7,128,128]{3,2,0,1:T(8,128)(2,1)}, u32[]{:S(2)}) copy-start(bf16[8,7,128,128]{3,2,0,1:T(8,128)(2,1)} %copy-done.14) | copy-start | bytes 5505028
  266.9 31.5 %copy-start.27 = (bf16[128,1024]{0,1:T(8,128)(2,1)S(1)}, bf16[128,1024]{0,1:T(8,128)(2,1)}, u32[]{:S(2)}) copy-start(bf16[128,1024]{0,1:T(8,128)(2,1)} %copy-done.25) | copy-start | bytes 786436
  290.5 1.0 copy-start.11
  292.3 18.9 %collective-permute-start.13 = (bf16[8,1,128,128]{2,3,1,0:T(8,128)(2,1)}, bf16[8,1,128,128]{2,3,1,0:T(8,128)(2,1)}, u32[]{:S(2)}, u32[]{:S(2)}) collective-permute-start(bf16[8,1,128,128]{2,3,1,0:T(8,128)(2,1)} %fusion.30), channel_id=1, source_target_pairs={{0,256},{256,0},{4,260},{260,4},{8,264},{264,8},{12,268},{268,12},... | collective-permute-start | bytes 786440 | tf_op jit(solution)/shard_map/ppermute | solution.py:20
  298.4 1.0 copy-start.18
  305.6 8.1 %copy-start.20 = (bf16[128,1024]{1,0:T(8,128)(2,1)S(1)}, bf16[128,1024]{1,0:T(8,128)(2,1)}, u32[]{:S(2)}) copy-start(bf16[128,1024]{1,0:T(8,128)(2,1)} %param.8) | copy-start | bytes 786436
  305.6 8.1 %copy-start.31 = (f32[8,128,128]{2,1,0:T(8,128)S(1)}, f32[8,128,128]{2,1,0:T(8,128)}, u32[]{:S(2)}) copy-start(f32[8,128,128]{2,1,0:T(8,128)} %fusion.74) | copy-start | bytes 1572868
  313.3 1.5 copy-start.22
  313.3 1.5 copy-start.33
Sparse Core Ops, SparseCore 0:
  243.9 26.9 reduce-scatter.1
where the time goes:
time: 324 us; the launch traced here: 323 us
  waiting for transfers between devices  173 us (53%)
  starting transfers between devices  72.8 us (22%)
  other arithmetic  21.7 us (7%)
  between operations  15 us (5%)
  local copies, waits for them, and re-layouts  14.9 us (5%)
  matrix products  13.7 us (4%)
  blocking collectives  12 us (4%)
    ppermute x14, waiting for transfers between devices, from_partner(): return lax.ppermute(block, axis, route)  173 us
    ppermute x14, starting transfers between devices, from_partner(): return lax.ppermute(block, axis, route)  68 us
    unnamed x80, local copies, waits for them, and re-layouts  14.2 us
    all_gather x1, blocking collectives, local(): lax.all_gather(hidden, 'head', axis=1, tiled=True)  12 us
    convert_element_type x6, other arithmetic, local(): pending.astype(jnp.bfloat16)  8.11 us
    convert_element_type x6, other arithmetic, local(): from_partner(pending.astype(jnp.bfloat16), 'seq', bit_pos)  6.68 us
  transfers between devices with their start and end apart: 16, of which 9 were waited for; matrix products, arithmetic and copies ran while one was open for 10% of the time, Pallas kernels for 0%

commit v1 on v0

v1 whole, which is shorter than its diff:
```python
import jax
import jax.numpy as jnp
from jax import lax
from jax.experimental import pallas as pl
from jax.experimental.pallas import tpu as pltpu
from jax.sharding import Mesh, PartitionSpec as P

DK = 128
SPAN = 128
HALF = 4
LANES = HALF * DK
SLOTS = 6
BF = jnp.bfloat16
F32 = jnp.float32


def dot(a, b, ca, cb):
    return lax.dot_general(a, b, (((ca,), (cb,)), ((), ())), preferred_element_type=F32)


def vmem(n):
    return [pl.BlockSpec(memory_space=pltpu.VMEM)] * n


def anymem(n):
    return [pl.BlockSpec(memory_space=pl.ANY)] * n


def smem(n):
    return [pl.BlockSpec(memory_space=pltpu.SMEM)] * n


def shape(*dims, kind=BF):
    return jax.ShapeDtypeStruct(dims, kind)


def pack_body(meta, q, k, v, g, hidden, gate, send, own, partial, sems):
    core = meta[0]
    mine = pl.multiple_of(core * LANES, LANES)
    theirs = pl.multiple_of((1 - core) * LANES, LANES)
    copies = []
    for i, src in enumerate((q, k, v, g)):
        copies.append(pltpu.make_async_copy(src.at[:, pl.ds(theirs, LANES)], send.at[i], sems.at[i]))
        copies.append(pltpu.make_async_copy(src.at[:, pl.ds(mine, LANES)], own.at[i], sems.at[4 + i]))
    for copy in copies:
        copy.start()
    logits = dot(gate[...], hidden[...], 0, 1)
    for c in range(2):
        for x in range(4):
            row = x * 64 + c * 32
            partial[c * 4 + x] = logits[row : row + 32]
    for copy in copies:
        copy.wait()


def states_body(meta, slot, parts, own, other, up, cols, chosen, near_state, near_grad, rows):
    core, z, y = meta[0], meta[1], meta[2]
    for s in range(2):
        c = core if s == 0 else 1 - core
        logits = parts[c * 4] + parts[c * 4 + 1] + parts[c * 4 + 2] + parts[c * 4 + 3]
        rows[:, s * SPAN : (s + 1) * SPAN] = logits
    for h in range(HALF):
        for l in range(8):
            chosen[h * 8 + l : h * 8 + l + 1, :] = rows[pl.ds(h * 8 + slot[l], 1), :]
    x = chosen[...]
    weights = jnp.maximum(x, 0.0) + jnp.log1p(jnp.exp(-jnp.abs(x)))
    padded = jnp.concatenate([weights, jnp.zeros((128 - 8 * HALF, 2 * SPAN), F32)], 0)
    for s in range(2):
        cols[s] = jnp.transpose(padded[:, s * SPAN : (s + 1) * SPAN])
    both = jnp.concatenate([cols[0], cols[1]], 0)
    first = core == 0
    for h in range(HALF):
        lanes = slice(h * DK, (h + 1) * DK)
        q = jnp.concatenate([own[0, :, lanes], other[0, :, lanes]], 0)
        g = jnp.concatenate([own[3, :, lanes], other[3, :, lanes]], 0).astype(F32)
        state_own = dot(own[1, :, lanes], own[2, :, lanes], 0, 0)
        state_other = dot(other[1, :, lanes], other[2, :, lanes], 0, 0)
        state = state_own + state_other
        near_state[h] = (jnp.where(first, state_own, state_other) / SPAN).astype(BF)
        near = both[:, h * 8 + 1 : h * 8 + 2]
        near_g = (near * g).astype(BF)
        grad_own = dot(q[:SPAN], near_g[:SPAN], 0, 0)
        grad_other = dot(q[SPAN:], near_g[SPAN:], 0, 0)
        near_grad[h] = (jnp.where(first, grad_other, grad_own) / SPAN).astype(BF)
        weighted = jnp.concatenate(
            [(both[:, h * 8 + 2 + i : h * 8 + 3 + i] * g).astype(BF) for i in range(SLOTS)], 1
        )
        grads = dot(q, weighted, 0, 0)
        for i in range(SLOTS):
            bit = (z >> i) & 1 if i < 3 else (y >> (i - 3)) & 1
            piece = jnp.where(bit == 1, grads[:, i * DK : (i + 1) * DK], state).astype(BF)
            up[2 * h, i] = piece[:64]
            up[2 * h + 1, i] = piece[64:]


def local_body(meta, own, other, cols, near_state, near_grad, part, sums):
    core = meta[0]
    at = lax.broadcasted_iota(jnp.int32, (SPAN, SPAN), 0)
    to = lax.broadcasted_iota(jnp.int32, (SPAN, SPAN), 1)
    causal = at >= to
    for s, src in enumerate((own, other)):
        upper = (core == 1) if s == 0 else (core == 0)
        total = jnp.zeros((SPAN, 128), F32)
        weights = cols[s]
        for h in range(HALF):
            lanes = slice(h * DK, (h + 1) * DK)
            q, k, v, g = (src[i, :, lanes] for i in range(4))
            gf = g.astype(F32)
            w0 = weights[:, h * 8 : h * 8 + 1]
            w1 = weights[:, h * 8 + 1 : h * 8 + 2]
            g0 = (w0 * gf).astype(BF)
            g1 = (w1 * gf).astype(BF)
            attend = jnp.where(causal, dot(q, k, 1, 1) / SPAN, 0.0).astype(BF)
            score = jnp.where(causal, dot(g0, v, 1, 1) / SPAN, 0.0).astype(BF)
            intra = dot(attend, v, 1, 0)
            zero = jnp.zeros((DK, DK), BF)
            level = jnp.where(upper, near_state[h], zero)
            back = jnp.where(upper, zero, near_grad[h])
            near = dot(q, level, 1, 0)
            part[s, 0, :, lanes] = w0 * intra + w1 * near
            part[s, 1, :, lanes] = dot(score, k, 1, 0) + dot(g1, level, 1, 1)
            part[s, 2, :, lanes] = dot(score, q, 0, 0) + dot(v, back, 1, 1)
            part[s, 3, :, lanes] = dot(attend, g0, 0, 0) + dot(k, back, 1, 0)
            total = jnp.where(to == h * 8, jnp.sum(gf * intra, -1, keepdims=True), total)
            total = jnp.where(to == h * 8 + 1, jnp.sum(gf * near, -1, keepdims=True), total)
        sums[s] = total


def along_z_body(meta, got, send):
    y = meta[2]
    totals = []
    for i in range(3, SLOTS):
        total = got[0, i].astype(F32)
        for z in range(1, 8):
            total = total + got[z, i].astype(F32)
        totals.append(total.astype(BF))
    send[y] = jnp.zeros_like(totals[0])
    for step in range(1, 8):
        send[y ^ step] = totals[step.bit_length() - 1]


def buckets_body(meta, got, from_y, down):
    y = meta[2]
    for i in range(3):
        width = 1 << i
        scale = 1.0 / (2 * width * SPAN)
        for block in range(8 // width):
            total = got[block * width, i].astype(F32)
            for z in range(block * width + 1, (block + 1) * width):
                total = total + got[z, i].astype(F32)
            total = (total * scale).astype(BF)
            target = block ^ 1
            for z in range(target * width, (target + 1) * width):
                down[z, i] = total
    for i in range(3):
        width = 1 << i
        scale = 1.0 / (16 * width * SPAN)
        total = from_y[y ^ width].astype(F32)
        for step in range(width + 1, 2 * width):
            total = total + from_y[y ^ step].astype(F32)
        total = (total * scale).astype(BF)
        for z in range(8):
            down[z, 3 + i] = total


def final_body(meta, slot, own, other, cols, chosen, part, sums, got, keep, send, logit_grad, rows):
    core, z, y = meta[0], meta[1], meta[2]
    lane = lax.broadcasted_iota(jnp.int32, (2 * SPAN, 128), 1)
    both = jnp.concatenate([cols[0], cols[1]], 0)
    total = jnp.concatenate([sums[0], sums[1]], 0)
    for h in range(HALF):
        lanes = slice(h * DK, (h + 1) * DK)
        q, k, v, g = (
            jnp.concatenate([own[i, :, lanes], other[i, :, lanes]], 0) for i in range(4)
        )
        gf = g.astype(F32)
        levels = []
        back = jnp.zeros((DK, DK), F32)
        for i in range(SLOTS):
            bit = (z >> i) & 1 if i < 3 else (y >> (i - 3)) & 1
            state = jnp.concatenate([got[2 * h, i], got[2 * h + 1, i]], 0)
            zero = jnp.zeros_like(state)
            levels.append(jnp.where(bit == 1, state, zero))
            back = back + jnp.where(bit == 1, zero, state).astype(F32)
        back = back.astype(BF)
        levels = jnp.concatenate(levels, 1)
        outs = dot(q, levels, 1, 0)
        mixed = jnp.concatenate([part[0, 0, :, lanes], part[1, 0, :, lanes]], 0)
        weighted = []
        for i in range(SLOTS):
            w = both[:, h * 8 + 2 + i : h * 8 + 3 + i]
            out = outs[:, i * DK : (i + 1) * DK]
            mixed = mixed + w * out
            weighted.append((w * gf).astype(BF))
            total = jnp.where(lane == h * 8 + 2 + i, jnp.sum(gf * out, -1, keepdims=True), total)
        dq = dot(jnp.concatenate(weighted, 1), levels, 1, 1)
        dk = dot(v, back, 1, 1)
        dv = dot(k, back, 1, 0)
        for s, dst in enumerate((keep, send)):
            span = slice(s * SPAN, (s + 1) * SPAN)
            dst[0, :, lanes] = mixed[span].astype(BF)
            dst[1, :, lanes] = (part[s, 1, :, lanes] + dq[span]).astype(BF)
            dst[2, :, lanes] = (part[s, 2, :, lanes] + dk[span]).astype(BF)
            dst[3, :, lanes] = (part[s, 3, :, lanes] + dv[span]).astype(BF)
    for s in range(2):
        c = core if s == 0 else 1 - core
        by_level = jnp.transpose(total[s * SPAN : (s + 1) * SPAN])[: 8 * HALF]
        by_level = by_level * jax.nn.sigmoid(chosen[:, s * SPAN : (s + 1) * SPAN])
        for h in range(HALF):
            for l in range(8):
                rows[pl.ds(h * 8 + slot[l], 1), :] = by_level[h * 8 + l : h * 8 + l + 1, :]
        ready = rows[...].astype(BF)
        for x in range(4):
            logit_grad[c * 4 + x] = ready


def unpack_body(meta, keep, got, logit_grad, gate, mixed, dq, dk, dv, dhidden, sems):
    core = meta[0]
    mine = pl.multiple_of(core * LANES, LANES)
    theirs = pl.multiple_of((1 - core) * LANES, LANES)
    copies = []
    for i, dst in enumerate((mixed, dq, dk, dv)):
        copies.append(pltpu.make_async_copy(keep.at[i], dst.at[:, pl.ds(mine, LANES)], sems.at[i]))
        copies.append(pltpu.make_async_copy(got.at[i], dst.at[:, pl.ds(theirs, LANES)], sems.at[4 + i]))
    for copy in copies:
        copy.start()
    grads = jnp.concatenate([logit_grad[c * 4 + x] for x in range(4) for c in range(2)], 0)
    dhidden[...] = dot(grads, gate[...], 0, 1).astype(BF)
    for copy in copies:
        copy.wait()


def local(queries, keys, values, hidden, gate_weight, level_slot, out_grad):
    core, z, y = lax.axis_index("core"), lax.axis_index("z"), lax.axis_index("y")
    meta = jnp.stack([core, z, y]).astype(jnp.int32)
    swap = [(0, 1), (1, 0)]

    def exchange(array, axis):
        return lax.all_to_all(array, axis, 0, 0, tiled=True)

    send, own, partial = pl.pallas_call(
        pack_body,
        out_shape=(shape(4, SPAN, LANES), shape(4, SPAN, LANES), shape(8, 32, SPAN, kind=F32)),
        in_specs=smem(1) + anymem(4) + vmem(2),
        out_specs=tuple(anymem(2) + vmem(1)),
        scratch_shapes=[pltpu.SemaphoreType.DMA((8,))],
        name="pack",
    )(meta, queries, keys, values, out_grad, hidden, gate_weight)
    other = lax.ppermute(send, "core", swap)
    parts = exchange(partial, ("core", "head"))
    up, cols, chosen, near_state, near_grad = pl.pallas_call(
        states_body,
        out_shape=(
            shape(8, SLOTS, 64, DK),
            shape(2, SPAN, 128, kind=F32),
            shape(8 * HALF, 2 * SPAN, kind=F32),
            shape(HALF, DK, DK),
            shape(HALF, DK, DK),
        ),
        in_specs=smem(2) + vmem(3),
        out_specs=tuple(vmem(5)),
        scratch_shapes=[pltpu.VMEM((8 * HALF, 2 * SPAN), F32)],
        name="states",
    )(meta, level_slot, parts, own, other)
    got = exchange(up, "z")
    part, sums = pl.pallas_call(
        local_body,
        out_shape=(shape(2, 4, SPAN, LANES, kind=F32), shape(2, SPAN, 128, kind=F32)),
        in_specs=smem(1) + vmem(5),
        out_specs=tuple(vmem(2)),
        name="local",
    )(meta, own, other, cols, near_state, near_grad)
    to_y = pl.pallas_call(
        along_z_body,
        out_shape=shape(8, 64, DK),
        in_specs=smem(1) + vmem(1),
        out_specs=vmem(1)[0],
        name="along_z",
    )(meta, got)
    from_y = exchange(to_y, "y")
    down = pl.pallas_call(
        buckets_body,
        out_shape=shape(8, SLOTS, 64, DK),
        in_specs=smem(1) + vmem(2),
        out_specs=vmem(1)[0],
        name="buckets",
    )(meta, got, from_y)
    sums_here = exchange(down, "z")
    keep, away, logit_grad = pl.pallas_call(
        final_body,
        out_shape=(shape(4, SPAN, LANES), shape(4, SPAN, LANES), shape(8, 8 * HALF, SPAN)),
        in_specs=smem(2) + vmem(7),
        out_specs=tuple(vmem(3)),
        scratch_shapes=[pltpu.VMEM((8 * HALF, SPAN), F32)],
        name="final",
    )(meta, level_slot, own, other, cols, chosen, part, sums, sums_here)
    back = lax.ppermute(away, "core", swap)
    all_grads = exchange(logit_grad, ("core", "head"))
    return pl.pallas_call(
        unpack_body,
        out_shape=(shape(SPAN, 2 * LANES),) * 4 + (shape(SPAN, hidden.shape[1]),),
        in_specs=smem(1) + anymem(2) + vmem(2),
        out_specs=tuple(anymem(4) + vmem(1)),
        scratch_shapes=[pltpu.SemaphoreType.DMA((8,))],
        name="unpack",
    )(meta, keep, back, all_grads, gate_weight)


def solution(mesh):
    names = ("y", "z", "core", "head")
    fine = Mesh(mesh.devices.reshape(8, 8, 2, 4), names)
    tokens = ("y", "z", "core")
    rows = P(tokens, "head")
    return jax.shard_map(
        local,
        mesh=fine,
        in_specs=(rows, rows, rows, rows, P("head", None), P(), rows),
        out_specs=(rows,) * 5,
        check_vma=False,
    )
```

time: 324 us -> 186 us (0.57)
  waiting for transfers between devices: 173 us -> 15.8 us
  Pallas kernels: 0 us -> 87.7 us
  starting transfers between devices: 72.8 us -> 17.6 us
  blocking collectives: 12 us -> 60.6 us
  other arithmetic: 21.7 us -> 0.62 us
  between operations: 15 us -> 0.68 us
  matrix products: 13.7 us -> 0 us
  local copies, waits for them, and re-layouts: 14.9 us -> 2.48 us
    ppermute x14 -> x2, waiting for transfers between devices: 173 us -> 0.01 us  [the longest x1 0.01 us: local(): other = lax.ppermute(send, 'core', swap)]
    pallas_call x0 -> x7, Pallas kernels: none -> 87.7 us  [the longest x1 34.6 us: local(): pl.pallas_call(pack_body, out_shape=(shape(4, SPAN, LANES), shape(4, SPAN...]
    all_to_all x0 -> x4, blocking collectives: none -> 60.6 us  [exchange(): return lax.all_to_all(array, axis, 0, 0, tiled=True)]
    ppermute x14 -> x2, starting transfers between devices: 68 us -> 14.1 us  [the longest x1 8.75 us: local(): other = lax.ppermute(send, 'core', swap)]
    convert_element_type x23 -> x0, other arithmetic: 20.4 us -> none  [the longest x6 8.11 us: local(): pending.astype(jnp.bfloat16)]
    all_to_all x1, waiting for transfers between devices: 0.01 us -> 15.8 us  [exchange(): return lax.all_to_all(array, axis, 0, 0, tiled=True)]
    dot_general x16 -> x0, matrix products: 13.7 us -> none  [the longest x1 3.2 us: local(): jnp.einsum('thd,thje->hjde', query_heads, weighted[:, :, 1 + local_bits:]...]
    all_gather x1 -> x0, blocking collectives: 12 us -> none  [local(): lax.all_gather(hidden, 'head', axis=1, tiled=True)]
  transfers between devices with their start and end apart: 16 -> 3, of which waited for: 9 -> 1; matrix products, arithmetic and copies ran while one was open for 10% -> 0% of each run, Pallas kernels for 0% -> 3%
where the time goes in v1:
time: 186 us
  Pallas kernels  87.7 us (47%)
  blocking collectives  60.6 us (33%)
  starting transfers between devices  17.6 us (9%)
  waiting for transfers between devices  15.8 us (8%)
  local copies, waits for them, and re-layouts  2.48 us (1%)
    all_to_all x4, blocking collectives, exchange(): return lax.all_to_all(array, axis, 0, 0, tiled=True)  60.6 us
    pallas_call x1, Pallas kernels, local(): pl.pallas_call(pack_body, out_shape=(shape(4, SPAN, LANES), shape(4, SPAN...  34.6 us
    pallas_call x1, Pallas kernels, local(): pl.pallas_call(unpack_body, out_shape=(shape(SPAN, 2 * LANES),) * 4 + (sh...  34.6 us
    all_to_all x1, waiting for transfers between devices, exchange(): return lax.all_to_all(array, axis, 0, 0, tiled=True)  15.8 us
    ppermute x1, starting transfers between devices, local(): other = lax.ppermute(send, 'core', swap)  8.75 us
    pallas_call x1, Pallas kernels, local(): pl.pallas_call(final_body, out_shape=(shape(4, SPAN, LANES), shape(4, SPA...  5.93 us
    ppermute x1, starting transfers between devices, local(): back = lax.ppermute(away, 'core', swap)  5.32 us
    pallas_call x1, Pallas kernels, local(): pl.pallas_call(local_body, out_shape=(shape(2, 4, SPAN, LANES, kind=F32),...  4.82 us
  transfers between devices with their start and end apart: 3, of which 1 were waited for; matrix products, arithmetic and copies ran while one was open for 0% of the time, Pallas kernels for 3%

profile of v1, /device:TPU:1, one launch (start us, length us, event | category | flops | bytes accessed | tf_op | source)
XLA Modules:
  0.0 185.5 jit_solution(3343492704064358544)
XLA Ops:
  0.6 0.6 pad_add_fusion.meta
  1.3 34.6 %pack.1 = (bf16[4,128,512]{2,1,0:T(8,128)(2,1)}, bf16[4,128,512]{2,1,0:T(8,128)(2,1)}, f32[8,32,128]{2,1,0:T(8,128)}) custom-call(s32[3]{0:T(128)} %pad_add_fusion.meta, bf16[128,1024]{1,0:T(8,128)(2,1)} %q.1, bf16[128,1024]{1,0:T(8,128)(2,1)} %k.1, bf16[128,1024]{1,0:T(8,128)(2,1)} %v.1, bf16[128,1024]{1,0:T(8,128)(2,1)} %g.1, bf16[128,512]{1,0:T(8,128)(2,1)} %hidden.1, ...), custom_call_target="tpu_custom_call" | custom-call | tf_op jit(solution)/shard_map/pack/pallas_call | solution.py:241
  35.9 8.7 %collective-permute-start = (bf16[4,128,512]{2,1,0:T(8,128)(2,1)}, bf16[4,128,512]{2,1,0:T(8,128)(2,1)S(1)}, u32[]{:S(2)}, u32[]{:S(2)}) collective-permute-start(bf16[4,128,512]{2,1,0:T(8,128)(2,1)} %get-tuple-element.19), channel_id=1, source_target_pairs={{0,4},{4,0},{1,5},{5,1},{2,6},{6,2},{3,7},{7,3},{8,12},{12,8},{9,1... | collective-permute-start | bytes 1572872 | tf_op jit(solution)/shard_map/ppermute | solution.py:249
  44.6 9.2 %all_to_all.25.parts = f32[8,32,128]{2,1,0:T(8,128)} all-to-all(f32[8,32,128]{2,1,0:T(8,128)} %get-tuple-element.20), channel_id=1, replica_groups=mesh['y'=8,'z'=8,'core'=2,'head'=4] {'core','head'}, dimensions={0} | all-to-all | bytes 262144 | tf_op jit(solution)/shard_map/all_to_all | solution.py:239
  53.8 0.0 collective-permute-done.other
  53.8 0.0 copy-start
  53.8 0.8 copy-done
  54.6 3.8 %states.1 = (bf16[8,6,64,128]{3,2,1,0:T(8,128)(2,1)}, f32[2,128,128]{2,1,0:T(8,128)}, f32[32,256]{1,0:T(8,128)}, bf16[4,128,128]{2,1,0:T(8,128)(2,1)}, bf16[4,128,128]{2,1,0:T(8,128)(2,1)}) custom-call(s32[3]{0:T(128)} %pad_add_fusion.meta, s32[8]{0:T(128)} %slot.3, f32[8,32,128]{2,1,0:T(8,128)} %all_to_all.25.parts, ...), custom_call_target="tpu_custom_call" | custom-call | tf_op jit(solution)/shard_map/states/pallas_call | solution.py:251
  58.4 27.6 %all_to_all.26.got = bf16[8,6,64,128]{3,2,1,0:T(8,128)(2,1)} all-to-all(bf16[8,6,64,128]{3,2,1,0:T(8,128)(2,1)} %get-tuple-element.27), channel_id=1, replica_groups=mesh['y'=8,'z'=8,'core'=2,'head'=4] {'z'}, dimensions={0} | all-to-all | bytes 1572864 | tf_op jit(solution)/shard_map/all_to_all | solution.py:239
  86.0 1.9 along_z.1
  87.8 15.0 %all_to_all.27.from_y = bf16[8,64,128]{2,1,0:T(8,128)(2,1)} all-to-all(bf16[8,64,128]{2,1,0:T(8,128)(2,1)} %along_z.1), channel_id=1, replica_groups=mesh['y'=8,'z'=8,'core'=2,'head'=4] {'y'}, dimensions={0} | all-to-all | bytes 262144 | tf_op jit(solution)/shard_map/all_to_all | solution.py:239
  102.8 2.1 %buckets.1 = bf16[8,6,64,128]{3,2,1,0:T(8,128)(2,1)} custom-call(s32[3]{0:T(128)} %pad_add_fusion.meta, bf16[8,6,64,128]{3,2,1,0:T(8,128)(2,1)} %all_to_all.26.got, bf16[8,64,128]{2,1,0:T(8,128)(2,1)} %all_to_all.27.from_y), custom_call_target="tpu_custom_call" | custom-call | tf_op jit(solution)/shard_map/buckets/pallas_call | solution.py:281
  104.9 3.5 %all-to-all-start.3 = ((bf16[8,6,64,128]{3,2,1,0:T(8,128)(2,1)}), bf16[8,6,64,128]{3,2,1,0:T(8,128)(2,1)S(1)}, u32[]{:S(2)}, u32[]{:S(2)}) async-start(bf16[8,6,64,128]{3,2,1,0:T(8,128)(2,1)} %buckets.1), calls=%async_computation.3 | async-start | bytes 1572864 | tf_op jit(solution)/shard_map/all_to_all | solution.py:239
  108.4 4.8 %local.1 = (f32[2,4,128,512]{3,2,1,0:T(8,128)}, f32[2,128,128]{2,1,0:T(8,128)}) custom-call(s32[3]{0:T(128)} %pad_add_fusion.meta, bf16[4,128,512]{2,1,0:T(8,128)(2,1)} %get-tuple-element.18.own, bf16[4,128,512]{2,1,0:T(8,128)(2,1)} %copy-done, f32[2,128,128]{2,1,0:T(8,128)} %get-tuple-element.21.cols, bf16[4,128,128]{2,1,0:T(8,128)(2,1)} %get-tuple-element.23.near_state, ...), custom_call_target="tpu_custom_call" | custom-call | tf_op jit(solution)/shard_map/local/pallas_call | solution.py:266
  113.3 15.8 %all-to-all-done.3.got = bf16[8,6,64,128]{3,2,1,0:T(8,128)(2,1)S(1)} async-done(((bf16[8,6,64,128]{3,2,1,0:T(8,128)(2,1)}), bf16[8,6,64,128]{3,2,1,0:T(8,128)(2,1)S(1)}, u32[]{:S(2)}, u32[]{:S(2)}) %all-to-all-start.3) | async-done | bytes 786464 | tf_op jit(solution)/shard_map/all_to_all | solution.py:239
  129.0 0.0 copy-start.1
  129.0 0.9 copy-done.1
  129.9 5.9 %final.1 = (bf16[4,128,512]{2,1,0:T(8,128)(2,1)}, bf16[4,128,512]{2,1,0:T(8,128)(2,1)}, bf16[8,32,128]{2,1,0:T(8,128)(2,1)}) custom-call(s32[3]{0:T(128)} %pad_add_fusion.meta, s32[8]{0:T(128)} %slot.3, bf16[4,128,512]{2,1,0:T(8,128)(2,1)} %get-tuple-element.18.own, bf16[4,128,512]{2,1,0:T(8,128)(2,1)} %copy-done, f32[2,128,128]{2,1,0:T(8,128)} %get-tuple-element.21.cols, ...), custom_call_target="tpu_custom_call" | custom-call | tf_op jit(solution)/shard_map/final/pallas_call | solution.py:289
  135.9 5.3 %collective-permute-start.1 = (bf16[4,128,512]{2,1,0:T(8,128)(2,1)}, bf16[4,128,512]{2,1,0:T(8,128)(2,1)S(1)}, u32[]{:S(2)}, u32[]{:S(2)}) collective-permute-start(bf16[4,128,512]{2,1,0:T(8,128)(2,1)} %get-tuple-element.29), channel_id=1, source_target_pairs={{0,4},{4,0},{1,5},{5,1},{2,6},{6,2},{3,7},{7,3},{8,12},{12,8},{9,1... | collective-permute-start | bytes 1572872 | tf_op jit(solution)/shard_map/ppermute | solution.py:297
  141.2 8.9 %all_to_all.28.logit_grad = bf16[8,32,128]{2,1,0:T(8,128)(2,1)} all-to-all(bf16[8,32,128]{2,1,0:T(8,128)(2,1)} %get-tuple-element.30), channel_id=1, replica_groups=mesh['y'=8,'z'=8,'core'=2,'head'=4] {'core','head'}, dimensions={0} | all-to-all | bytes 131072 | tf_op jit(solution)/shard_map/all_to_all | solution.py:239
  150.1 0.0 collective-permute-done.1.got
  150.1 0.0 copy-start.2
  150.1 0.8 copy-done.2
  150.9 34.6 %unpack.1 = (bf16[128,1024]{1,0:T(8,128)(2,1)}, bf16[128,1024]{1,0:T(8,128)(2,1)}, bf16[128,1024]{1,0:T(8,128)(2,1)}, bf16[128,1024]{1,0:T(8,128)(2,1)}, bf16[128,512]{1,0:T(8,128)(2,1)}) custom-call(s32[3]{0:T(128)} %pad_add_fusion.meta, bf16[4,128,512]{2,1,0:T(8,128)(2,1)} %get-tuple-element.28.keep, bf16[4,128,512]{2,1,0:T(8,128)(2,1)} %copy-done.2, ...), custom_call_target="tpu_custom_call" | custom-call | tf_op jit(solution)/shard_map/unpack/pallas_call | solution.py:299
Async XLA Ops:
  35.9 17.9 %collective-permute-start = (bf16[4,128,512]{2,1,0:T(8,128)(2,1)}, bf16[4,128,512]{2,1,0:T(8,128)(2,1)S(1)}, u32[]{:S(2)}, u32[]{:S(2)}) collective-permute-start(bf16[4,128,512]{2,1,0:T(8,128)(2,1)} %get-tuple-element.19), channel_id=1, source_target_pairs={{0,4},{4,0},{1,5},{5,1},{2,6},{6,2},{3,7},{7,3},{8,12},{12,8},{9,1... | collective-permute-start | bytes 1572872 | tf_op jit(solution)/shard_map/ppermute | solution.py:249
  53.8 0.8 copy-start
  104.9 24.1 %all-to-all-start.3 = ((bf16[8,6,64,128]{3,2,1,0:T(8,128)(2,1)}), bf16[8,6,64,128]{3,2,1,0:T(8,128)(2,1)S(1)}, u32[]{:S(2)}, u32[]{:S(2)}) async-start(bf16[8,6,64,128]{3,2,1,0:T(8,128)(2,1)} %buckets.1), calls=%async_computation.3 | async-start | bytes 1572864 | tf_op jit(solution)/shard_map/all_to_all | solution.py:239
  129.0 0.9 copy-start.1
  135.9 14.3 %collective-permute-start.1 = (bf16[4,128,512]{2,1,0:T(8,128)(2,1)}, bf16[4,128,512]{2,1,0:T(8,128)(2,1)S(1)}, u32[]{:S(2)}, u32[]{:S(2)}) collective-permute-start(bf16[4,128,512]{2,1,0:T(8,128)(2,1)} %get-tuple-element.29), channel_id=1, source_target_pairs={{0,4},{4,0},{1,5},{5,1},{2,6},{6,2},{3,7},{7,3},{8,12},{12,8},{9,1... | collective-permute-start | bytes 1572872 | tf_op jit(solution)/shard_map/ppermute | solution.py:297
  150.1 0.8 copy-start.2

commit v2 on v1

--- a/solution.py
+++ b/solution.py
@@ -31,26 +31,27 @@
 
 
 def shape(*dims, kind=BF):
-    return jax.ShapeDtypeStruct(dims, kind)
-
-
-def pack_body(meta, q, k, v, g, hidden, gate, send, own, partial, sems):
-    core = meta[0]
-    mine = pl.multiple_of(core * LANES, LANES)
-    theirs = pl.multiple_of((1 - core) * LANES, LANES)
-    copies = []
+    return pltpu.VMEM(dims, kind)
+
+
+def near(*arrays):
+    return [pltpu.with_memory_space_constraint(a, pltpu.VMEM) for a in arrays]
+
+
+SMALL = pltpu.CompilerParams(vmem_limit_bytes=16 << 20)
+
+
+def pack_body(meta, q, k, v, g, hidden, gate, send, own, partial):
+    first = meta[0] == 0
     for i, src in enumerate((q, k, v, g)):
-        copies.append(pltpu.make_async_copy(src.at[:, pl.ds(theirs, LANES)], send.at[i], sems.at[i]))
-        copies.append(pltpu.make_async_copy(src.at[:, pl.ds(mine, LANES)], own.at[i], sems.at[4 + i]))
-    for copy in copies:
-        copy.start()
+        low, high = src[:, :LANES], src[:, LANES:]
+        own[i] = jnp.where(first, low, high)
+        send[i] = jnp.where(first, high, low)
     logits = dot(gate[...], hidden[...], 0, 1)
     for c in range(2):
         for x in range(4):
             row = x * 64 + c * 32
             partial[c * 4 + x] = logits[row : row + 32]
-    for copy in copies:
-        copy.wait()
 
 
 def states_body(meta, slot, parts, own, other, up, cols, chosen, near_state, near_grad, rows):
@@ -214,20 +215,14 @@
             logit_grad[c * 4 + x] = ready
 
 
-def unpack_body(meta, keep, got, logit_grad, gate, mixed, dq, dk, dv, dhidden, sems):
-    core = meta[0]
-    mine = pl.multiple_of(core * LANES, LANES)
-    theirs = pl.multiple_of((1 - core) * LANES, LANES)
-    copies = []
+def unpack_body(meta, keep, got, logit_grad, gate, mixed, dq, dk, dv, dhidden):
+    first = meta[0] == 0
     for i, dst in enumerate((mixed, dq, dk, dv)):
-        copies.append(pltpu.make_async_copy(keep.at[i], dst.at[:, pl.ds(mine, LANES)], sems.at[i]))
-        copies.append(pltpu.make_async_copy(got.at[i], dst.at[:, pl.ds(theirs, LANES)], sems.at[4 + i]))
-    for copy in copies:
-        copy.start()
+        here, there = keep[i], got[i]
+        dst[:, :LANES] = jnp.where(first, here, there)
+        dst[:, LANES:] = jnp.where(first, there, here)
     grads = jnp.concatenate([logit_grad[c * 4 + x] for x in range(4) for c in range(2)], 0)
     dhidden[...] = dot(grads, gate[...], 0, 1).astype(BF)
-    for copy in copies:
-        copy.wait()
 
 
 def local(queries, keys, values, hidden, gate_weight, level_slot, out_grad):
@@ -241,9 +236,9 @@
     send, own, partial = pl.pallas_call(
         pack_body,
         out_shape=(shape(4, SPAN, LANES), shape(4, SPAN, LANES), shape(8, 32, SPAN, kind=F32)),
-        in_specs=smem(1) + anymem(4) + vmem(2),
-        out_specs=tuple(anymem(2) + vmem(1)),
-        scratch_shapes=[pltpu.SemaphoreType.DMA((8,))],
+        in_specs=smem(1) + vmem(6),
+        out_specs=tuple(vmem(3)),
+        compiler_params=SMALL,
         name="pack",
     )(meta, queries, keys, values, out_grad, hidden, gate_weight)
     other = lax.ppermute(send, "core", swap)
@@ -260,31 +255,35 @@
         in_specs=smem(2) + vmem(3),
         out_specs=tuple(vmem(5)),
         scratch_shapes=[pltpu.VMEM((8 * HALF, 2 * SPAN), F32)],
+        compiler_params=SMALL,
         name="states",
-    )(meta, level_slot, parts, own, other)
+    )(meta, level_slot, *near(parts, own, other))
     got = exchange(up, "z")
     part, sums = pl.pallas_call(
         local_body,
         out_shape=(shape(2, 4, SPAN, LANES, kind=F32), shape(2, SPAN, 128, kind=F32)),
         in_specs=smem(1) + vmem(5),
         out_specs=tuple(vmem(2)),
+        compiler_params=SMALL,
         name="local",
-    )(meta, own, other, cols, near_state, near_grad)
+    )(meta, *near(own, other, cols, near_state, near_grad))
     to_y = pl.pallas_call(
         along_z_body,
         out_shape=shape(8, 64, DK),
         in_specs=smem(1) + vmem(1),
         out_specs=vmem(1)[0],
+        compiler_params=SMALL,
         name="along_z",
-    )(meta, got)
+    )(meta, *near(got))
     from_y = exchange(to_y, "y")
     down = pl.pallas_call(
         buckets_body,
         out_shape=shape(8, SLOTS, 64, DK),
         in_specs=smem(1) + vmem(2),
         out_specs=vmem(1)[0],
+        compiler_params=SMALL,
         name="buckets",
-    )(meta, got, from_y)
+    )(meta, *near(got, from_y))
     sums_here = exchange(down, "z")
     keep, away, logit_grad = pl.pallas_call(
         final_body,
@@ -292,18 +291,20 @@
         in_specs=smem(2) + vmem(7),
         out_specs=tuple(vmem(3)),
         scratch_shapes=[pltpu.VMEM((8 * HALF, SPAN), F32)],
+        compiler_params=SMALL,
         name="final",
-    )(meta, level_slot, own, other, cols, chosen, part, sums, sums_here)
+    )(meta, level_slot, *near(own, other, cols, chosen, part, sums, sums_here))
     back = lax.ppermute(away, "core", swap)
     all_grads = exchange(logit_grad, ("core", "head"))
+    outs = (jax.ShapeDtypeStruct((SPAN, 2 * LANES), BF),) * 4
     return pl.pallas_call(
         unpack_body,
-        out_shape=(shape(SPAN, 2 * LANES),) * 4 + (shape(SPAN, hidden.shape[1]),),
-        in_specs=smem(1) + anymem(2) + vmem(2),
-        out_specs=tuple(anymem(4) + vmem(1)),
-        scratch_shapes=[pltpu.SemaphoreType.DMA((8,))],
+        out_shape=outs + (jax.ShapeDtypeStruct((SPAN, hidden.shape[1]), BF),),
+        in_specs=smem(1) + vmem(4),
+        out_specs=tuple(vmem(5)),
+        compiler_params=SMALL,
         name="unpack",
-    )(meta, keep, back, all_grads, gate_weight)
+    )(meta, *near(keep, back, all_grads), gate_weight)
 
 
 def solution(mesh):

time: 186 us -> 116 us (0.62)
  Pallas kernels: 87.7 us -> 12.9 us
  local copies, waits for them, and re-layouts: 2.48 us -> 9.24 us
  blocking collectives: 60.6 us -> 58.1 us
    pallas_call x1, Pallas kernels: 34.6 us -> 0.84 us  [local(): pl.pallas_call(pack_body, out_shape=(shape(4, SPAN, LANES), shape(4, SPAN...]
    pallas_call x1, Pallas kernels: 34.6 us -> 1.66 us  [local(): pl.pallas_call(unpack_body, out_shape=outs + (jax.ShapeDtypeStruct((SPAN,...]
    unnamed x6 -> x22, local copies, waits for them, and re-layouts: 2.48 us -> 9.24 us
    all_to_all x4, blocking collectives: 60.6 us -> 58.1 us  [exchange(): return lax.all_to_all(array, axis, 0, 0, tiled=True)]
    pallas_call x1, Pallas kernels: 5.93 us -> 3.44 us  [local(): pl.pallas_call(final_body, out_shape=(shape(4, SPAN, LANES), shape(4, SPA...]
    pallas_call x1, Pallas kernels: 4.82 us -> 2.75 us  [local(): pl.pallas_call(local_body, out_shape=(shape(2, 4, SPAN, LANES, kind=F32),...]
  transfers between devices with their start and end apart: 3 -> 3, of which waited for: 1 -> 1; matrix products, arithmetic and copies ran while one was open for 0% -> 0% of each run, Pallas kernels for 3% -> 2%
where the time goes in v2:
time: 116 us; the launch traced here: 115 us
  blocking collectives  58.1 us (50%)
  starting transfers between devices  17.6 us (15%)
  waiting for transfers between devices  16.5 us (14%)
  Pallas kernels  12.9 us (11%)
  local copies, waits for them, and re-layouts  9.24 us (8%)
    all_to_all x4, blocking collectives, exchange(): return lax.all_to_all(array, axis, 0, 0, tiled=True)  58.1 us
    all_to_all x1, waiting for transfers between devices, exchange(): return lax.all_to_all(array, axis, 0, 0, tiled=True)  16.5 us
    unnamed x22, local copies, waits for them, and re-layouts  9.24 us
    ppermute x1, starting transfers between devices, local(): other = lax.ppermute(send, 'core', swap)  8.75 us
    ppermute x1, starting transfers between devices, local(): back = lax.ppermute(away, 'core', swap)  5.34 us
    all_to_all x1, starting transfers between devices, exchange(): return lax.all_to_all(array, axis, 0, 0, tiled=True)  3.55 us
    pallas_call x1, Pallas kernels, local(): pl.pallas_call(final_body, out_shape=(shape(4, SPAN, LANES), shape(4, SPA...  3.44 us
    pallas_call x1, Pallas kernels, local(): pl.pallas_call(local_body, out_shape=(shape(2, 4, SPAN, LANES, kind=F32),...  2.75 us
  transfers between devices with their start and end apart: 3, of which 1 were waited for; matrix products, arithmetic and copies ran while one was open for 0% of the time, Pallas kernels for 2%

profile of v2, /device:TPU:1, one launch (start us, length us, event | category | flops | bytes accessed | tf_op | source)
XLA Modules:
  0.0 115.2 jit_solution(2900992393762236945)
XLA Ops:
  0.6 0.1 pad_add_fusion.meta
  0.7 0.0 copy-start.2
  0.7 0.9 copy-done.2
  1.7 0.0 copy-start.4
  1.7 0.9 copy-done.4
  2.6 0.0 copy-start.5
  2.6 0.9 copy-done.5
  3.6 0.0 copy-start.6
  3.6 0.9 copy-done.6
  4.5 0.0 copy-start.7
  4.5 0.9 copy-done.7
  5.5 0.0 copy-start.8
  5.5 0.9 copy-done.8
  6.4 0.8 pack.1
  7.2 8.7 %collective-permute-start = (bf16[4,128,512]{2,1,0:T(8,128)(2,1)S(1)}, bf16[4,128,512]{2,1,0:T(8,128)(2,1)S(1)}, u32[]{:S(2)}, u32[]{:S(2)}) collective-permute-start(bf16[4,128,512]{2,1,0:T(8,128)(2,1)S(1)} %get-tuple-element.19), channel_id=1, source_target_pairs={{0,4},{4,0},{1,5},{5,1},{2,6},{6,2},{3,7},{7,3},{8,12},{12,8},{9,1... | collective-permute-start | bytes 1572872 | tf_op jit(solution)/shard_map/ppermute | solution.py:244
  16.0 7.6 %all_to_all.25.parts = f32[8,32,128]{2,1,0:T(8,128)S(1)} all-to-all(f32[8,32,128]{2,1,0:T(8,128)S(1)} %get-tuple-element.20), channel_id=1, replica_groups=mesh['y'=8,'z'=8,'core'=2,'head'=4] {'core','head'}, dimensions={0} | all-to-all | bytes 262144 | tf_op jit(solution)/shard_map/all_to_all | solution.py:234
  23.6 0.0 collective-permute-done.other
  23.6 0.0 copy-start.9
  23.6 0.7 copy-done.9
  24.2 2.1 %states.1 = (bf16[8,6,64,128]{3,2,1,0:T(8,128)(2,1)S(1)}, f32[2,128,128]{2,1,0:T(8,128)S(1)}, f32[32,256]{1,0:T(8,128)S(1)}, bf16[4,128,128]{2,1,0:T(8,128)(2,1)S(1)}, bf16[4,128,128]{2,1,0:T(8,128)(2,1)S(1)}) custom-call(s32[3]{0:T(128)S(1)} %pad_add_fusion.meta, s32[8]{0:T(128)S(1)} %copy-done.9, f32[8,32,128]{2,1,0:T(8,128)S(1)} %all_to_all.25.parts, ...), custom_call_target="tpu_custom_call" | custom-call | tf_op jit(solution)/shard_map/states/pallas_call | solution.py:246
  26.3 28.6 %all_to_all.26.got = bf16[8,6,64,128]{3,2,1,0:T(8,128)(2,1)S(1)} all-to-all(bf16[8,6,64,128]{3,2,1,0:T(8,128)(2,1)S(1)} %get-tuple-element.27), channel_id=1, replica_groups=mesh['y'=8,'z'=8,'core'=2,'head'=4] {'z'}, dimensions={0} | all-to-all | bytes 1572864 | tf_op jit(solution)/shard_map/all_to_all | solution.py:234
  54.9 0.6 along_z.1
  55.5 14.6 %all_to_all.27.from_y = bf16[8,64,128]{2,1,0:T(8,128)(2,1)S(1)} all-to-all(bf16[8,64,128]{2,1,0:T(8,128)(2,1)S(1)} %along_z.1), channel_id=1, replica_groups=mesh['y'=8,'z'=8,'core'=2,'head'=4] {'y'}, dimensions={0} | all-to-all | bytes 262144 | tf_op jit(solution)/shard_map/all_to_all | solution.py:234
  70.2 0.0 copy-start.10
  70.2 1.5 %buckets.1 = bf16[8,6,64,128]{3,2,1,0:T(8,128)(2,1)} custom-call(s32[3]{0:T(128)S(1)} %pad_add_fusion.meta, bf16[8,6,64,128]{3,2,1,0:T(8,128)(2,1)S(1)} %all_to_all.26.got, bf16[8,64,128]{2,1,0:T(8,128)(2,1)S(1)} %all_to_all.27.from_y), custom_call_target="tpu_custom_call" | custom-call | tf_op jit(solution)/shard_map/buckets/pallas_call | solution.py:279
  71.7 3.5 %all-to-all-start.3 = ((bf16[8,6,64,128]{3,2,1,0:T(8,128)(2,1)}), bf16[8,6,64,128]{3,2,1,0:T(8,128)(2,1)S(1)}, u32[]{:S(2)}, u32[]{:S(2)}) async-start(bf16[8,6,64,128]{3,2,1,0:T(8,128)(2,1)} %buckets.1), calls=%async_computation.3 | async-start | bytes 1572864 | tf_op jit(solution)/shard_map/all_to_all | solution.py:234
  75.2 2.7 %local.1 = (f32[2,4,128,512]{3,2,1,0:T(8,128)S(1)}, f32[2,128,128]{2,1,0:T(8,128)S(1)}) custom-call(s32[3]{0:T(128)S(1)} %pad_add_fusion.meta, bf16[4,128,512]{2,1,0:T(8,128)(2,1)S(1)} %get-tuple-element.18.own, bf16[4,128,512]{2,1,0:T(8,128)(2,1)S(1)} %collective-permute-done.other, f32[2,128,128]{2,1,0:T(8,128)S(1)} %get-tuple-element.21.cols, ...), custom_call_target="tpu_custom_call" | custom-call | tf_op jit(solution)/shard_map/local/pallas_call | solution.py:262
  78.0 0.0 copy-start
  78.0 1.3 %copy-done = f32[2,4,128,512]{3,2,1,0:T(8,128)} copy-done((f32[2,4,128,512]{3,2,1,0:T(8,128)}, f32[2,4,128,512]{3,2,1,0:T(8,128)S(1)}, u32[]{:S(2)}) %copy-start) | copy-done | bytes 2097176
  79.3 16.5 %all-to-all-done.3.got = bf16[8,6,64,128]{3,2,1,0:T(8,128)(2,1)S(1)} async-done(((bf16[8,6,64,128]{3,2,1,0:T(8,128)(2,1)}), bf16[8,6,64,128]{3,2,1,0:T(8,128)(2,1)S(1)}, u32[]{:S(2)}, u32[]{:S(2)}) %all-to-all-start.3) | async-done | bytes 786464 | tf_op jit(solution)/shard_map/all_to_all | solution.py:234
  95.8 0.0 copy-done.10
  95.8 0.0 copy-start.1
  95.8 1.6 %copy-done.1 = f32[2,4,128,512]{3,2,1,0:T(8,128)S(1)} copy-done((f32[2,4,128,512]{3,2,1,0:T(8,128)S(1)}, f32[2,4,128,512]{3,2,1,0:T(8,128)}, u32[]{:S(2)}) %copy-start.1) | copy-done | bytes 2097176
  97.4 0.0 copy-start.3
  97.4 3.4 %final.1 = (bf16[4,128,512]{2,1,0:T(8,128)(2,1)S(1)}, bf16[4,128,512]{2,1,0:T(8,128)(2,1)S(1)}, bf16[8,32,128]{2,1,0:T(8,128)(2,1)S(1)}) custom-call(s32[3]{0:T(128)S(1)} %pad_add_fusion.meta, s32[8]{0:T(128)S(1)} %copy-done.10, bf16[4,128,512]{2,1,0:T(8,128)(2,1)S(1)} %get-tuple-element.18.own, bf16[4,128,512]{2,1,0:T(8,128)(2,1)S(1)} %collective-permute-done.other, ...), custom_call_target="tpu_custom_call" | custom-call | tf_op jit(solution)/shard_map/final/pallas_call | solution.py:288
  100.9 5.3 %collective-permute-start.1 = (bf16[4,128,512]{2,1,0:T(8,128)(2,1)S(1)}, bf16[4,128,512]{2,1,0:T(8,128)(2,1)S(1)}, u32[]{:S(2)}, u32[]{:S(2)}) collective-permute-start(bf16[4,128,512]{2,1,0:T(8,128)(2,1)S(1)} %get-tuple-element.29), channel_id=1, source_target_pairs={{0,4},{4,0},{1,5},{5,1},{2,6},{6,2},{3,7},{7,3},{8,12},{12,8},{9,1... | collective-permute-start | bytes 1572872 | tf_op jit(solution)/shard_map/ppermute | solution.py:297
  106.2 7.3 %all_to_all.28.logit_grad = bf16[8,32,128]{2,1,0:T(8,128)(2,1)S(1)} all-to-all(bf16[8,32,128]{2,1,0:T(8,128)(2,1)S(1)} %get-tuple-element.30), channel_id=1, replica_groups=mesh['y'=8,'z'=8,'core'=2,'head'=4] {'core','head'}, dimensions={0} | all-to-all | bytes 131072 | tf_op jit(solution)/shard_map/all_to_all | solution.py:234
  113.6 0.0 collective-permute-done.1.got
  113.6 0.0 copy-done.3
  113.6 1.7 %unpack.1 = (bf16[128,1024]{1,0:T(8,128)(2,1)}, bf16[128,1024]{1,0:T(8,128)(2,1)}, bf16[128,1024]{1,0:T(8,128)(2,1)}, bf16[128,1024]{1,0:T(8,128)(2,1)}, bf16[128,512]{1,0:T(8,128)(2,1)}) custom-call(s32[3]{0:T(128)S(1)} %pad_add_fusion.meta, bf16[4,128,512]{2,1,0:T(8,128)(2,1)S(1)} %get-tuple-element.28.keep, ...), custom_call_target="tpu_custom_call" | custom-call | tf_op jit(solution)/shard_map/unpack/pallas_call | solution.py:300
Async XLA Ops:
  0.7 1.0 copy-start.2
  1.7 0.9 copy-start.4
  2.6 0.9 copy-start.5
  3.6 0.9 copy-start.6
  4.5 0.9 copy-start.7
  5.5 0.9 copy-start.8
  7.2 16.3 %collective-permute-start = (bf16[4,128,512]{2,1,0:T(8,128)(2,1)S(1)}, bf16[4,128,512]{2,1,0:T(8,128)(2,1)S(1)}, u32[]{:S(2)}, u32[]{:S(2)}) collective-permute-start(bf16[4,128,512]{2,1,0:T(8,128)(2,1)S(1)} %get-tuple-element.19), channel_id=1, source_target_pairs={{0,4},{4,0},{1,5},{5,1},{2,6},{6,2},{3,7},{7,3},{8,12},{12,8},{9,1... | collective-permute-start | bytes 1572872 | tf_op jit(solution)/shard_map/ppermute | solution.py:244
  23.6 0.7 copy-start.9
  70.2 25.7 %copy-start.10 = (s32[8]{0:T(128)S(1)}, s32[8]{0:T(128)}, u32[]{:S(2)}) copy-start(s32[8]{0:T(128)} %slot.3) | copy-start | bytes 100
  71.7 24.1 %all-to-all-start.3 = ((bf16[8,6,64,128]{3,2,1,0:T(8,128)(2,1)}), bf16[8,6,64,128]{3,2,1,0:T(8,128)(2,1)S(1)}, u32[]{:S(2)}, u32[]{:S(2)}) async-start(bf16[8,6,64,128]{3,2,1,0:T(8,128)(2,1)} %buckets.1), calls=%async_computation.3 | async-start | bytes 1572864 | tf_op jit(solution)/shard_map/all_to_all | solution.py:234
  78.0 1.3 %copy-start = (f32[2,4,128,512]{3,2,1,0:T(8,128)}, f32[2,4,128,512]{3,2,1,0:T(8,128)S(1)}, u32[]{:S(2)}) copy-start(f32[2,4,128,512]{3,2,1,0:T(8,128)S(1)} %get-tuple-element.25.part) | copy-start | bytes 6291460
  95.8 1.6 %copy-start.1 = (f32[2,4,128,512]{3,2,1,0:T(8,128)S(1)}, f32[2,4,128,512]{3,2,1,0:T(8,128)}, u32[]{:S(2)}) copy-start(f32[2,4,128,512]{3,2,1,0:T(8,128)} %copy-done) | copy-start | bytes 6291460
  97.4 16.1 %copy-start.3 = (bf16[512,256]{1,0:T(8,128)(2,1)S(1)}, bf16[512,256]{1,0:T(8,128)(2,1)}, u32[]{:S(2)}) copy-start(bf16[512,256]{1,0:T(8,128)(2,1)} %gate.3) | copy-start | bytes 786436
  100.9 12.7 %collective-permute-start.1 = (bf16[4,128,512]{2,1,0:T(8,128)(2,1)S(1)}, bf16[4,128,512]{2,1,0:T(8,128)(2,1)S(1)}, u32[]{:S(2)}, u32[]{:S(2)}) collective-permute-start(bf16[4,128,512]{2,1,0:T(8,128)(2,1)S(1)} %get-tuple-element.29), channel_id=1, source_target_pairs={{0,4},{4,0},{1,5},{5,1},{2,6},{6,2},{3,7},{7,3},{8,12},{12,8},{9,1... | collective-permute-start | bytes 1572872 | tf_op jit(solution)/shard_map/ppermute | solution.py:297

commit v3 on v2

--- a/solution.py
+++ b/solution.py
@@ -4,6 +4,7 @@
 from jax.experimental import pallas as pl
 from jax.experimental.pallas import tpu as pltpu
 from jax.sharding import Mesh, PartitionSpec as P
+
 
 DK = 128
 SPAN = 128
@@ -22,8 +23,8 @@
     return [pl.BlockSpec(memory_space=pltpu.VMEM)] * n
 
 
-def anymem(n):
-    return [pl.BlockSpec(memory_space=pl.ANY)] * n
+def hbm(n):
+    return [pl.BlockSpec(memory_space=pltpu.HBM)] * n
 
 
 def smem(n):
@@ -38,23 +39,44 @@
     return [pltpu.with_memory_space_constraint(a, pltpu.VMEM) for a in arrays]
 
 
+def far(*arrays):
+    return [pltpu.with_memory_space_constraint(a, pltpu.HBM) for a in arrays]
+
+
 SMALL = pltpu.CompilerParams(vmem_limit_bytes=16 << 20)
 
 
-def pack_body(meta, q, k, v, g, hidden, gate, send, own, partial):
-    first = meta[0] == 0
+def pack_body(meta, q, k, v, g, hidden, gate, send, own, partial, held, held_hidden, held_gate, sems):
+    copies = [
+        pltpu.make_async_copy(hidden, held_hidden, sems.at[0]),
+        pltpu.make_async_copy(gate.at[:256], held_gate.at[:256], sems.at[1]),
+        pltpu.make_async_copy(gate.at[256:], held_gate.at[256:], sems.at[2]),
+    ]
     for i, src in enumerate((q, k, v, g)):
-        low, high = src[:, :LANES], src[:, LANES:]
-        own[i] = jnp.where(first, low, high)
-        send[i] = jnp.where(first, high, low)
-    logits = dot(gate[...], hidden[...], 0, 1)
+        for part in range(2):
+            rows = slice(part * 64, part * 64 + 64)
+            copies.append(
+                pltpu.make_async_copy(src.at[rows], held.at[i, rows], sems.at[3 + 2 * i + part])
+            )
+    for copy in copies:
+        copy.start()
+    for copy in copies[:3]:
+        copy.wait()
+    logits = dot(held_gate[...], held_hidden[...], 0, 1)
     for c in range(2):
         for x in range(4):
             row = x * 64 + c * 32
             partial[c * 4 + x] = logits[row : row + 32]
-
-
-def states_body(meta, slot, parts, own, other, up, cols, chosen, near_state, near_grad, rows):
+    first = meta[0] == 0
+    for i in range(4):
+        copies[3 + 2 * i].wait()
+        copies[4 + 2 * i].wait()
+        low, high = held[i, :, :LANES], held[i, :, LANES:]
+        own[i] = jnp.where(first, low, high)
+        send[i] = jnp.where(first, high, low)
+
+
+def states_body(meta, parts, own, other, up, cols, chosen, near_state, near_grad, rows):
     core, z, y = meta[0], meta[1], meta[2]
     for s in range(2):
         c = core if s == 0 else 1 - core
@@ -62,7 +84,7 @@
         rows[:, s * SPAN : (s + 1) * SPAN] = logits
     for h in range(HALF):
         for l in range(8):
-            chosen[h * 8 + l : h * 8 + l + 1, :] = rows[pl.ds(h * 8 + slot[l], 1), :]
+            chosen[h * 8 + l : h * 8 + l + 1, :] = rows[pl.ds(h * 8 + meta[3 + l], 1), :]
     x = chosen[...]
     weights = jnp.maximum(x, 0.0) + jnp.log1p(jnp.exp(-jnp.abs(x)))
     padded = jnp.concatenate([weights, jnp.zeros((128 - 8 * HALF, 2 * SPAN), F32)], 0)
@@ -94,12 +116,12 @@
             up[2 * h + 1, i] = piece[64:]
 
 
-def local_body(meta, own, other, cols, near_state, near_grad, part, sums):
+def local_body(meta, own, other, cols, near_state, near_grad, part_own, part_other, sums):
     core = meta[0]
     at = lax.broadcasted_iota(jnp.int32, (SPAN, SPAN), 0)
     to = lax.broadcasted_iota(jnp.int32, (SPAN, SPAN), 1)
     causal = at >= to
-    for s, src in enumerate((own, other)):
+    for s, (src, part) in enumerate(((own, part_own), (other, part_other))):
         upper = (core == 1) if s == 0 else (core == 0)
         total = jnp.zeros((SPAN, 128), F32)
         weights = cols[s]
@@ -118,10 +140,10 @@
             level = jnp.where(upper, near_state[h], zero)
             back = jnp.where(upper, zero, near_grad[h])
             near = dot(q, level, 1, 0)
-            part[s, 0, :, lanes] = w0 * intra + w1 * near
-            part[s, 1, :, lanes] = dot(score, k, 1, 0) + dot(g1, level, 1, 1)
-            part[s, 2, :, lanes] = dot(score, q, 0, 0) + dot(v, back, 1, 1)
-            part[s, 3, :, lanes] = dot(attend, g0, 0, 0) + dot(k, back, 1, 0)
+            part[0, :, lanes] = (w0 * intra + w1 * near).astype(BF)
+            part[1, :, lanes] = (dot(score, k, 1, 0) + dot(g1, level, 1, 1)).astype(BF)
+            part[2, :, lanes] = (dot(score, q, 0, 0) + dot(v, back, 1, 1)).astype(BF)
+            part[3, :, lanes] = (dot(attend, g0, 0, 0) + dot(k, back, 1, 0)).astype(BF)
             total = jnp.where(to == h * 8, jnp.sum(gf * intra, -1, keepdims=True), total)
             total = jnp.where(to == h * 8 + 1, jnp.sum(gf * near, -1, keepdims=True), total)
         sums[s] = total
@@ -164,55 +186,79 @@
             down[z, 3 + i] = total
 
 
-def final_body(meta, slot, own, other, cols, chosen, part, sums, got, keep, send, logit_grad, rows):
-    core, z, y = meta[0], meta[1], meta[2]
+def level_bits(meta):
+    return [(meta[1 + i // 3] >> (i % 3)) & 1 for i in range(SLOTS)]
+
+
+def bucket_sum(got, h, i):
+    return jnp.concatenate([got[2 * h, i], got[2 * h + 1, i]], 0)
+
+
+def outputs_body(
+    meta, own, other, cols, chosen, part_own, part_other, sums, got, new_own, new_other, logit_grad, rows
+):
+    core = meta[0]
+    bits = level_bits(meta)
     lane = lax.broadcasted_iota(jnp.int32, (2 * SPAN, 128), 1)
     both = jnp.concatenate([cols[0], cols[1]], 0)
     total = jnp.concatenate([sums[0], sums[1]], 0)
     for h in range(HALF):
         lanes = slice(h * DK, (h + 1) * DK)
-        q, k, v, g = (
-            jnp.concatenate([own[i, :, lanes], other[i, :, lanes]], 0) for i in range(4)
-        )
-        gf = g.astype(F32)
+        q = jnp.concatenate([own[0, :, lanes], other[0, :, lanes]], 0)
+        gf = jnp.concatenate([own[3, :, lanes], other[3, :, lanes]], 0).astype(F32)
         levels = []
-        back = jnp.zeros((DK, DK), F32)
         for i in range(SLOTS):
-            bit = (z >> i) & 1 if i < 3 else (y >> (i - 3)) & 1
-            state = jnp.concatenate([got[2 * h, i], got[2 * h + 1, i]], 0)
-            zero = jnp.zeros_like(state)
-            levels.append(jnp.where(bit == 1, state, zero))
-            back = back + jnp.where(bit == 1, zero, state).astype(F32)
-        back = back.astype(BF)
-        levels = jnp.concatenate(levels, 1)
-        outs = dot(q, levels, 1, 0)
-        mixed = jnp.concatenate([part[0, 0, :, lanes], part[1, 0, :, lanes]], 0)
-        weighted = []
+            state = bucket_sum(got, h, i)
+            levels.append(jnp.where(bits[i] == 1, state, jnp.zeros_like(state)))
+        outs = dot(q, jnp.concatenate(levels, 1), 1, 0)
+        mix = jnp.concatenate([part_own[0, :, lanes], part_other[0, :, lanes]], 0).astype(F32)
         for i in range(SLOTS):
-            w = both[:, h * 8 + 2 + i : h * 8 + 3 + i]
             out = outs[:, i * DK : (i + 1) * DK]
-            mixed = mixed + w * out
-            weighted.append((w * gf).astype(BF))
+            mix = mix + both[:, h * 8 + 2 + i : h * 8 + 3 + i] * out
             total = jnp.where(lane == h * 8 + 2 + i, jnp.sum(gf * out, -1, keepdims=True), total)
-        dq = dot(jnp.concatenate(weighted, 1), levels, 1, 1)
-        dk = dot(v, back, 1, 1)
-        dv = dot(k, back, 1, 0)
-        for s, dst in enumerate((keep, send)):
-            span = slice(s * SPAN, (s + 1) * SPAN)
-            dst[0, :, lanes] = mixed[span].astype(BF)
-            dst[1, :, lanes] = (part[s, 1, :, lanes] + dq[span]).astype(BF)
-            dst[2, :, lanes] = (part[s, 2, :, lanes] + dk[span]).astype(BF)
-            dst[3, :, lanes] = (part[s, 3, :, lanes] + dv[span]).astype(BF)
+        new_own[0, :, lanes] = mix[:SPAN].astype(BF)
+        new_other[0, :, lanes] = mix[SPAN:].astype(BF)
     for s in range(2):
         c = core if s == 0 else 1 - core
         by_level = jnp.transpose(total[s * SPAN : (s + 1) * SPAN])[: 8 * HALF]
         by_level = by_level * jax.nn.sigmoid(chosen[:, s * SPAN : (s + 1) * SPAN])
         for h in range(HALF):
             for l in range(8):
-                rows[pl.ds(h * 8 + slot[l], 1), :] = by_level[h * 8 + l : h * 8 + l + 1, :]
+                rows[pl.ds(h * 8 + meta[3 + l], 1), :] = by_level[h * 8 + l : h * 8 + l + 1, :]
         ready = rows[...].astype(BF)
         for x in range(4):
             logit_grad[c * 4 + x] = ready
+
+
+def grads_body(meta, own, other, cols, part_own, part_other, got, keep, send):
+    bits = level_bits(meta)
+    both = jnp.concatenate([cols[0], cols[1]], 0)
+    for h in range(HALF):
+        lanes = slice(h * DK, (h + 1) * DK)
+        k, v, g = (
+            jnp.concatenate([own[i, :, lanes], other[i, :, lanes]], 0) for i in range(1, 4)
+        )
+        gf = g.astype(F32)
+        levels, weighted = [], []
+        back = jnp.zeros((DK, DK), F32)
+        for i in range(SLOTS):
+            state = bucket_sum(got, h, i)
+            zero = jnp.zeros_like(state)
+            levels.append(jnp.where(bits[i] == 1, state, zero))
+            back = back + jnp.where(bits[i] == 1, zero, state).astype(F32)
+            weighted.append((both[:, h * 8 + 2 + i : h * 8 + 3 + i] * gf).astype(BF))
+        back = back.astype(BF)
+        found = (
+            dot(jnp.concatenate(weighted, 1), jnp.concatenate(levels, 1), 1, 1),
+            dot(v, back, 1, 1),
+            dot(k, back, 1, 0),
+        )
+        for s, (part, dst) in enumerate(((part_own, keep), (part_other, send))):
+            span = slice(s * SPAN, (s + 1) * SPAN)
+            for i in range(3):
+                dst[1 + i, :, lanes] = (
+                    part[1 + i, :, lanes].astype(F32) + found[i][span]
+                ).astype(BF)
 
 
 def unpack_body(meta, keep, got, logit_grad, gate, mixed, dq, dk, dv, dhidden):
@@ -227,7 +273,8 @@
 
 def local(queries, keys, values, hidden, gate_weight, level_slot, out_grad):
     core, z, y = lax.axis_index("core"), lax.axis_index("z"), lax.axis_index("y")
-    meta = jnp.stack([core, z, y]).astype(jnp.int32)
+    place = jnp.stack([core, z, y]).astype(jnp.int32)
+    meta = jnp.concatenate([place, level_slot])
     swap = [(0, 1), (1, 0)]
 
     def exchange(array, axis):
@@ -236,11 +283,17 @@
     send, own, partial = pl.pallas_call(
         pack_body,
         out_shape=(shape(4, SPAN, LANES), shape(4, SPAN, LANES), shape(8, 32, SPAN, kind=F32)),
-        in_specs=smem(1) + vmem(6),
+        in_specs=smem(1) + hbm(6),
         out_specs=tuple(vmem(3)),
+        scratch_shapes=[
+            pltpu.VMEM((4, SPAN, 2 * LANES), BF),
+            pltpu.VMEM(hidden.shape, BF),
+            pltpu.VMEM(gate_weight.shape, BF),
+            pltpu.SemaphoreType.DMA((11,)),
+        ],
         compiler_params=SMALL,
         name="pack",
-    )(meta, queries, keys, values, out_grad, hidden, gate_weight)
+    )(meta, *far(queries, keys, values, out_grad, hidden, gate_weight))
     other = lax.ppermute(send, "core", swap)
     parts = exchange(partial, ("core", "head"))
     up, cols, chosen, near_state, near_grad = pl.pallas_call(
@@ -252,18 +305,18 @@
             shape(HALF, DK, DK),
             shape(HALF, DK, DK),
         ),
-        in_specs=smem(2) + vmem(3),
+        in_specs=smem(1) + vmem(3),
         out_specs=tuple(vmem(5)),
         scratch_shapes=[pltpu.VMEM((8 * HALF, 2 * SPAN), F32)],
         compiler_params=SMALL,
         name="states",
-    )(meta, level_slot, *near(parts, own, other))
+    )(meta, *near(parts, own, other))
     got = exchange(up, "z")
-    part, sums = pl.pallas_call(
+    part_own, part_other, sums = pl.pallas_call(
         local_body,
-        out_shape=(shape(2, 4, SPAN, LANES, kind=F32), shape(2, SPAN, 128, kind=F32)),
+        out_shape=(shape(4, SPAN, LANES), shape(4, SPAN, LANES), shape(2, SPAN, 128, kind=F32)),
         in_specs=smem(1) + vmem(5),
-        out_specs=tuple(vmem(2)),
+        out_specs=tuple(vmem(3)),
         compiler_params=SMALL,
         name="local",
     )(meta, *near(own, other, cols, near_state, near_grad))
@@ -285,17 +338,27 @@
         name="buckets",
     )(meta, *near(got, from_y))
     sums_here = exchange(down, "z")
-    keep, away, logit_grad = pl.pallas_call(
-        final_body,
+    part_own, part_other, logit_grad = pl.pallas_call(
+        outputs_body,
         out_shape=(shape(4, SPAN, LANES), shape(4, SPAN, LANES), shape(8, 8 * HALF, SPAN)),
-        in_specs=smem(2) + vmem(7),
+        in_specs=smem(1) + vmem(8),
         out_specs=tuple(vmem(3)),
         scratch_shapes=[pltpu.VMEM((8 * HALF, SPAN), F32)],
-        compiler_params=SMALL,
-        name="final",
-    )(meta, level_slot, *near(own, other, cols, chosen, part, sums, sums_here))
+        input_output_aliases={5: 0, 6: 1},
+        compiler_params=SMALL,
+        name="outputs",
+    )(meta, *near(own, other, cols, chosen, part_own, part_other, sums, sums_here))
+    all_grads = exchange(logit_grad, ("core", "head"))
+    keep, away = pl.pallas_call(
+        grads_body,
+        out_shape=(shape(4, SPAN, LANES), shape(4, SPAN, LANES)),
+        in_specs=smem(1) + vmem(6),
+        out_specs=tuple(vmem(2)),
+        input_output_aliases={4: 0, 5: 1},
+        compiler_params=SMALL,
+        name="grads",
+    )(meta, *near(own, other, cols, part_own, part_other, sums_here))
     back = lax.ppermute(away, "core", swap)
-    all_grads = exchange(logit_grad, ("core", "head"))
     outs = (jax.ShapeDtypeStruct((SPAN, 2 * LANES), BF),) * 4
     return pl.pallas_call(
         unpack_body,

time: 116 us -> 111 us (0.957)
  local copies, waits for them, and re-layouts: 9.24 us -> 0.65 us
  Pallas kernels: 12.9 us -> 15.9 us
  waiting for transfers between devices: 16.5 us -> 17.9 us
    unnamed x22 -> x4, local copies, waits for them, and re-layouts: 9.24 us -> 0.65 us
    pallas_call x2 -> x3, Pallas kernels: 6.19 us -> 7.93 us  [the longest x1 3.29 us: local(): pl.pallas_call(outputs_body, out_shape=(shape(4, SPAN, LANES), shape(4, S...]
    all_to_all x1, waiting for transfers between devices: 16.5 us -> 17.9 us  [exchange(): return lax.all_to_all(array, axis, 0, 0, tiled=True)]
    pallas_call x1, Pallas kernels: 0.84 us -> 2.05 us  [local(): pl.pallas_call(pack_body, out_shape=(shape(4, SPAN, LANES), shape(4, SPAN...]
where the time goes in v3:
time: 111 us
  blocking collectives  58.1 us (52%)
  waiting for transfers between devices  17.9 us (16%)
  starting transfers between devices  17.6 us (16%)
  Pallas kernels  15.9 us (14%)
    all_to_all x4, blocking collectives, exchange(): return lax.all_to_all(array, axis, 0, 0, tiled=True)  58.1 us
    all_to_all x1, waiting for transfers between devices, exchange(): return lax.all_to_all(array, axis, 0, 0, tiled=True)  17.9 us
    ppermute x1, starting transfers between devices, local(): other = lax.ppermute(send, 'core', swap)  8.75 us
    ppermute x1, starting transfers between devices, local(): back = lax.ppermute(away, 'core', swap)  5.34 us
    all_to_all x1, starting transfers between devices, exchange(): return lax.all_to_all(array, axis, 0, 0, tiled=True)  3.55 us
    pallas_call x1, Pallas kernels, local(): pl.pallas_call(outputs_body, out_shape=(shape(4, SPAN, LANES), shape(4, S...  3.29 us
    pallas_call x1, Pallas kernels, local(): pl.pallas_call(local_body, out_shape=(shape(4, SPAN, LANES), shape(4, SPA...  2.73 us
  transfers between devices with their start and end apart: 3, of which 1 were waited for; matrix products, arithmetic and copies ran while one was open for 0% of the time, Pallas kernels for 2%

profile of v3, /device:TPU:1, one launch (start us, length us, event | category | flops | bytes accessed | tf_op | source)
XLA Modules:
  0.0 110.9 jit_solution(11544340509410922300)
XLA Ops:
  0.6 0.0 copy-start.1
  0.6 0.6 copy-done.1
  1.3 0.1 pad_add_fusion.meta
  1.4 2.1 %pack.1 = (bf16[4,128,512]{2,1,0:T(8,128)(2,1)S(1)}, bf16[4,128,512]{2,1,0:T(8,128)(2,1)S(1)}, f32[8,32,128]{2,1,0:T(8,128)S(1)}) custom-call(s32[11]{0:T(128)S(1)} %pad_add_fusion.meta, bf16[128,1024]{1,0:T(8,128)(2,1)} %q.1, bf16[128,1024]{1,0:T(8,128)(2,1)} %k.1, bf16[128,1024]{1,0:T(8,128)(2,1)} %v.1, bf16[128,1024]{1,0:T(8,128)(2,1)} %g.1, ...), custom_call_target="tpu_custom_call" | custom-call | tf_op jit(solution)/shard_map/pack/pallas_call | solution.py:283
  3.4 8.7 %collective-permute-start = (bf16[4,128,512]{2,1,0:T(8,128)(2,1)S(1)}, bf16[4,128,512]{2,1,0:T(8,128)(2,1)S(1)}, u32[]{:S(2)}, u32[]{:S(2)}) collective-permute-start(bf16[4,128,512]{2,1,0:T(8,128)(2,1)S(1)} %get-tuple-element.22), channel_id=1, source_target_pairs={{0,4},{4,0},{1,5},{5,1},{2,6},{6,2},{3,7},{7,3},{8,12},{12,8},{9,1... | collective-permute-start | bytes 1572872 | tf_op jit(solution)/shard_map/ppermute | solution.py:297
  12.2 7.6 %all_to_all.25.parts = f32[8,32,128]{2,1,0:T(8,128)S(1)} all-to-all(f32[8,32,128]{2,1,0:T(8,128)S(1)} %get-tuple-element.23), channel_id=1, replica_groups=mesh['y'=8,'z'=8,'core'=2,'head'=4] {'core','head'}, dimensions={0} | all-to-all | bytes 262144 | tf_op jit(solution)/shard_map/all_to_all | solution.py:281
  19.8 0.0 collective-permute-done.other
  19.8 2.1 %states.1 = (bf16[8,6,64,128]{3,2,1,0:T(8,128)(2,1)S(1)}, f32[2,128,128]{2,1,0:T(8,128)S(1)}, f32[32,256]{1,0:T(8,128)S(1)}, bf16[4,128,128]{2,1,0:T(8,128)(2,1)S(1)}, bf16[4,128,128]{2,1,0:T(8,128)(2,1)S(1)}) custom-call(s32[11]{0:T(128)S(1)} %pad_add_fusion.meta, f32[8,32,128]{2,1,0:T(8,128)S(1)} %all_to_all.25.parts, ...), custom_call_target="tpu_custom_call" | custom-call | tf_op jit(solution)/shard_map/states/pallas_call | solution.py:299
  21.9 28.6 %all_to_all.26.got = bf16[8,6,64,128]{3,2,1,0:T(8,128)(2,1)S(1)} all-to-all(bf16[8,6,64,128]{3,2,1,0:T(8,128)(2,1)S(1)} %get-tuple-element.31), channel_id=1, replica_groups=mesh['y'=8,'z'=8,'core'=2,'head'=4] {'z'}, dimensions={0} | all-to-all | bytes 1572864 | tf_op jit(solution)/shard_map/all_to_all | solution.py:281
  50.5 0.6 along_z.1
  51.1 14.6 %all_to_all.27.from_y = bf16[8,64,128]{2,1,0:T(8,128)(2,1)S(1)} all-to-all(bf16[8,64,128]{2,1,0:T(8,128)(2,1)S(1)} %along_z.1), channel_id=1, replica_groups=mesh['y'=8,'z'=8,'core'=2,'head'=4] {'y'}, dimensions={0} | all-to-all | bytes 262144 | tf_op jit(solution)/shard_map/all_to_all | solution.py:281
  65.7 1.5 %buckets.1 = bf16[8,6,64,128]{3,2,1,0:T(8,128)(2,1)} custom-call(s32[11]{0:T(128)S(1)} %pad_add_fusion.meta, bf16[8,6,64,128]{3,2,1,0:T(8,128)(2,1)S(1)} %all_to_all.26.got, bf16[8,64,128]{2,1,0:T(8,128)(2,1)S(1)} %all_to_all.27.from_y), custom_call_target="tpu_custom_call" | custom-call | tf_op jit(solution)/shard_map/buckets/pallas_call | solution.py:332
  67.2 3.5 %all-to-all-start.3 = ((bf16[8,6,64,128]{3,2,1,0:T(8,128)(2,1)}), bf16[8,6,64,128]{3,2,1,0:T(8,128)(2,1)S(1)}, u32[]{:S(2)}, u32[]{:S(2)}) async-start(bf16[8,6,64,128]{3,2,1,0:T(8,128)(2,1)} %buckets.1), calls=%async_computation.3 | async-start | bytes 1572864 | tf_op jit(solution)/shard_map/all_to_all | solution.py:281
  70.8 2.7 %local.1 = (bf16[4,128,512]{2,1,0:T(8,128)(2,1)S(1)}, bf16[4,128,512]{2,1,0:T(8,128)(2,1)S(1)}, f32[2,128,128]{2,1,0:T(8,128)S(1)}) custom-call(s32[11]{0:T(128)S(1)} %pad_add_fusion.meta, bf16[4,128,512]{2,1,0:T(8,128)(2,1)S(1)} %get-tuple-element.21.own, bf16[4,128,512]{2,1,0:T(8,128)(2,1)S(1)} %collective-permute-done.other, ...), custom_call_target="tpu_custom_call" | custom-call | tf_op jit(solution)/shard_map/local/pallas_call | solution.py:315
  73.5 17.9 %all-to-all-done.3.got = bf16[8,6,64,128]{3,2,1,0:T(8,128)(2,1)S(1)} async-done(((bf16[8,6,64,128]{3,2,1,0:T(8,128)(2,1)}), bf16[8,6,64,128]{3,2,1,0:T(8,128)(2,1)S(1)}, u32[]{:S(2)}, u32[]{:S(2)}) %all-to-all-start.3) | async-done | bytes 786464 | tf_op jit(solution)/shard_map/all_to_all | solution.py:281
  91.4 3.3 %outputs.1 = (bf16[4,128,512]{2,1,0:T(8,128)(2,1)S(1)}, bf16[4,128,512]{2,1,0:T(8,128)(2,1)S(1)}, bf16[8,32,128]{2,1,0:T(8,128)(2,1)S(1)}) custom-call(s32[11]{0:T(128)S(1)} %pad_add_fusion.meta, bf16[4,128,512]{2,1,0:T(8,128)(2,1)S(1)} %get-tuple-element.21.own, ...), custom_call_target="tpu_custom_call", output_to_operand_aliasing={{0}: (5, {}), {1}: (6, {})} | custom-call | tf_op jit(solution)/shard_map/outputs/pallas_call | solution.py:341
  94.7 0.0 copy-start
  94.7 1.9 %grads.1 = (bf16[4,128,512]{2,1,0:T(8,128)(2,1)S(1)}, bf16[4,128,512]{2,1,0:T(8,128)(2,1)S(1)}) custom-call(s32[11]{0:T(128)S(1)} %pad_add_fusion.meta, bf16[4,128,512]{2,1,0:T(8,128)(2,1)S(1)} %get-tuple-element.21.own, bf16[4,128,512]{2,1,0:T(8,128)(2,1)S(1)} %collective-permute-done.other, ...), custom_call_target="tpu_custom_call", output_to_operand_aliasing={{0}: (4, {}), {1}: (5, {})} | custom-call | tf_op jit(solution)/shard_map/grads/pallas_call | solution.py:352
  96.6 5.3 %collective-permute-start.1 = (bf16[4,128,512]{2,1,0:T(8,128)(2,1)S(1)}, bf16[4,128,512]{2,1,0:T(8,128)(2,1)S(1)}, u32[]{:S(2)}, u32[]{:S(2)}) collective-permute-start(bf16[4,128,512]{2,1,0:T(8,128)(2,1)S(1)} %get-tuple-element.35), channel_id=1, source_target_pairs={{0,4},{4,0},{1,5},{5,1},{2,6},{6,2},{3,7},{7,3},{8,12},{12,8},{9,1... | collective-permute-start | bytes 1572872 | tf_op jit(solution)/shard_map/ppermute | solution.py:361
  101.9 7.3 %all_to_all.28.logit_grad = bf16[8,32,128]{2,1,0:T(8,128)(2,1)S(1)} all-to-all(bf16[8,32,128]{2,1,0:T(8,128)(2,1)S(1)} %get-tuple-element.36), channel_id=1, replica_groups=mesh['y'=8,'z'=8,'core'=2,'head'=4] {'core','head'}, dimensions={0} | all-to-all | bytes 131072 | tf_op jit(solution)/shard_map/all_to_all | solution.py:281
  109.3 0.0 collective-permute-done.1.got
  109.3 0.0 copy-done
  109.3 1.7 %unpack.1 = (bf16[128,1024]{1,0:T(8,128)(2,1)}, bf16[128,1024]{1,0:T(8,128)(2,1)}, bf16[128,1024]{1,0:T(8,128)(2,1)}, bf16[128,1024]{1,0:T(8,128)(2,1)}, bf16[128,512]{1,0:T(8,128)(2,1)}) custom-call(s32[11]{0:T(128)S(1)} %pad_add_fusion.meta, bf16[4,128,512]{2,1,0:T(8,128)(2,1)S(1)} %get-tuple-element.34.keep, ...), custom_call_target="tpu_custom_call" | custom-call | tf_op jit(solution)/shard_map/unpack/pallas_call | solution.py:363
Async XLA Ops:
  0.6 0.7 copy-start.1
  3.4 16.3 %collective-permute-start = (bf16[4,128,512]{2,1,0:T(8,128)(2,1)S(1)}, bf16[4,128,512]{2,1,0:T(8,128)(2,1)S(1)}, u32[]{:S(2)}, u32[]{:S(2)}) collective-permute-start(bf16[4,128,512]{2,1,0:T(8,128)(2,1)S(1)} %get-tuple-element.22), channel_id=1, source_target_pairs={{0,4},{4,0},{1,5},{5,1},{2,6},{6,2},{3,7},{7,3},{8,12},{12,8},{9,1... | collective-permute-start | bytes 1572872 | tf_op jit(solution)/shard_map/ppermute | solution.py:297
  67.2 24.1 %all-to-all-start.3 = ((bf16[8,6,64,128]{3,2,1,0:T(8,128)(2,1)}), bf16[8,6,64,128]{3,2,1,0:T(8,128)(2,1)S(1)}, u32[]{:S(2)}, u32[]{:S(2)}) async-start(bf16[8,6,64,128]{3,2,1,0:T(8,128)(2,1)} %buckets.1), calls=%async_computation.3 | async-start | bytes 1572864 | tf_op jit(solution)/shard_map/all_to_all | solution.py:281
  94.7 14.6 %copy-start = (bf16[512,256]{1,0:T(8,128)(2,1)S(1)}, bf16[512,256]{1,0:T(8,128)(2,1)}, u32[]{:S(2)}) copy-start(bf16[512,256]{1,0:T(8,128)(2,1)} %gate.3) | copy-start | bytes 786436
  96.6 12.7 %collective-permute-start.1 = (bf16[4,128,512]{2,1,0:T(8,128)(2,1)S(1)}, bf16[4,128,512]{2,1,0:T(8,128)(2,1)S(1)}, u32[]{:S(2)}, u32[]{:S(2)}) collective-permute-start(bf16[4,128,512]{2,1,0:T(8,128)(2,1)S(1)} %get-tuple-element.35), channel_id=1, source_target_pairs={{0,4},{4,0},{1,5},{5,1},{2,6},{6,2},{3,7},{7,3},{8,12},{12,8},{9,1... | collective-permute-start | bytes 1572872 | tf_op jit(solution)/shard_map/ppermute | solution.py:361

commit v4 on v3

--- a/solution.py
+++ b/solution.py
@@ -11,6 +11,8 @@
 HALF = 4
 LANES = HALF * DK
 SLOTS = 6
+DIRECT = 2
+SPREAD = SLOTS - DIRECT
 BF = jnp.bfloat16
 F32 = jnp.float32
 
@@ -46,7 +48,7 @@
 SMALL = pltpu.CompilerParams(vmem_limit_bytes=16 << 20)
 
 
-def pack_body(meta, q, k, v, g, hidden, gate, send, own, partial, held, held_hidden, held_gate, sems):
+def pack_body(q, k, v, g, hidden, gate, send, own, partial, held, held_hidden, held_gate, sems):
     copies = [
         pltpu.make_async_copy(hidden, held_hidden, sems.at[0]),
         pltpu.make_async_copy(gate.at[:256], held_gate.at[:256], sems.at[1]),
@@ -67,7 +69,7 @@
         for x in range(4):
             row = x * 64 + c * 32
             partial[c * 4 + x] = logits[row : row + 32]
-    first = meta[0] == 0
+    first = lax.axis_index("core") == 0
     for i in range(4):
         copies[3 + 2 * i].wait()
         copies[4 + 2 * i].wait()
@@ -76,7 +78,7 @@
         send[i] = jnp.where(first, high, low)
 
 
-def states_body(meta, parts, own, other, up, cols, chosen, near_state, near_grad, rows):
+def states_body(meta, parts, own, other, up, pair, cols, chosen, near_state, near_grad, rows):
     core, z, y = meta[0], meta[1], meta[2]
     for s in range(2):
         c = core if s == 0 else 1 - core
@@ -112,8 +114,11 @@
         for i in range(SLOTS):
             bit = (z >> i) & 1 if i < 3 else (y >> (i - 3)) & 1
             piece = jnp.where(bit == 1, grads[:, i * DK : (i + 1) * DK], state).astype(BF)
-            up[2 * h, i] = piece[:64]
-            up[2 * h + 1, i] = piece[64:]
+            if i < DIRECT:
+                pair[i, h] = piece
+            else:
+                up[2 * h, i - DIRECT] = piece[:64]
+                up[2 * h + 1, i - DIRECT] = piece[64:]
 
 
 def local_body(meta, own, other, cols, near_state, near_grad, part_own, part_other, sums):
@@ -149,10 +154,10 @@
         sums[s] = total
 
 
-def along_z_body(meta, got, send):
+def along_z_body(meta, got, send, halves):
     y = meta[2]
     totals = []
-    for i in range(3, SLOTS):
+    for i in range(SPREAD - 3, SPREAD):
         total = got[0, i].astype(F32)
         for z in range(1, 8):
             total = total + got[z, i].astype(F32)
@@ -160,42 +165,48 @@
     send[y] = jnp.zeros_like(totals[0])
     for step in range(1, 8):
         send[y ^ step] = totals[step.bit_length() - 1]
-
-
-def buckets_body(meta, got, from_y, down):
+    for half in range(2):
+        total = got[4 * half, 0].astype(F32)
+        for z in range(4 * half + 1, 4 * half + 4):
+            total = total + got[z, 0].astype(F32)
+        halves[half] = (total * (1.0 / (8 * SPAN))).astype(BF)
+
+
+def pair_body(pair, pair_got, pair_sum):
+    for h in range(HALF):
+        pair_sum[h] = (pair[1, h].astype(F32) + pair_got[1, h].astype(F32)).astype(BF)
+
+
+def buckets_body(meta, halves, from_y, pair_got, quad_got, down, direct):
     y = meta[2]
+    for z in range(8):
+        down[z, 0] = halves[1 - z // 4]
     for i in range(3):
         width = 1 << i
-        scale = 1.0 / (2 * width * SPAN)
-        for block in range(8 // width):
-            total = got[block * width, i].astype(F32)
-            for z in range(block * width + 1, (block + 1) * width):
-                total = total + got[z, i].astype(F32)
-            total = (total * scale).astype(BF)
-            target = block ^ 1
-            for z in range(target * width, (target + 1) * width):
-                down[z, i] = total
-    for i in range(3):
-        width = 1 << i
-        scale = 1.0 / (16 * width * SPAN)
         total = from_y[y ^ width].astype(F32)
         for step in range(width + 1, 2 * width):
             total = total + from_y[y ^ step].astype(F32)
-        total = (total * scale).astype(BF)
+        total = (total * (1.0 / (16 * width * SPAN))).astype(BF)
         for z in range(8):
-            down[z, 3 + i] = total
+            down[z, 1 + i] = total
+    for h in range(HALF):
+        direct[0, h] = pair_got[0, h] * (1.0 / (2 * SPAN))
+        direct[1, h] = quad_got[h] * (1.0 / (4 * SPAN))
 
 
 def level_bits(meta):
     return [(meta[1 + i // 3] >> (i % 3)) & 1 for i in range(SLOTS)]
 
 
-def bucket_sum(got, h, i):
-    return jnp.concatenate([got[2 * h, i], got[2 * h + 1, i]], 0)
+def bucket_sum(direct, got, h, i):
+    if i < DIRECT:
+        return direct[i, h]
+    return jnp.concatenate([got[2 * h, i - DIRECT], got[2 * h + 1, i - DIRECT]], 0)
 
 
 def outputs_body(
-    meta, own, other, cols, chosen, part_own, part_other, sums, got, new_own, new_other, logit_grad, rows
+    meta, own, other, cols, chosen, part_own, part_other, sums, direct, got,
+    new_own, new_other, logit_grad, rows,
 ):
     core = meta[0]
     bits = level_bits(meta)
@@ -208,7 +219,7 @@
         gf = jnp.concatenate([own[3, :, lanes], other[3, :, lanes]], 0).astype(F32)
         levels = []
         for i in range(SLOTS):
-            state = bucket_sum(got, h, i)
+            state = bucket_sum(direct, got, h, i)
             levels.append(jnp.where(bits[i] == 1, state, jnp.zeros_like(state)))
         outs = dot(q, jnp.concatenate(levels, 1), 1, 0)
         mix = jnp.concatenate([part_own[0, :, lanes], part_other[0, :, lanes]], 0).astype(F32)
@@ -230,7 +241,7 @@
             logit_grad[c * 4 + x] = ready
 
 
-def grads_body(meta, own, other, cols, part_own, part_other, got, keep, send):
+def grads_body(meta, own, other, cols, part_own, part_other, direct, got, keep, send):
     bits = level_bits(meta)
     both = jnp.concatenate([cols[0], cols[1]], 0)
     for h in range(HALF):
@@ -242,7 +253,7 @@
         levels, weighted = [], []
         back = jnp.zeros((DK, DK), F32)
         for i in range(SLOTS):
-            state = bucket_sum(got, h, i)
+            state = bucket_sum(direct, got, h, i)
             zero = jnp.zeros_like(state)
             levels.append(jnp.where(bits[i] == 1, state, zero))
             back = back + jnp.where(bits[i] == 1, zero, state).astype(F32)
@@ -280,10 +291,13 @@
     def exchange(array, axis):
         return lax.all_to_all(array, axis, 0, 0, tiled=True)
 
+    def flip(array, distance):
+        return lax.ppermute(array, "z", [(i, i ^ distance) for i in range(8)])
+
     send, own, partial = pl.pallas_call(
         pack_body,
         out_shape=(shape(4, SPAN, LANES), shape(4, SPAN, LANES), shape(8, 32, SPAN, kind=F32)),
-        in_specs=smem(1) + hbm(6),
+        in_specs=hbm(6),
         out_specs=tuple(vmem(3)),
         scratch_shapes=[
             pltpu.VMEM((4, SPAN, 2 * LANES), BF),
@@ -293,25 +307,45 @@
         ],
         compiler_params=SMALL,
         name="pack",
-    )(meta, *far(queries, keys, values, out_grad, hidden, gate_weight))
+    )(*far(queries, keys, values, out_grad, hidden, gate_weight))
     other = lax.ppermute(send, "core", swap)
     parts = exchange(partial, ("core", "head"))
-    up, cols, chosen, near_state, near_grad = pl.pallas_call(
+    up, pair, cols, chosen, near_state, near_grad = pl.pallas_call(
         states_body,
         out_shape=(
-            shape(8, SLOTS, 64, DK),
+            shape(8, SPREAD, 64, DK),
+            shape(DIRECT, HALF, DK, DK),
             shape(2, SPAN, 128, kind=F32),
             shape(8 * HALF, 2 * SPAN, kind=F32),
             shape(HALF, DK, DK),
             shape(HALF, DK, DK),
         ),
         in_specs=smem(1) + vmem(3),
-        out_specs=tuple(vmem(5)),
+        out_specs=tuple(vmem(6)),
         scratch_shapes=[pltpu.VMEM((8 * HALF, 2 * SPAN), F32)],
         compiler_params=SMALL,
         name="states",
     )(meta, *near(parts, own, other))
+    pair_got = flip(pair, 1)
     got = exchange(up, "z")
+    to_y, halves = pl.pallas_call(
+        along_z_body,
+        out_shape=(shape(8, 64, DK), shape(2, 64, DK)),
+        in_specs=smem(1) + vmem(1),
+        out_specs=tuple(vmem(2)),
+        compiler_params=SMALL,
+        name="along_z",
+    )(meta, *near(got))
+    pair_sum = pl.pallas_call(
+        pair_body,
+        out_shape=shape(HALF, DK, DK),
+        in_specs=vmem(2),
+        out_specs=vmem(1)[0],
+        compiler_params=SMALL,
+        name="pair",
+    )(*near(pair, pair_got))
+    quad_got = flip(pair_sum, 2)
+    from_y = exchange(to_y, "y")
     part_own, part_other, sums = pl.pallas_call(
         local_body,
         out_shape=(shape(4, SPAN, LANES), shape(4, SPAN, LANES), shape(2, SPAN, 128, kind=F32)),
@@ -320,44 +354,35 @@
         compiler_params=SMALL,
         name="local",
     )(meta, *near(own, other, cols, near_state, near_grad))
-    to_y = pl.pallas_call(
-        along_z_body,
-        out_shape=shape(8, 64, DK),
-        in_specs=smem(1) + vmem(1),
-        out_specs=vmem(1)[0],
-        compiler_params=SMALL,
-        name="along_z",
-    )(meta, *near(got))
-    from_y = exchange(to_y, "y")
-    down = pl.pallas_call(
+    down, direct = pl.pallas_call(
         buckets_body,
-        out_shape=shape(8, SLOTS, 64, DK),
-        in_specs=smem(1) + vmem(2),
-        out_specs=vmem(1)[0],
+        out_shape=(shape(8, SPREAD, 64, DK), shape(DIRECT, HALF, DK, DK)),
+        in_specs=smem(1) + vmem(4),
+        out_specs=tuple(vmem(2)),
         compiler_params=SMALL,
         name="buckets",
-    )(meta, *near(got, from_y))
+    )(meta, *near(halves, from_y, pair_got, quad_got))
     sums_here = exchange(down, "z")
     part_own, part_other, logit_grad = pl.pallas_call(
         outputs_body,
         out_shape=(shape(4, SPAN, LANES), shape(4, SPAN, LANES), shape(8, 8 * HALF, SPAN)),
-        in_specs=smem(1) + vmem(8),
+        in_specs=smem(1) + vmem(9),
         out_specs=tuple(vmem(3)),
         scratch_shapes=[pltpu.VMEM((8 * HALF, SPAN), F32)],
         input_output_aliases={5: 0, 6: 1},
         compiler_params=SMALL,
         name="outputs",
-    )(meta, *near(own, other, cols, chosen, part_own, part_other, sums, sums_here))
+    )(meta, *near(own, other, cols, chosen, part_own, part_other, sums, direct, sums_here))
     all_grads = exchange(logit_grad, ("core", "head"))
     keep, away = pl.pallas_call(
         grads_body,
         out_shape=(shape(4, SPAN, LANES), shape(4, SPAN, LANES)),
-        in_specs=smem(1) + vmem(6),
+        in_specs=smem(1) + vmem(7),
         out_specs=tuple(vmem(2)),
         input_output_aliases={4: 0, 5: 1},
         compiler_params=SMALL,
         name="grads",
-    )(meta, *near(own, other, cols, part_own, part_other, sums_here))
+    )(meta, *near(own, other, cols, part_own, part_other, direct, sums_here))
     back = lax.ppermute(away, "core", swap)
     outs = (jax.ShapeDtypeStruct((SPAN, 2 * LANES), BF),) * 4
     return pl.pallas_call(

time: 111 us -> 102 us (0.919)
  blocking collectives: 58.1 us -> 7.42 us
  starting transfers between devices: 17.6 us -> 39.1 us
  waiting for transfers between devices: 17.9 us -> 36.5 us
  Pallas kernels: 15.9 us -> 17.4 us
    all_to_all x4 -> x1, blocking collectives: 58.1 us -> 7.42 us  [exchange(): return lax.all_to_all(array, axis, 0, 0, tiled=True)]
    all_to_all x1 -> x4, starting transfers between devices: 3.55 us -> 19.4 us  [exchange(): return lax.all_to_all(array, axis, 0, 0, tiled=True)]
    all_to_all x1 -> x4, waiting for transfers between devices: 17.9 us -> 30.9 us  [exchange(): return lax.all_to_all(array, axis, 0, 0, tiled=True)]
    ppermute x0 -> x2, waiting for transfers between devices: none -> 5.64 us  [flip(): return lax.ppermute(array, 'z', [(i, i ^ distance) for i in range(8)])]
    ppermute x0 -> x2, starting transfers between devices: none -> 5.28 us  [flip(): return lax.ppermute(array, 'z', [(i, i ^ distance) for i in range(8)])]
    pallas_call x3 -> x4, Pallas kernels: 4.22 us -> 5.62 us  [the longest x1 2.91 us: local(): pl.pallas_call(states_body, out_shape=(shape(8, SPREAD, 64, DK), shape(DI...]
  transfers between devices with their start and end apart: 3 -> 8, of which waited for: 1 -> 5; matrix products, arithmetic and copies ran while one was open for 0% -> 0% of each run, Pallas kernels for 2% -> 4%
where the time goes in v4:
time: 102 us
  starting transfers between devices  39.1 us (38%)
  waiting for transfers between devices  36.5 us (36%)
  Pallas kernels  17.4 us (17%)
  blocking collectives  7.42 us (7%)
    all_to_all x4, waiting for transfers between devices, exchange(): return lax.all_to_all(array, axis, 0, 0, tiled=True)  30.9 us
    all_to_all x4, starting transfers between devices, exchange(): return lax.all_to_all(array, axis, 0, 0, tiled=True)  19.4 us
    ppermute x1, starting transfers between devices, local(): other = lax.ppermute(send, 'core', swap)  8.75 us
    all_to_all x1, blocking collectives, exchange(): return lax.all_to_all(array, axis, 0, 0, tiled=True)  7.42 us
    ppermute x2, waiting for transfers between devices, flip(): return lax.ppermute(array, 'z', [(i, i ^ distance) for i in range(8)])  5.64 us
    ppermute x1, starting transfers between devices, local(): back = lax.ppermute(away, 'core', swap)  5.61 us
    ppermute x2, starting transfers between devices, flip(): return lax.ppermute(array, 'z', [(i, i ^ distance) for i in range(8)])  5.28 us
    pallas_call x1, Pallas kernels, local(): pl.pallas_call(outputs_body, out_shape=(shape(4, SPAN, LANES), shape(4, S...  3.32 us
  transfers between devices with their start and end apart: 8, of which 5 were waited for; matrix products, arithmetic and copies ran while one was open for 0% of the time, Pallas kernels for 4%

profile of v4, /device:TPU:1, one launch (start us, length us, event | category | flops | bytes accessed | tf_op | source)
XLA Modules:
  0.0 101.9 jit_solution(15861974101764170236)
XLA Ops:
  0.6 2.2 %pack.1 = (bf16[4,128,512]{2,1,0:T(8,128)(2,1)S(1)}, bf16[4,128,512]{2,1,0:T(8,128)(2,1)S(1)}, f32[8,32,128]{2,1,0:T(8,128)}) custom-call(bf16[128,1024]{1,0:T(8,128)(2,1)} %q.1, bf16[128,1024]{1,0:T(8,128)(2,1)} %k.1, bf16[128,1024]{1,0:T(8,128)(2,1)} %v.1, bf16[128,1024]{1,0:T(8,128)(2,1)} %g.1, bf16[128,512]{1,0:T(8,128)(2,1)} %hidden.1, ...), custom_call_target="tpu_custom_call" | custom-call | tf_op jit(solution)/shard_map/pack/pallas_call | solution.py:297
  2.8 8.7 %collective-permute-start = (bf16[4,128,512]{2,1,0:T(8,128)(2,1)S(1)}, bf16[4,128,512]{2,1,0:T(8,128)(2,1)S(1)}, u32[]{:S(2)}, u32[]{:S(2)}) collective-permute-start(bf16[4,128,512]{2,1,0:T(8,128)(2,1)S(1)} %get-tuple-element.27), channel_id=1, source_target_pairs={{0,4},{4,0},{1,5},{5,1},{2,6},{6,2},{3,7},{7,3},{8,12},{12,8},{9,1... | collective-permute-start | bytes 1572872 | tf_op jit(solution)/shard_map/ppermute | solution.py:311
  11.5 3.3 %all-to-all-start = ((f32[8,32,128]{2,1,0:T(8,128)}), f32[8,32,128]{2,1,0:T(8,128)S(1)}, u32[]{:S(2)}, u32[]{:S(2)}) async-start(f32[8,32,128]{2,1,0:T(8,128)} %get-tuple-element.28), calls=%async_computation | async-start | bytes 262144 | tf_op jit(solution)/shard_map/all_to_all | solution.py:292
  14.9 0.0 copy-start.1
  14.9 0.6 copy-done.1
  15.6 0.1 pad_add_fusion.meta
  15.6 4.4 %all-to-all-done.parts = f32[8,32,128]{2,1,0:T(8,128)S(1)} async-done(((f32[8,32,128]{2,1,0:T(8,128)}), f32[8,32,128]{2,1,0:T(8,128)S(1)}, u32[]{:S(2)}, u32[]{:S(2)}) %all-to-all-start) | async-done | bytes 131104 | tf_op jit(solution)/shard_map/all_to_all | solution.py:292
  20.1 0.0 collective-permute-done.other
  20.1 2.9 %states.1 = (bf16[8,4,64,128]{3,2,1,0:T(8,128)(2,1)}, bf16[2,4,128,128]{3,2,1,0:T(8,128)(2,1)S(1)}, f32[2,128,128]{2,1,0:T(8,128)S(1)}, f32[32,256]{1,0:T(8,128)...) custom-call(s32[11]{0:T(128)S(1)} %pad_add_fusion.meta, f32[8,32,128]{2,1,0:T(8,128)S(1)} %all-to-all-done.parts, ...), custom_call_target="tpu_custom_call" | custom-call | tf_op jit(solution)/shard_map/states/pallas_call | solution.py:313
  23.0 5.8 %all-to-all-start.1 = ((bf16[8,4,64,128]{3,2,1,0:T(8,128)(2,1)}), bf16[8,4,64,128]{3,2,1,0:T(8,128)(2,1)S(1)}, u32[]{:S(2)}, u32[]{:S(2)}) async-start(bf16[8,4,64,128]{3,2,1,0:T(8,128)(2,1)} %get-tuple-element.36), calls=%async_computation.1 | async-start | bytes 1048576 | tf_op jit(solution)/shard_map/all_to_all | solution.py:292
  28.8 3.4 %collective-permute-start.1 = (bf16[2,4,128,128]{3,2,1,0:T(8,128)(2,1)S(1)}, bf16[2,4,128,128]{3,2,1,0:T(8,128)(2,1)S(1)}, u32[]{:S(2)}, u32[]{:S(2)}) collective-permute-start(bf16[2,4,128,128]{3,2,1,0:T(8,128)(2,1)S(1)} %get-tuple-element.39.pair), channel_id=1, source_target_pairs={{0,8},{8,0},{16,24},{24,16},{32,40},{40,32},{48,56},{56,48},{1,9},... | collective-permute-start | bytes 786440 | tf_op jit(solution)/shard_map/ppermute | solution.py:295
  32.1 14.4 %all-to-all-done.1.got = bf16[8,4,64,128]{3,2,1,0:T(8,128)(2,1)S(1)} async-done(((bf16[8,4,64,128]{3,2,1,0:T(8,128)(2,1)}), bf16[8,4,64,128]{3,2,1,0:T(8,128)(2,1)S(1)}, u32[]{:S(2)}, u32[]{:S(2)}) %all-to-all-start.1) | async-done | bytes 524320 | tf_op jit(solution)/shard_map/all_to_all | solution.py:292
  46.5 1.3 %along_z.1 = (bf16[8,64,128]{2,1,0:T(8,128)(2,1)}, bf16[2,64,128]{2,1,0:T(8,128)(2,1)S(1)}) custom-call(s32[11]{0:T(128)S(1)} %pad_add_fusion.meta, bf16[8,4,64,128]{3,2,1,0:T(8,128)(2,1)S(1)} %all-to-all-done.1.got), custom_call_target="tpu_custom_call" | custom-call | tf_op jit(solution)/shard_map/along_z/pallas_call | solution.py:331
  47.8 6.8 %all-to-all-start.2 = ((bf16[8,64,128]{2,1,0:T(8,128)(2,1)}), bf16[8,64,128]{2,1,0:T(8,128)(2,1)S(1)}, u32[]{:S(2)}, u32[]{:S(2)}) async-start(bf16[8,64,128]{2,1,0:T(8,128)(2,1)} %get-tuple-element.38), calls=%async_computation.2 | async-start | bytes 262144 | tf_op jit(solution)/shard_map/all_to_all | solution.py:292
  54.6 0.0 collective-permute-done.1.pair_got
  54.6 1.9 %collective-permute-start.2 = (bf16[4,128,128]{2,1,0:T(8,128)(2,1)S(1)}, bf16[4,128,128]{2,1,0:T(8,128)(2,1)S(1)}, u32[]{:S(2)}, u32[]{:S(2)}) collective-permute-start(bf16[4,128,128]{2,1,0:T(8,128)(2,1)S(1)} %pair.1), channel_id=1, source_target_pairs={{0,16},{8,24},{16,0},{24,8},{32,48},{40,56},{48,32},{56,40},{1,17}... | collective-permute-start | bytes 393224 | tf_op jit(solution)/shard_map/ppermute | solution.py:295
  56.6 5.6 %collective-permute-done.2.quad_got = bf16[4,128,128]{2,1,0:T(8,128)(2,1)S(1)} collective-permute-done((bf16[4,128,128]{2,1,0:T(8,128)(2,1)S(1)}, bf16[4,128,128]{2,1,0:T(8,128)(2,1)S(1)}, u32[]{:S(2)}, u32[]{:S(2)}) %collective-permute-start.2) | collective-permute-done | bytes 131104 | tf_op jit(solution)/shard_map/ppermute | solution.py:295
  62.2 0.1 all-to-all-done.2.from_y
  62.3 1.4 %buckets.1 = (bf16[8,4,64,128]{3,2,1,0:T(8,128)(2,1)}, bf16[2,4,128,128]{3,2,1,0:T(8,128)(2,1)S(1)}) custom-call(s32[11]{0:T(128)S(1)} %pad_add_fusion.meta, bf16[2,64,128]{2,1,0:T(8,128)(2,1)S(1)} %get-tuple-element.37.halves, bf16[8,64,128]{2,1,0:T(8,128)(2,1)S(1)} %all-to-all-done.2.from_y, bf16[2,4,128,128]{3,2,1,0:T(8,128)(2,1)S(1)} %collective-permute-done.1.pair_got, ...), custom_call_target="tpu_custom_call" | custom-call | tf_op jit(solution)/shard_map/buckets/pallas_call | solution.py:357
  63.8 3.5 %all-to-all-start.3 = ((bf16[8,4,64,128]{3,2,1,0:T(8,128)(2,1)}), bf16[8,4,64,128]{3,2,1,0:T(8,128)(2,1)S(1)}, u32[]{:S(2)}, u32[]{:S(2)}) async-start(bf16[8,4,64,128]{3,2,1,0:T(8,128)(2,1)} %get-tuple-element.41), calls=%async_computation.3 | async-start | bytes 1048576 | tf_op jit(solution)/shard_map/all_to_all | solution.py:292
  67.3 2.7 %local.1 = (bf16[4,128,512]{2,1,0:T(8,128)(2,1)S(1)}, bf16[4,128,512]{2,1,0:T(8,128)(2,1)S(1)}, f32[2,128,128]{2,1,0:T(8,128)S(1)}) custom-call(s32[11]{0:T(128)S(1)} %pad_add_fusion.meta, bf16[4,128,512]{2,1,0:T(8,128)(2,1)S(1)} %get-tuple-element.26.own, bf16[4,128,512]{2,1,0:T(8,128)(2,1)S(1)} %collective-permute-done.other, ...), custom_call_target="tpu_custom_call" | custom-call | tf_op jit(solution)/shard_map/local/pallas_call | solution.py:349
  70.0 11.9 %all-to-all-done.3.got = bf16[8,4,64,128]{3,2,1,0:T(8,128)(2,1)S(1)} async-done(((bf16[8,4,64,128]{3,2,1,0:T(8,128)(2,1)}), bf16[8,4,64,128]{3,2,1,0:T(8,128)(2,1)S(1)}, u32[]{:S(2)}, u32[]{:S(2)}) %all-to-all-start.3) | async-done | bytes 524320 | tf_op jit(solution)/shard_map/all_to_all | solution.py:292
  81.9 3.3 %outputs.1 = (bf16[4,128,512]{2,1,0:T(8,128)(2,1)S(1)}, bf16[4,128,512]{2,1,0:T(8,128)(2,1)S(1)}, bf16[8,32,128]{2,1,0:T(8,128)(2,1)S(1)}) custom-call(s32[11]{0:T(128)S(1)} %pad_add_fusion.meta, bf16[4,128,512]{2,1,0:T(8,128)(2,1)S(1)} %get-tuple-element.26.own, ...), custom_call_target="tpu_custom_call", output_to_operand_aliasing={{0}: (5, {}), {1}: (6, {})} | custom-call | tf_op jit(solution)/shard_map/outputs/pallas_call | solution.py:366
  85.2 0.0 copy-start
  85.2 1.9 %grads.1 = (bf16[4,128,512]{2,1,0:T(8,128)(2,1)S(1)}, bf16[4,128,512]{2,1,0:T(8,128)(2,1)S(1)}) custom-call(s32[11]{0:T(128)S(1)} %pad_add_fusion.meta, bf16[4,128,512]{2,1,0:T(8,128)(2,1)S(1)} %get-tuple-element.26.own, bf16[4,128,512]{2,1,0:T(8,128)(2,1)S(1)} %collective-permute-done.other, ...), custom_call_target="tpu_custom_call", output_to_operand_aliasing={{0}: (4, {}), {1}: (5, {})} | custom-call | tf_op jit(solution)/shard_map/grads/pallas_call | solution.py:377
  87.2 5.6 %collective-permute-start.3 = (bf16[4,128,512]{2,1,0:T(8,128)(2,1)S(1)}, bf16[4,128,512]{2,1,0:T(8,128)(2,1)S(1)}, u32[]{:S(2)}, u32[]{:S(2)}) collective-permute-start(bf16[4,128,512]{2,1,0:T(8,128)(2,1)S(1)} %get-tuple-element.45), channel_id=1, source_target_pairs={{0,4},{4,0},{1,5},{5,1},{2,6},{6,2},{3,7},{7,3},{8,12},{12,8},{9,1... | collective-permute-start | bytes 1572872 | tf_op jit(solution)/shard_map/ppermute | solution.py:386
  92.8 7.4 %all_to_all.25.logit_grad = bf16[8,32,128]{2,1,0:T(8,128)(2,1)S(1)} all-to-all(bf16[8,32,128]{2,1,0:T(8,128)(2,1)S(1)} %get-tuple-element.46), channel_id=1, replica_groups=mesh['y'=8,'z'=8,'core'=2,'head'=4] {'core','head'}, dimensions={0} | all-to-all | bytes 131072 | tf_op jit(solution)/shard_map/all_to_all | solution.py:292
  100.2 0.0 collective-permute-done.3.got
  100.2 0.0 copy-done
  100.2 1.7 %unpack.1 = (bf16[128,1024]{1,0:T(8,128)(2,1)}, bf16[128,1024]{1,0:T(8,128)(2,1)}, bf16[128,1024]{1,0:T(8,128)(2,1)}, bf16[128,1024]{1,0:T(8,128)(2,1)}, bf16[128,512]{1,0:T(8,128)(2,1)}) custom-call(s32[11]{0:T(128)S(1)} %pad_add_fusion.meta, bf16[4,128,512]{2,1,0:T(8,128)(2,1)S(1)} %get-tuple-element.44.keep, ...), custom_call_target="tpu_custom_call" | custom-call | tf_op jit(solution)/shard_map/unpack/pallas_call | solution.py:388
  (1 shorter events, 0.0 us)
Async XLA Ops:
  2.8 17.3 %collective-permute-start = (bf16[4,128,512]{2,1,0:T(8,128)(2,1)S(1)}, bf16[4,128,512]{2,1,0:T(8,128)(2,1)S(1)}, u32[]{:S(2)}, u32[]{:S(2)}) collective-permute-start(bf16[4,128,512]{2,1,0:T(8,128)(2,1)S(1)} %get-tuple-element.27), channel_id=1, source_target_pairs={{0,4},{4,0},{1,5},{5,1},{2,6},{6,2},{3,7},{7,3},{8,12},{12,8},{9,1... | collective-permute-start | bytes 1572872 | tf_op jit(solution)/shard_map/ppermute | solution.py:311
  11.5 8.5 %all-to-all-start = ((f32[8,32,128]{2,1,0:T(8,128)}), f32[8,32,128]{2,1,0:T(8,128)S(1)}, u32[]{:S(2)}, u32[]{:S(2)}) async-start(f32[8,32,128]{2,1,0:T(8,128)} %get-tuple-element.28), calls=%async_computation | async-start | bytes 262144 | tf_op jit(solution)/shard_map/all_to_all | solution.py:292
  14.9 0.7 copy-start.1
  23.0 23.5 %all-to-all-start.1 = ((bf16[8,4,64,128]{3,2,1,0:T(8,128)(2,1)}), bf16[8,4,64,128]{3,2,1,0:T(8,128)(2,1)S(1)}, u32[]{:S(2)}, u32[]{:S(2)}) async-start(bf16[8,4,64,128]{3,2,1,0:T(8,128)(2,1)} %get-tuple-element.36), calls=%async_computation.1 | async-start | bytes 1048576 | tf_op jit(solution)/shard_map/all_to_all | solution.py:292
  28.8 25.8 %collective-permute-start.1 = (bf16[2,4,128,128]{3,2,1,0:T(8,128)(2,1)S(1)}, bf16[2,4,128,128]{3,2,1,0:T(8,128)(2,1)S(1)}, u32[]{:S(2)}, u32[]{:S(2)}) collective-permute-start(bf16[2,4,128,128]{3,2,1,0:T(8,128)(2,1)S(1)} %get-tuple-element.39.pair), channel_id=1, source_target_pairs={{0,8},{8,0},{16,24},{24,16},{32,40},{40,32},{48,56},{56,48},{1,9},... | collective-permute-start | bytes 786440 | tf_op jit(solution)/shard_map/ppermute | solution.py:295
  47.8 14.6 %all-to-all-start.2 = ((bf16[8,64,128]{2,1,0:T(8,128)(2,1)}), bf16[8,64,128]{2,1,0:T(8,128)(2,1)S(1)}, u32[]{:S(2)}, u32[]{:S(2)}) async-start(bf16[8,64,128]{2,1,0:T(8,128)(2,1)} %get-tuple-element.38), calls=%async_computation.2 | async-start | bytes 262144 | tf_op jit(solution)/shard_map/all_to_all | solution.py:292
  54.6 7.6 %collective-permute-start.2 = (bf16[4,128,128]{2,1,0:T(8,128)(2,1)S(1)}, bf16[4,128,128]{2,1,0:T(8,128)(2,1)S(1)}, u32[]{:S(2)}, u32[]{:S(2)}) collective-permute-start(bf16[4,128,128]{2,1,0:T(8,128)(2,1)S(1)} %pair.1), channel_id=1, source_target_pairs={{0,16},{8,24},{16,0},{24,8},{32,48},{40,56},{48,32},{56,40},{1,17}... | collective-permute-start | bytes 393224 | tf_op jit(solution)/shard_map/ppermute | solution.py:295
  63.8 18.2 %all-to-all-start.3 = ((bf16[8,4,64,128]{3,2,1,0:T(8,128)(2,1)}), bf16[8,4,64,128]{3,2,1,0:T(8,128)(2,1)S(1)}, u32[]{:S(2)}, u32[]{:S(2)}) async-start(bf16[8,4,64,128]{3,2,1,0:T(8,128)(2,1)} %get-tuple-element.41), calls=%async_computation.3 | async-start | bytes 1048576 | tf_op jit(solution)/shard_map/all_to_all | solution.py:292
  85.2 15.0 %copy-start = (bf16[512,256]{1,0:T(8,128)(2,1)S(1)}, bf16[512,256]{1,0:T(8,128)(2,1)}, u32[]{:S(2)}) copy-start(bf16[512,256]{1,0:T(8,128)(2,1)} %gate.3) | copy-start | bytes 786436
  87.2 13.0 %collective-permute-start.3 = (bf16[4,128,512]{2,1,0:T(8,128)(2,1)S(1)}, bf16[4,128,512]{2,1,0:T(8,128)(2,1)S(1)}, u32[]{:S(2)}, u32[]{:S(2)}) collective-permute-start(bf16[4,128,512]{2,1,0:T(8,128)(2,1)S(1)} %get-tuple-element.45), channel_id=1, source_target_pairs={{0,4},{4,0},{1,5},{5,1},{2,6},{6,2},{3,7},{7,3},{8,12},{12,8},{9,1... | collective-permute-start | bytes 1572872 | tf_op jit(solution)/shard_map/ppermute | solution.py:386

commit v5 on v4

--- a/solution.py
+++ b/solution.py
@@ -78,15 +78,25 @@
         send[i] = jnp.where(first, high, low)
 
 
-def states_body(meta, parts, own, other, up, pair, cols, chosen, near_state, near_grad, rows):
+def pre_body(own, other, state, near_state):
+    first = lax.axis_index("core") == 0
+    for h in range(HALF):
+        lanes = slice(h * DK, (h + 1) * DK)
+        state_own = dot(own[1, :, lanes], own[2, :, lanes], 0, 0)
+        state_other = dot(other[1, :, lanes], other[2, :, lanes], 0, 0)
+        state[h] = (state_own + state_other).astype(BF)
+        near_state[h] = (jnp.where(first, state_own, state_other) / SPAN).astype(BF)
+
+
+def states_body(meta, parts, own, other, state, up, pair, cols, logits, near_grad, chosen):
     core, z, y = meta[0], meta[1], meta[2]
     for s in range(2):
         c = core if s == 0 else 1 - core
-        logits = parts[c * 4] + parts[c * 4 + 1] + parts[c * 4 + 2] + parts[c * 4 + 3]
-        rows[:, s * SPAN : (s + 1) * SPAN] = logits
+        total = parts[c * 4] + parts[c * 4 + 1] + parts[c * 4 + 2] + parts[c * 4 + 3]
+        logits[:, s * SPAN : (s + 1) * SPAN] = total
     for h in range(HALF):
         for l in range(8):
-            chosen[h * 8 + l : h * 8 + l + 1, :] = rows[pl.ds(h * 8 + meta[3 + l], 1), :]
+            chosen[h * 8 + l : h * 8 + l + 1, :] = logits[pl.ds(h * 8 + meta[3 + l], 1), :]
     x = chosen[...]
     weights = jnp.maximum(x, 0.0) + jnp.log1p(jnp.exp(-jnp.abs(x)))
     padded = jnp.concatenate([weights, jnp.zeros((128 - 8 * HALF, 2 * SPAN), F32)], 0)
@@ -98,10 +108,6 @@
         lanes = slice(h * DK, (h + 1) * DK)
         q = jnp.concatenate([own[0, :, lanes], other[0, :, lanes]], 0)
         g = jnp.concatenate([own[3, :, lanes], other[3, :, lanes]], 0).astype(F32)
-        state_own = dot(own[1, :, lanes], own[2, :, lanes], 0, 0)
-        state_other = dot(other[1, :, lanes], other[2, :, lanes], 0, 0)
-        state = state_own + state_other
-        near_state[h] = (jnp.where(first, state_own, state_other) / SPAN).astype(BF)
         near = both[:, h * 8 + 1 : h * 8 + 2]
         near_g = (near * g).astype(BF)
         grad_own = dot(q[:SPAN], near_g[:SPAN], 0, 0)
@@ -111,9 +117,10 @@
             [(both[:, h * 8 + 2 + i : h * 8 + 3 + i] * g).astype(BF) for i in range(SLOTS)], 1
         )
         grads = dot(q, weighted, 0, 0)
+        held = state[h]
         for i in range(SLOTS):
             bit = (z >> i) & 1 if i < 3 else (y >> (i - 3)) & 1
-            piece = jnp.where(bit == 1, grads[:, i * DK : (i + 1) * DK], state).astype(BF)
+            piece = jnp.where(bit == 1, grads[:, i * DK : (i + 1) * DK].astype(BF), held)
             if i < DIRECT:
                 pair[i, h] = piece
             else:
@@ -121,14 +128,20 @@
                 up[2 * h + 1, i - DIRECT] = piece[64:]
 
 
+def row_picker(meta, h, levels):
+    row = lax.broadcasted_iota(jnp.int32, (8 * HALF, DK), 0)
+    return jnp.concatenate(
+        [jnp.where(row == h * 8 + meta[3 + l], 1.0, 0.0).astype(BF) for l in levels], 1
+    )
+
+
 def local_body(meta, own, other, cols, near_state, near_grad, part_own, part_other, sums):
     core = meta[0]
     at = lax.broadcasted_iota(jnp.int32, (SPAN, SPAN), 0)
-    to = lax.broadcasted_iota(jnp.int32, (SPAN, SPAN), 1)
-    causal = at >= to
+    causal = at >= lax.broadcasted_iota(jnp.int32, (SPAN, SPAN), 1)
     for s, (src, part) in enumerate(((own, part_own), (other, part_other))):
         upper = (core == 1) if s == 0 else (core == 0)
-        total = jnp.zeros((SPAN, 128), F32)
+        total = jnp.zeros((8 * HALF, SPAN), F32)
         weights = cols[s]
         for h in range(HALF):
             lanes = slice(h * DK, (h + 1) * DK)
@@ -149,9 +162,9 @@
             part[1, :, lanes] = (dot(score, k, 1, 0) + dot(g1, level, 1, 1)).astype(BF)
             part[2, :, lanes] = (dot(score, q, 0, 0) + dot(v, back, 1, 1)).astype(BF)
             part[3, :, lanes] = (dot(attend, g0, 0, 0) + dot(k, back, 1, 0)).astype(BF)
-            total = jnp.where(to == h * 8, jnp.sum(gf * intra, -1, keepdims=True), total)
-            total = jnp.where(to == h * 8 + 1, jnp.sum(gf * near, -1, keepdims=True), total)
-        sums[s] = total
+            products = jnp.concatenate([(gf * intra).astype(BF), (gf * near).astype(BF)], 1)
+            total = total + dot(row_picker(meta, h, (0, 1)), products, 1, 1)
+        sums[:, s * SPAN : (s + 1) * SPAN] = total
 
 
 def along_z_body(meta, got, send, halves):
@@ -205,14 +218,13 @@
 
 
 def outputs_body(
-    meta, own, other, cols, chosen, part_own, part_other, sums, direct, got,
-    new_own, new_other, logit_grad, rows,
+    meta, own, other, cols, logits, part_own, part_other, sums, direct, got,
+    new_own, new_other, logit_grad,
 ):
     core = meta[0]
     bits = level_bits(meta)
-    lane = lax.broadcasted_iota(jnp.int32, (2 * SPAN, 128), 1)
     both = jnp.concatenate([cols[0], cols[1]], 0)
-    total = jnp.concatenate([sums[0], sums[1]], 0)
+    total = sums[...]
     for h in range(HALF):
         lanes = slice(h * DK, (h + 1) * DK)
         q = jnp.concatenate([own[0, :, lanes], other[0, :, lanes]], 0)
@@ -223,22 +235,21 @@
             levels.append(jnp.where(bits[i] == 1, state, jnp.zeros_like(state)))
         outs = dot(q, jnp.concatenate(levels, 1), 1, 0)
         mix = jnp.concatenate([part_own[0, :, lanes], part_other[0, :, lanes]], 0).astype(F32)
+        products = []
         for i in range(SLOTS):
             out = outs[:, i * DK : (i + 1) * DK]
             mix = mix + both[:, h * 8 + 2 + i : h * 8 + 3 + i] * out
-            total = jnp.where(lane == h * 8 + 2 + i, jnp.sum(gf * out, -1, keepdims=True), total)
+            products.append((gf * out).astype(BF))
+        total = total + dot(
+            row_picker(meta, h, range(2, 8)), jnp.concatenate(products, 1), 1, 1
+        )
         new_own[0, :, lanes] = mix[:SPAN].astype(BF)
         new_other[0, :, lanes] = mix[SPAN:].astype(BF)
+    ready = (total * jax.nn.sigmoid(logits[...])).astype(BF)
     for s in range(2):
         c = core if s == 0 else 1 - core
-        by_level = jnp.transpose(total[s * SPAN : (s + 1) * SPAN])[: 8 * HALF]
-        by_level = by_level * jax.nn.sigmoid(chosen[:, s * SPAN : (s + 1) * SPAN])
-        for h in range(HALF):
-            for l in range(8):
-                rows[pl.ds(h * 8 + meta[3 + l], 1), :] = by_level[h * 8 + l : h * 8 + l + 1, :]
-        ready = rows[...].astype(BF)
         for x in range(4):
-            logit_grad[c * 4 + x] = ready
+            logit_grad[c * 4 + x] = ready[:, s * SPAN : (s + 1) * SPAN]
 
 
 def grads_body(meta, own, other, cols, part_own, part_other, direct, got, keep, send):
@@ -272,14 +283,30 @@
                 ).astype(BF)
 
 
-def unpack_body(meta, keep, got, logit_grad, gate, mixed, dq, dk, dv, dhidden):
-    first = meta[0] == 0
-    for i, dst in enumerate((mixed, dq, dk, dv)):
-        here, there = keep[i], got[i]
-        dst[:, :LANES] = jnp.where(first, here, there)
-        dst[:, LANES:] = jnp.where(first, there, here)
+def first_body(keep, logit_grad, gate, mixed, dq, dk, dv, dhidden, sems):
+    mine = pl.multiple_of(lax.axis_index("core") * LANES, LANES)
+    copies = [
+        pltpu.make_async_copy(keep.at[i], dst.at[:, pl.ds(mine, LANES)], sems.at[i])
+        for i, dst in enumerate((mixed, dq, dk, dv))
+    ]
+    for copy in copies:
+        copy.start()
     grads = jnp.concatenate([logit_grad[c * 4 + x] for x in range(4) for c in range(2)], 0)
     dhidden[...] = dot(grads, gate[...], 0, 1).astype(BF)
+    for copy in copies:
+        copy.wait()
+
+
+def second_body(got, old_mixed, old_dq, old_dk, old_dv, mixed, dq, dk, dv, sems):
+    theirs = pl.multiple_of((1 - lax.axis_index("core")) * LANES, LANES)
+    copies = [
+        pltpu.make_async_copy(got.at[i], dst.at[:, pl.ds(theirs, LANES)], sems.at[i])
+        for i, dst in enumerate((mixed, dq, dk, dv))
+    ]
+    for copy in copies:
+        copy.start()
+    for copy in copies:
+        copy.wait()
 
 
 def local(queries, keys, values, hidden, gate_weight, level_slot, out_grad):
@@ -310,7 +337,15 @@
     )(*far(queries, keys, values, out_grad, hidden, gate_weight))
     other = lax.ppermute(send, "core", swap)
     parts = exchange(partial, ("core", "head"))
-    up, pair, cols, chosen, near_state, near_grad = pl.pallas_call(
+    state, near_state = pl.pallas_call(
+        pre_body,
+        out_shape=(shape(HALF, DK, DK), shape(HALF, DK, DK)),
+        in_specs=vmem(2),
+        out_specs=tuple(vmem(2)),
+        compiler_params=SMALL,
+        name="pre",
+    )(*near(own, other))
+    up, pair, cols, logits, near_grad = pl.pallas_call(
         states_body,
         out_shape=(
             shape(8, SPREAD, 64, DK),
@@ -318,14 +353,13 @@
             shape(2, SPAN, 128, kind=F32),
             shape(8 * HALF, 2 * SPAN, kind=F32),
             shape(HALF, DK, DK),
-            shape(HALF, DK, DK),
         ),
-        in_specs=smem(1) + vmem(3),
-        out_specs=tuple(vmem(6)),
+        in_specs=smem(1) + vmem(4),
+        out_specs=tuple(vmem(5)),
         scratch_shapes=[pltpu.VMEM((8 * HALF, 2 * SPAN), F32)],
         compiler_params=SMALL,
         name="states",
-    )(meta, *near(parts, own, other))
+    )(meta, *near(parts, own, other, state))
     pair_got = flip(pair, 1)
     got = exchange(up, "z")
     to_y, halves = pl.pallas_call(
@@ -348,7 +382,11 @@
     from_y = exchange(to_y, "y")
     part_own, part_other, sums = pl.pallas_call(
         local_body,
-        out_shape=(shape(4, SPAN, LANES), shape(4, SPAN, LANES), shape(2, SPAN, 128, kind=F32)),
+        out_shape=(
+            shape(4, SPAN, LANES),
+            shape(4, SPAN, LANES),
+            shape(8 * HALF, 2 * SPAN, kind=F32),
+        ),
         in_specs=smem(1) + vmem(5),
         out_specs=tuple(vmem(3)),
         compiler_params=SMALL,
@@ -368,11 +406,10 @@
         out_shape=(shape(4, SPAN, LANES), shape(4, SPAN, LANES), shape(8, 8 * HALF, SPAN)),
         in_specs=smem(1) + vmem(9),
         out_specs=tuple(vmem(3)),
-        scratch_shapes=[pltpu.VMEM((8 * HALF, SPAN), F32)],
         input_output_aliases={5: 0, 6: 1},
         compiler_params=SMALL,
         name="outputs",
-    )(meta, *near(own, other, cols, chosen, part_own, part_other, sums, direct, sums_here))
+    )(meta, *near(own, other, cols, logits, part_own, part_other, sums, direct, sums_here))
     all_grads = exchange(logit_grad, ("core", "head"))
     keep, away = pl.pallas_call(
         grads_body,
@@ -384,15 +421,27 @@
         name="grads",
     )(meta, *near(own, other, cols, part_own, part_other, direct, sums_here))
     back = lax.ppermute(away, "core", swap)
-    outs = (jax.ShapeDtypeStruct((SPAN, 2 * LANES), BF),) * 4
-    return pl.pallas_call(
-        unpack_body,
-        out_shape=outs + (jax.ShapeDtypeStruct((SPAN, hidden.shape[1]), BF),),
-        in_specs=smem(1) + vmem(4),
-        out_specs=tuple(vmem(5)),
-        compiler_params=SMALL,
-        name="unpack",
-    )(meta, *near(keep, back, all_grads), gate_weight)
+    wide = pltpu.HBM((SPAN, 2 * LANES), BF)
+    *outs, dhidden = pl.pallas_call(
+        first_body,
+        out_shape=(wide,) * 4 + (jax.ShapeDtypeStruct((SPAN, hidden.shape[1]), BF),),
+        in_specs=vmem(3),
+        out_specs=tuple(hbm(4) + vmem(1)),
+        scratch_shapes=[pltpu.SemaphoreType.DMA((4,))],
+        compiler_params=SMALL,
+        name="first",
+    )(*near(keep, all_grads), gate_weight)
+    outs = pl.pallas_call(
+        second_body,
+        out_shape=(wide,) * 4,
+        in_specs=vmem(1) + hbm(4),
+        out_specs=tuple(hbm(4)),
+        input_output_aliases={1: 0, 2: 1, 3: 2, 4: 3},
+        scratch_shapes=[pltpu.SemaphoreType.DMA((4,))],
+        compiler_params=SMALL,
+        name="second",
+    )(*near(back), *far(*outs))
+    return (*outs, dhidden)
 
 
 def solution(mesh):

time: 102 us -> 101 us (level)
    pallas_call x1, Pallas kernels: 3.32 us -> 1.6 us  [local(): pl.pallas_call(outputs_body, out_shape=(shape(4, SPAN, LANES), shape(4, S...]
    pallas_call x1 -> x3, Pallas kernels: 1.66 us -> 2.61 us  [the longest x1 1.52 us: local(): pl.pallas_call(first_body, out_shape=(wide,) * 4 + (jax.ShapeDtypeStruct(...]
  transfers between devices with their start and end apart: 8 -> 8, of which waited for: 5 -> 5; matrix products, arithmetic and copies ran while one was open for 0% -> 0% of each run, Pallas kernels for 4% -> 6%
where the time goes in v5:
time: 101 us
  starting transfers between devices  39.1 us (39%)
  waiting for transfers between devices  36.2 us (36%)
  Pallas kernels  16.6 us (16%)
  blocking collectives  7.42 us (7%)
    all_to_all x4, waiting for transfers between devices, exchange(): return lax.all_to_all(array, axis, 0, 0, tiled=True)  30.5 us
    all_to_all x4, starting transfers between devices, exchange(): return lax.all_to_all(array, axis, 0, 0, tiled=True)  19.4 us
    ppermute x1, starting transfers between devices, local(): other = lax.ppermute(send, 'core', swap)  8.75 us
    all_to_all x1, blocking collectives, exchange(): return lax.all_to_all(array, axis, 0, 0, tiled=True)  7.42 us
    ppermute x2, waiting for transfers between devices, flip(): return lax.ppermute(array, 'z', [(i, i ^ distance) for i in range(8)])  5.64 us
    ppermute x1, starting transfers between devices, local(): back = lax.ppermute(away, 'core', swap)  5.61 us
    ppermute x2, starting transfers between devices, flip(): return lax.ppermute(array, 'z', [(i, i ^ distance) for i in range(8)])  5.28 us
    pallas_call x1, Pallas kernels, local(): pl.pallas_call(states_body, out_shape=(shape(8, SPREAD, 64, DK), shape(DI...  2.86 us
  transfers between devices with their start and end apart: 8, of which 5 were waited for; matrix products, arithmetic and copies ran while one was open for 0% of the time, Pallas kernels for 6%

profile of v5, /device:TPU:1, one launch (start us, length us, event | category | flops | bytes accessed | tf_op | source)
XLA Modules:
  0.0 100.8 jit_solution(3912122846077781797)
XLA Ops:
  0.6 2.2 %pack.1 = (bf16[4,128,512]{2,1,0:T(8,128)(2,1)S(1)}, bf16[4,128,512]{2,1,0:T(8,128)(2,1)S(1)}, f32[8,32,128]{2,1,0:T(8,128)}) custom-call(bf16[128,1024]{1,0:T(8,128)(2,1)} %q.1, bf16[128,1024]{1,0:T(8,128)(2,1)} %k.1, bf16[128,1024]{1,0:T(8,128)(2,1)} %v.1, bf16[128,1024]{1,0:T(8,128)(2,1)} %g.1, bf16[128,512]{1,0:T(8,128)(2,1)} %hidden.1, ...), custom_call_target="tpu_custom_call" | custom-call | tf_op jit(solution)/shard_map/pack/pallas_call | solution.py:324
  2.8 8.7 %collective-permute-start = (bf16[4,128,512]{2,1,0:T(8,128)(2,1)S(1)}, bf16[4,128,512]{2,1,0:T(8,128)(2,1)S(1)}, u32[]{:S(2)}, u32[]{:S(2)}) collective-permute-start(bf16[4,128,512]{2,1,0:T(8,128)(2,1)S(1)} %get-tuple-element.37), channel_id=1, source_target_pairs={{0,4},{4,0},{1,5},{5,1},{2,6},{6,2},{3,7},{7,3},{8,12},{12,8},{9,1... | collective-permute-start | bytes 1572872 | tf_op jit(solution)/shard_map/ppermute | solution.py:338
  11.5 3.3 %all-to-all-start = ((f32[8,32,128]{2,1,0:T(8,128)}), f32[8,32,128]{2,1,0:T(8,128)S(1)}, u32[]{:S(2)}, u32[]{:S(2)}) async-start(f32[8,32,128]{2,1,0:T(8,128)} %get-tuple-element.38), calls=%async_computation | async-start | bytes 262144 | tf_op jit(solution)/shard_map/all_to_all | solution.py:319
  14.9 0.0 copy-start.1
  14.9 0.6 copy-done.1
  15.6 0.1 pad_add_fusion.meta
  15.6 0.0 collective-permute-done.other
  15.6 0.3 pre.1
  15.9 4.2 %all-to-all-done.parts = f32[8,32,128]{2,1,0:T(8,128)S(1)} async-done(((f32[8,32,128]{2,1,0:T(8,128)}), f32[8,32,128]{2,1,0:T(8,128)S(1)}, u32[]{:S(2)}, u32[]{:S(2)}) %all-to-all-start) | async-done | bytes 131104 | tf_op jit(solution)/shard_map/all_to_all | solution.py:319
  20.1 2.9 %states.1 = (bf16[8,4,64,128]{3,2,1,0:T(8,128)(2,1)}, bf16[2,4,128,128]{3,2,1,0:T(8,128)(2,1)S(1)}, f32[2,128,128]{2,1,0:T(8,128)S(1)}, f32[32,256]{1,0:T(8,128)S(1)}, bf16[4,128,128]{2,1,0:T(8,128)(2,1)S(1)}) custom-call(s32[11]{0:T(128)S(1)} %pad_add_fusion.meta, f32[8,32,128]{2,1,0:T(8,128)S(1)} %all-to-all-done.parts, ...), custom_call_target="tpu_custom_call" | custom-call | tf_op jit(solution)/shard_map/states/pallas_call | solution.py:348
  22.9 5.8 %all-to-all-start.1 = ((bf16[8,4,64,128]{3,2,1,0:T(8,128)(2,1)}), bf16[8,4,64,128]{3,2,1,0:T(8,128)(2,1)S(1)}, u32[]{:S(2)}, u32[]{:S(2)}) async-start(bf16[8,4,64,128]{3,2,1,0:T(8,128)(2,1)} %get-tuple-element.47), calls=%async_computation.1 | async-start | bytes 1048576 | tf_op jit(solution)/shard_map/all_to_all | solution.py:319
  28.7 3.4 %collective-permute-start.1 = (bf16[2,4,128,128]{3,2,1,0:T(8,128)(2,1)S(1)}, bf16[2,4,128,128]{3,2,1,0:T(8,128)(2,1)S(1)}, u32[]{:S(2)}, u32[]{:S(2)}) collective-permute-start(bf16[2,4,128,128]{3,2,1,0:T(8,128)(2,1)S(1)} %get-tuple-element.50.pair), channel_id=1, source_target_pairs={{0,8},{8,0},{16,24},{24,16},{32,40},{40,32},{48,56},{56,48},{1,9},... | collective-permute-start | bytes 786440 | tf_op jit(solution)/shard_map/ppermute | solution.py:322
  32.1 14.4 %all-to-all-done.1.got = bf16[8,4,64,128]{3,2,1,0:T(8,128)(2,1)S(1)} async-done(((bf16[8,4,64,128]{3,2,1,0:T(8,128)(2,1)}), bf16[8,4,64,128]{3,2,1,0:T(8,128)(2,1)S(1)}, u32[]{:S(2)}, u32[]{:S(2)}) %all-to-all-start.1) | async-done | bytes 524320 | tf_op jit(solution)/shard_map/all_to_all | solution.py:319
  46.5 1.3 %along_z.1 = (bf16[8,64,128]{2,1,0:T(8,128)(2,1)}, bf16[2,64,128]{2,1,0:T(8,128)(2,1)S(1)}) custom-call(s32[11]{0:T(128)S(1)} %pad_add_fusion.meta, bf16[8,4,64,128]{3,2,1,0:T(8,128)(2,1)S(1)} %all-to-all-done.1.got), custom_call_target="tpu_custom_call" | custom-call | tf_op jit(solution)/shard_map/along_z/pallas_call | solution.py:365
  47.7 6.8 %all-to-all-start.2 = ((bf16[8,64,128]{2,1,0:T(8,128)(2,1)}), bf16[8,64,128]{2,1,0:T(8,128)(2,1)S(1)}, u32[]{:S(2)}, u32[]{:S(2)}) async-start(bf16[8,64,128]{2,1,0:T(8,128)(2,1)} %get-tuple-element.49), calls=%async_computation.2 | async-start | bytes 262144 | tf_op jit(solution)/shard_map/all_to_all | solution.py:319
  54.5 0.0 collective-permute-done.1.pair_got
  54.6 1.9 %collective-permute-start.2 = (bf16[4,128,128]{2,1,0:T(8,128)(2,1)S(1)}, bf16[4,128,128]{2,1,0:T(8,128)(2,1)S(1)}, u32[]{:S(2)}, u32[]{:S(2)}) collective-permute-start(bf16[4,128,128]{2,1,0:T(8,128)(2,1)S(1)} %pair.1), channel_id=1, source_target_pairs={{0,16},{8,24},{16,0},{24,8},{32,48},{40,56},{48,32},{56,40},{1,17}... | collective-permute-start | bytes 393224 | tf_op jit(solution)/shard_map/ppermute | solution.py:322
  56.5 5.6 %collective-permute-done.2.quad_got = bf16[4,128,128]{2,1,0:T(8,128)(2,1)S(1)} collective-permute-done((bf16[4,128,128]{2,1,0:T(8,128)(2,1)S(1)}, bf16[4,128,128]{2,1,0:T(8,128)(2,1)S(1)}, u32[]{:S(2)}, u32[]{:S(2)}) %collective-permute-start.2) | collective-permute-done | bytes 131104 | tf_op jit(solution)/shard_map/ppermute | solution.py:322
  62.1 0.1 all-to-all-done.2.from_y
  62.3 1.4 %buckets.1 = (bf16[8,4,64,128]{3,2,1,0:T(8,128)(2,1)}, bf16[2,4,128,128]{3,2,1,0:T(8,128)(2,1)S(1)}) custom-call(s32[11]{0:T(128)S(1)} %pad_add_fusion.meta, bf16[2,64,128]{2,1,0:T(8,128)(2,1)S(1)} %get-tuple-element.48.halves, bf16[8,64,128]{2,1,0:T(8,128)(2,1)S(1)} %all-to-all-done.2.from_y, bf16[2,4,128,128]{3,2,1,0:T(8,128)(2,1)S(1)} %collective-permute-done.1.pair_got, ...), custom_call_target="tpu_custom_call" | custom-call | tf_op jit(solution)/shard_map/buckets/pallas_call | solution.py:395
  63.7 3.5 %all-to-all-start.3 = ((bf16[8,4,64,128]{3,2,1,0:T(8,128)(2,1)}), bf16[8,4,64,128]{3,2,1,0:T(8,128)(2,1)S(1)}, u32[]{:S(2)}, u32[]{:S(2)}) async-start(bf16[8,4,64,128]{3,2,1,0:T(8,128)(2,1)} %get-tuple-element.52), calls=%async_computation.3 | async-start | bytes 1048576 | tf_op jit(solution)/shard_map/all_to_all | solution.py:319
  67.2 2.8 %local.1 = (bf16[4,128,512]{2,1,0:T(8,128)(2,1)S(1)}, bf16[4,128,512]{2,1,0:T(8,128)(2,1)S(1)}, f32[32,256]{1,0:T(8,128)S(1)}) custom-call(s32[11]{0:T(128)S(1)} %pad_add_fusion.meta, bf16[4,128,512]{2,1,0:T(8,128)(2,1)S(1)} %get-tuple-element.36.own, bf16[4,128,512]{2,1,0:T(8,128)(2,1)S(1)} %collective-permute-done.other, ...), custom_call_target="tpu_custom_call" | custom-call | tf_op jit(solution)/shard_map/local/pallas_call | solution.py:383
  70.0 11.9 %all-to-all-done.3.got = bf16[8,4,64,128]{3,2,1,0:T(8,128)(2,1)S(1)} async-done(((bf16[8,4,64,128]{3,2,1,0:T(8,128)(2,1)}), bf16[8,4,64,128]{3,2,1,0:T(8,128)(2,1)S(1)}, u32[]{:S(2)}, u32[]{:S(2)}) %all-to-all-start.3) | async-done | bytes 524320 | tf_op jit(solution)/shard_map/all_to_all | solution.py:319
  81.9 1.6 %outputs.1 = (bf16[4,128,512]{2,1,0:T(8,128)(2,1)S(1)}, bf16[4,128,512]{2,1,0:T(8,128)(2,1)S(1)}, bf16[8,32,128]{2,1,0:T(8,128)(2,1)S(1)}) custom-call(s32[11]{0:T(128)S(1)} %pad_add_fusion.meta, bf16[4,128,512]{2,1,0:T(8,128)(2,1)S(1)} %get-tuple-element.36.own, ...), custom_call_target="tpu_custom_call", output_to_operand_aliasing={{0}: (5, {}), {1}: (6, {})} | custom-call | tf_op jit(solution)/shard_map/outputs/pallas_call | solution.py:404
  83.5 0.0 copy-start
  83.5 1.9 %grads.1 = (bf16[4,128,512]{2,1,0:T(8,128)(2,1)S(1)}, bf16[4,128,512]{2,1,0:T(8,128)(2,1)S(1)}) custom-call(s32[11]{0:T(128)S(1)} %pad_add_fusion.meta, bf16[4,128,512]{2,1,0:T(8,128)(2,1)S(1)} %get-tuple-element.36.own, bf16[4,128,512]{2,1,0:T(8,128)(2,1)S(1)} %collective-permute-done.other, ...), custom_call_target="tpu_custom_call", output_to_operand_aliasing={{0}: (4, {}), {1}: (5, {})} | custom-call | tf_op jit(solution)/shard_map/grads/pallas_call | solution.py:414
  85.4 5.6 %collective-permute-start.3 = (bf16[4,128,512]{2,1,0:T(8,128)(2,1)S(1)}, bf16[4,128,512]{2,1,0:T(8,128)(2,1)S(1)}, u32[]{:S(2)}, u32[]{:S(2)}) collective-permute-start(bf16[4,128,512]{2,1,0:T(8,128)(2,1)S(1)} %get-tuple-element.55), channel_id=1, source_target_pairs={{0,4},{4,0},{1,5},{5,1},{2,6},{6,2},{3,7},{7,3},{8,12},{12,8},{9,1... | collective-permute-start | bytes 1572872 | tf_op jit(solution)/shard_map/ppermute | solution.py:423
  91.0 7.4 %all_to_all.25.logit_grad = bf16[8,32,128]{2,1,0:T(8,128)(2,1)S(1)} all-to-all(bf16[8,32,128]{2,1,0:T(8,128)(2,1)S(1)} %get-tuple-element.57), channel_id=1, replica_groups=mesh['y'=8,'z'=8,'core'=2,'head'=4] {'core','head'}, dimensions={0} | all-to-all | bytes 131072 | tf_op jit(solution)/shard_map/all_to_all | solution.py:319
  98.4 0.0 copy-done
  98.4 1.5 %first.1 = (bf16[128,1024]{1,0:T(8,128)(2,1)}, bf16[128,1024]{1,0:T(8,128)(2,1)}, bf16[128,1024]{1,0:T(8,128)(2,1)}, bf16[128,1024]{1,0:T(8,128)(2,1)}, bf16[128,512]{1,0:T(8,128)(2,1)}) custom-call(bf16[4,128,512]{2,1,0:T(8,128)(2,1)S(1)} %get-tuple-element.56.keep, bf16[8,32,128]{2,1,0:T(8,128)(2,1)S(1)} %all_to_all.25.logit_grad, bf16[512,256]{1,0:T(8,128)(2,1)S(1)} %copy-done), custom_call_target="tpu_custom_call" | custom-call | tf_op jit(solution)/shard_map/first/pallas_call | solution.py:425
  100.0 0.0 collective-permute-done.3.got
  100.0 0.8 second.1
  (1 shorter events, 0.0 us)
Async XLA Ops:
  2.8 12.8 %collective-permute-start = (bf16[4,128,512]{2,1,0:T(8,128)(2,1)S(1)}, bf16[4,128,512]{2,1,0:T(8,128)(2,1)S(1)}, u32[]{:S(2)}, u32[]{:S(2)}) collective-permute-start(bf16[4,128,512]{2,1,0:T(8,128)(2,1)S(1)} %get-tuple-element.37), channel_id=1, source_target_pairs={{0,4},{4,0},{1,5},{5,1},{2,6},{6,2},{3,7},{7,3},{8,12},{12,8},{9,1... | collective-permute-start | bytes 1572872 | tf_op jit(solution)/shard_map/ppermute | solution.py:338
  11.5 8.5 %all-to-all-start = ((f32[8,32,128]{2,1,0:T(8,128)}), f32[8,32,128]{2,1,0:T(8,128)S(1)}, u32[]{:S(2)}, u32[]{:S(2)}) async-start(f32[8,32,128]{2,1,0:T(8,128)} %get-tuple-element.38), calls=%async_computation | async-start | bytes 262144 | tf_op jit(solution)/shard_map/all_to_all | solution.py:319
  14.9 0.7 copy-start.1
  22.9 23.5 %all-to-all-start.1 = ((bf16[8,4,64,128]{3,2,1,0:T(8,128)(2,1)}), bf16[8,4,64,128]{3,2,1,0:T(8,128)(2,1)S(1)}, u32[]{:S(2)}, u32[]{:S(2)}) async-start(bf16[8,4,64,128]{3,2,1,0:T(8,128)(2,1)} %get-tuple-element.47), calls=%async_computation.1 | async-start | bytes 1048576 | tf_op jit(solution)/shard_map/all_to_all | solution.py:319
  28.7 25.8 %collective-permute-start.1 = (bf16[2,4,128,128]{3,2,1,0:T(8,128)(2,1)S(1)}, bf16[2,4,128,128]{3,2,1,0:T(8,128)(2,1)S(1)}, u32[]{:S(2)}, u32[]{:S(2)}) collective-permute-start(bf16[2,4,128,128]{3,2,1,0:T(8,128)(2,1)S(1)} %get-tuple-element.50.pair), channel_id=1, source_target_pairs={{0,8},{8,0},{16,24},{24,16},{32,40},{40,32},{48,56},{56,48},{1,9},... | collective-permute-start | bytes 786440 | tf_op jit(solution)/shard_map/ppermute | solution.py:322
  47.7 14.6 %all-to-all-start.2 = ((bf16[8,64,128]{2,1,0:T(8,128)(2,1)}), bf16[8,64,128]{2,1,0:T(8,128)(2,1)S(1)}, u32[]{:S(2)}, u32[]{:S(2)}) async-start(bf16[8,64,128]{2,1,0:T(8,128)(2,1)} %get-tuple-element.49), calls=%async_computation.2 | async-start | bytes 262144 | tf_op jit(solution)/shard_map/all_to_all | solution.py:319
  54.6 7.6 %collective-permute-start.2 = (bf16[4,128,128]{2,1,0:T(8,128)(2,1)S(1)}, bf16[4,128,128]{2,1,0:T(8,128)(2,1)S(1)}, u32[]{:S(2)}, u32[]{:S(2)}) collective-permute-start(bf16[4,128,128]{2,1,0:T(8,128)(2,1)S(1)} %pair.1), channel_id=1, source_target_pairs={{0,16},{8,24},{16,0},{24,8},{32,48},{40,56},{48,32},{56,40},{1,17}... | collective-permute-start | bytes 393224 | tf_op jit(solution)/shard_map/ppermute | solution.py:322
  63.7 18.2 %all-to-all-start.3 = ((bf16[8,4,64,128]{3,2,1,0:T(8,128)(2,1)}), bf16[8,4,64,128]{3,2,1,0:T(8,128)(2,1)S(1)}, u32[]{:S(2)}, u32[]{:S(2)}) async-start(bf16[8,4,64,128]{3,2,1,0:T(8,128)(2,1)} %get-tuple-element.52), calls=%async_computation.3 | async-start | bytes 1048576 | tf_op jit(solution)/shard_map/all_to_all | solution.py:319
  83.5 15.0 %copy-start = (bf16[512,256]{1,0:T(8,128)(2,1)S(1)}, bf16[512,256]{1,0:T(8,128)(2,1)}, u32[]{:S(2)}) copy-start(bf16[512,256]{1,0:T(8,128)(2,1)} %gate.3) | copy-start | bytes 786436
  85.4 14.6 %collective-permute-start.3 = (bf16[4,128,512]{2,1,0:T(8,128)(2,1)S(1)}, bf16[4,128,512]{2,1,0:T(8,128)(2,1)S(1)}, u32[]{:S(2)}, u32[]{:S(2)}) collective-permute-start(bf16[4,128,512]{2,1,0:T(8,128)(2,1)S(1)} %get-tuple-element.55), channel_id=1, source_target_pairs={{0,4},{4,0},{1,5},{5,1},{2,6},{6,2},{3,7},{7,3},{8,12},{12,8},{9,1... | collective-permute-start | bytes 1572872 | tf_op jit(solution)/shard_map/ppermute | solution.py:423

commit v6 on v5

--- a/solution.py
+++ b/solution.py
@@ -48,32 +48,33 @@
 SMALL = pltpu.CompilerParams(vmem_limit_bytes=16 << 20)
 
 
-def pack_body(q, k, v, g, hidden, gate, send, own, partial, held, held_hidden, held_gate, sems):
-    copies = [
-        pltpu.make_async_copy(hidden, held_hidden, sems.at[0]),
-        pltpu.make_async_copy(gate.at[:256], held_gate.at[:256], sems.at[1]),
-        pltpu.make_async_copy(gate.at[256:], held_gate.at[256:], sems.at[2]),
-    ]
-    for i, src in enumerate((q, k, v, g)):
-        for part in range(2):
-            rows = slice(part * 64, part * 64 + 64)
-            copies.append(
-                pltpu.make_async_copy(src.at[rows], held.at[i, rows], sems.at[3 + 2 * i + part])
-            )
+def logits_body(hidden, gate, g, partial, held_g, held_hidden, held_gate, sems):
+    copies = []
+    for part in range(4):
+        rows = slice(part * 128, part * 128 + 128)
+        copies.append(pltpu.make_async_copy(gate.at[rows], held_gate.at[rows], sems.at[part]))
+    for part in range(2):
+        rows = slice(part * 64, part * 64 + 64)
+        copies.append(
+            pltpu.make_async_copy(hidden.at[rows], held_hidden.at[rows], sems.at[4 + part])
+        )
+    copies.append(pltpu.make_async_copy(g, held_g, sems.at[6]))
     for copy in copies:
         copy.start()
-    for copy in copies[:3]:
+    for copy in copies[:6]:
         copy.wait()
-    logits = dot(held_gate[...], held_hidden[...], 0, 1)
+    logits = jnp.transpose(dot(held_hidden[...], held_gate[...], 1, 0))
     for c in range(2):
         for x in range(4):
             row = x * 64 + c * 32
             partial[c * 4 + x] = logits[row : row + 32]
+    copies[6].wait()
+
+
+def pack_body(q, k, v, g, send, own):
     first = lax.axis_index("core") == 0
-    for i in range(4):
-        copies[3 + 2 * i].wait()
-        copies[4 + 2 * i].wait()
-        low, high = held[i, :, :LANES], held[i, :, LANES:]
+    for i, src in enumerate((q, k, v, g)):
+        low, high = src[:, :LANES], src[:, LANES:]
         own[i] = jnp.where(first, low, high)
         send[i] = jnp.where(first, high, low)
 
@@ -321,22 +322,29 @@
     def flip(array, distance):
         return lax.ppermute(array, "z", [(i, i ^ distance) for i in range(8)])
 
-    send, own, partial = pl.pallas_call(
-        pack_body,
-        out_shape=(shape(4, SPAN, LANES), shape(4, SPAN, LANES), shape(8, 32, SPAN, kind=F32)),
-        in_specs=hbm(6),
-        out_specs=tuple(vmem(3)),
+    partial, held_g = pl.pallas_call(
+        logits_body,
+        out_shape=(shape(8, 32, SPAN, kind=F32), shape(SPAN, 2 * LANES)),
+        in_specs=hbm(3),
+        out_specs=tuple(vmem(2)),
         scratch_shapes=[
-            pltpu.VMEM((4, SPAN, 2 * LANES), BF),
             pltpu.VMEM(hidden.shape, BF),
             pltpu.VMEM(gate_weight.shape, BF),
-            pltpu.SemaphoreType.DMA((11,)),
+            pltpu.SemaphoreType.DMA((7,)),
         ],
         compiler_params=SMALL,
+        name="logits",
+    )(*far(hidden, gate_weight, out_grad))
+    parts = exchange(partial, ("core", "head"))
+    send, own = pl.pallas_call(
+        pack_body,
+        out_shape=(shape(4, SPAN, LANES), shape(4, SPAN, LANES)),
+        in_specs=vmem(4),
+        out_specs=tuple(vmem(2)),
+        compiler_params=SMALL,
         name="pack",
-    )(*far(queries, keys, values, out_grad, hidden, gate_weight))
+    )(*near(queries, keys, values, held_g))
     other = lax.ppermute(send, "core", swap)
-    parts = exchange(partial, ("core", "head"))
     state, near_state = pl.pallas_call(
         pre_body,
         out_shape=(shape(HALF, DK, DK), shape(HALF, DK, DK)),

time: 101 us -> 102 us (level)
    pallas_call x1, Pallas kernels: 2.15 us -> 0.09 us  [local(): pl.pallas_call(pack_body, out_shape=(shape(4, SPAN, LANES), shape(4, SPAN...]
    pallas_call x0 -> x1, Pallas kernels: none -> 2.03 us  [local(): pl.pallas_call(logits_body, out_shape=(shape(8, 32, SPAN, kind=F32), shap...]
where the time goes in v6:
time: 102 us
  starting transfers between devices  39.1 us (38%)
  waiting for transfers between devices  36.2 us (35%)
  Pallas kernels  16.6 us (16%)
  blocking collectives  7.42 us (7%)
  local copies, waits for them, and re-layouts  1.61 us (2%)
    all_to_all x4, waiting for transfers between devices, exchange(): return lax.all_to_all(array, axis, 0, 0, tiled=True)  30.5 us
    all_to_all x4, starting transfers between devices, exchange(): return lax.all_to_all(array, axis, 0, 0, tiled=True)  19.4 us
    ppermute x1, starting transfers between devices, local(): other = lax.ppermute(send, 'core', swap)  8.75 us
    all_to_all x1, blocking collectives, exchange(): return lax.all_to_all(array, axis, 0, 0, tiled=True)  7.42 us
    ppermute x2, waiting for transfers between devices, flip(): return lax.ppermute(array, 'z', [(i, i ^ distance) for i in range(8)])  5.64 us
    ppermute x1, starting transfers between devices, local(): back = lax.ppermute(away, 'core', swap)  5.61 us
    ppermute x2, starting transfers between devices, flip(): return lax.ppermute(array, 'z', [(i, i ^ distance) for i in range(8)])  5.28 us
    pallas_call x1, Pallas kernels, local(): pl.pallas_call(states_body, out_shape=(shape(8, SPREAD, 64, DK), shape(DI...  2.87 us
  transfers between devices with their start and end apart: 8, of which 5 were waited for; matrix products, arithmetic and copies ran while one was open for 0% of the time, Pallas kernels for 6%

profile of v6, /device:TPU:1, one launch (start us, length us, event | category | flops | bytes accessed | tf_op | source)
XLA Modules:
  0.0 101.8 jit_solution(6584699160939895348)
XLA Ops:
  0.6 0.0 copy-start.2
  0.6 0.0 copy-start.1
  0.7 2.0 %logits.1 = (f32[8,32,128]{2,1,0:T(8,128)}, bf16[128,1024]{1,0:T(8,128)(2,1)S(1)}) custom-call(bf16[128,512]{1,0:T(8,128)(2,1)} %hidden.1, bf16[512,256]{1,0:T(8,128)(2,1)} %gate.3, bf16[128,1024]{1,0:T(8,128)(2,1)} %g.1), custom_call_target="tpu_custom_call" | custom-call | tf_op jit(solution)/shard_map/logits/pallas_call | solution.py:325
  2.7 0.0 copy-done.2
  2.7 0.0 copy-done.1
  2.7 0.0 copy-start.3
  2.7 0.9 copy-done.3
  3.7 0.1 pack.1
  3.8 8.7 %collective-permute-start = (bf16[4,128,512]{2,1,0:T(8,128)(2,1)S(1)}, bf16[4,128,512]{2,1,0:T(8,128)(2,1)S(1)}, u32[]{:S(2)}, u32[]{:S(2)}) collective-permute-start(bf16[4,128,512]{2,1,0:T(8,128)(2,1)S(1)} %get-tuple-element.39), channel_id=1, source_target_pairs={{0,4},{4,0},{1,5},{5,1},{2,6},{6,2},{3,7},{7,3},{8,12},{12,8},{9,1... | collective-permute-start | bytes 1572872 | tf_op jit(solution)/shard_map/ppermute | solution.py:347
  12.5 3.3 %all-to-all-start = ((f32[8,32,128]{2,1,0:T(8,128)}), f32[8,32,128]{2,1,0:T(8,128)S(1)}, u32[]{:S(2)}, u32[]{:S(2)}) async-start(f32[8,32,128]{2,1,0:T(8,128)} %get-tuple-element.40), calls=%async_computation | async-start | bytes 262144 | tf_op jit(solution)/shard_map/all_to_all | solution.py:320
  15.9 0.0 copy-start.4
  15.9 0.6 copy-done.4
  16.5 0.1 pad_add_fusion.meta
  16.6 0.0 collective-permute-done.other
  16.6 0.3 pre.1
  16.9 4.2 %all-to-all-done.parts = f32[8,32,128]{2,1,0:T(8,128)S(1)} async-done(((f32[8,32,128]{2,1,0:T(8,128)}), f32[8,32,128]{2,1,0:T(8,128)S(1)}, u32[]{:S(2)}, u32[]{:S(2)}) %all-to-all-start) | async-done | bytes 131104 | tf_op jit(solution)/shard_map/all_to_all | solution.py:320
  21.0 2.9 %states.1 = (bf16[8,4,64,128]{3,2,1,0:T(8,128)(2,1)}, bf16[2,4,128,128]{3,2,1,0:T(8,128)(2,1)S(1)}, f32[2,128,128]{2,1,0:T(8,128)S(1)}, f32[32,256]{1,0:T(8,128)S(1)}, bf16[4,128,128]{2,1,0:T(8,128)(2,1)S(1)}) custom-call(s32[11]{0:T(128)S(1)} %pad_add_fusion.meta, f32[8,32,128]{2,1,0:T(8,128)S(1)} %all-to-all-done.parts, ...), custom_call_target="tpu_custom_call" | custom-call | tf_op jit(solution)/shard_map/states/pallas_call | solution.py:356
  23.9 5.8 %all-to-all-start.1 = ((bf16[8,4,64,128]{3,2,1,0:T(8,128)(2,1)}), bf16[8,4,64,128]{3,2,1,0:T(8,128)(2,1)S(1)}, u32[]{:S(2)}, u32[]{:S(2)}) async-start(bf16[8,4,64,128]{3,2,1,0:T(8,128)(2,1)} %get-tuple-element.49), calls=%async_computation.1 | async-start | bytes 1048576 | tf_op jit(solution)/shard_map/all_to_all | solution.py:320
  29.7 3.4 %collective-permute-start.1 = (bf16[2,4,128,128]{3,2,1,0:T(8,128)(2,1)S(1)}, bf16[2,4,128,128]{3,2,1,0:T(8,128)(2,1)S(1)}, u32[]{:S(2)}, u32[]{:S(2)}) collective-permute-start(bf16[2,4,128,128]{3,2,1,0:T(8,128)(2,1)S(1)} %get-tuple-element.52.pair), channel_id=1, source_target_pairs={{0,8},{8,0},{16,24},{24,16},{32,40},{40,32},{48,56},{56,48},{1,9},... | collective-permute-start | bytes 786440 | tf_op jit(solution)/shard_map/ppermute | solution.py:323
  33.0 14.4 %all-to-all-done.1.got = bf16[8,4,64,128]{3,2,1,0:T(8,128)(2,1)S(1)} async-done(((bf16[8,4,64,128]{3,2,1,0:T(8,128)(2,1)}), bf16[8,4,64,128]{3,2,1,0:T(8,128)(2,1)S(1)}, u32[]{:S(2)}, u32[]{:S(2)}) %all-to-all-start.1) | async-done | bytes 524320 | tf_op jit(solution)/shard_map/all_to_all | solution.py:320
  47.4 1.3 %along_z.1 = (bf16[8,64,128]{2,1,0:T(8,128)(2,1)}, bf16[2,64,128]{2,1,0:T(8,128)(2,1)S(1)}) custom-call(s32[11]{0:T(128)S(1)} %pad_add_fusion.meta, bf16[8,4,64,128]{3,2,1,0:T(8,128)(2,1)S(1)} %all-to-all-done.1.got), custom_call_target="tpu_custom_call" | custom-call | tf_op jit(solution)/shard_map/along_z/pallas_call | solution.py:373
  48.7 6.8 %all-to-all-start.2 = ((bf16[8,64,128]{2,1,0:T(8,128)(2,1)}), bf16[8,64,128]{2,1,0:T(8,128)(2,1)S(1)}, u32[]{:S(2)}, u32[]{:S(2)}) async-start(bf16[8,64,128]{2,1,0:T(8,128)(2,1)} %get-tuple-element.51), calls=%async_computation.2 | async-start | bytes 262144 | tf_op jit(solution)/shard_map/all_to_all | solution.py:320
  55.5 0.0 collective-permute-done.1.pair_got
  55.5 1.9 %collective-permute-start.2 = (bf16[4,128,128]{2,1,0:T(8,128)(2,1)S(1)}, bf16[4,128,128]{2,1,0:T(8,128)(2,1)S(1)}, u32[]{:S(2)}, u32[]{:S(2)}) collective-permute-start(bf16[4,128,128]{2,1,0:T(8,128)(2,1)S(1)} %pair.1), channel_id=1, source_target_pairs={{0,16},{8,24},{16,0},{24,8},{32,48},{40,56},{48,32},{56,40},{1,17}... | collective-permute-start | bytes 393224 | tf_op jit(solution)/shard_map/ppermute | solution.py:323
  57.5 5.6 %collective-permute-done.2.quad_got = bf16[4,128,128]{2,1,0:T(8,128)(2,1)S(1)} collective-permute-done((bf16[4,128,128]{2,1,0:T(8,128)(2,1)S(1)}, bf16[4,128,128]{2,1,0:T(8,128)(2,1)S(1)}, u32[]{:S(2)}, u32[]{:S(2)}) %collective-permute-start.2) | collective-permute-done | bytes 131104 | tf_op jit(solution)/shard_map/ppermute | solution.py:323
  63.1 0.1 all-to-all-done.2.from_y
  63.3 1.4 %buckets.1 = (bf16[8,4,64,128]{3,2,1,0:T(8,128)(2,1)}, bf16[2,4,128,128]{3,2,1,0:T(8,128)(2,1)S(1)}) custom-call(s32[11]{0:T(128)S(1)} %pad_add_fusion.meta, bf16[2,64,128]{2,1,0:T(8,128)(2,1)S(1)} %get-tuple-element.50.halves, bf16[8,64,128]{2,1,0:T(8,128)(2,1)S(1)} %all-to-all-done.2.from_y, bf16[2,4,128,128]{3,2,1,0:T(8,128)(2,1)S(1)} %collective-permute-done.1.pair_got, ...), custom_call_target="tpu_custom_call" | custom-call | tf_op jit(solution)/shard_map/buckets/pallas_call | solution.py:403
  64.7 3.5 %all-to-all-start.3 = ((bf16[8,4,64,128]{3,2,1,0:T(8,128)(2,1)}), bf16[8,4,64,128]{3,2,1,0:T(8,128)(2,1)S(1)}, u32[]{:S(2)}, u32[]{:S(2)}) async-start(bf16[8,4,64,128]{3,2,1,0:T(8,128)(2,1)} %get-tuple-element.54), calls=%async_computation.3 | async-start | bytes 1048576 | tf_op jit(solution)/shard_map/all_to_all | solution.py:320
  68.2 2.8 %local.1 = (bf16[4,128,512]{2,1,0:T(8,128)(2,1)S(1)}, bf16[4,128,512]{2,1,0:T(8,128)(2,1)S(1)}, f32[32,256]{1,0:T(8,128)S(1)}) custom-call(s32[11]{0:T(128)S(1)} %pad_add_fusion.meta, bf16[4,128,512]{2,1,0:T(8,128)(2,1)S(1)} %get-tuple-element.38.own, bf16[4,128,512]{2,1,0:T(8,128)(2,1)S(1)} %collective-permute-done.other, ...), custom_call_target="tpu_custom_call" | custom-call | tf_op jit(solution)/shard_map/local/pallas_call | solution.py:391
  71.0 11.9 %all-to-all-done.3.got = bf16[8,4,64,128]{3,2,1,0:T(8,128)(2,1)S(1)} async-done(((bf16[8,4,64,128]{3,2,1,0:T(8,128)(2,1)}), bf16[8,4,64,128]{3,2,1,0:T(8,128)(2,1)S(1)}, u32[]{:S(2)}, u32[]{:S(2)}) %all-to-all-start.3) | async-done | bytes 524320 | tf_op jit(solution)/shard_map/all_to_all | solution.py:320
  82.8 1.6 %outputs.1 = (bf16[4,128,512]{2,1,0:T(8,128)(2,1)S(1)}, bf16[4,128,512]{2,1,0:T(8,128)(2,1)S(1)}, bf16[8,32,128]{2,1,0:T(8,128)(2,1)S(1)}) custom-call(s32[11]{0:T(128)S(1)} %pad_add_fusion.meta, bf16[4,128,512]{2,1,0:T(8,128)(2,1)S(1)} %get-tuple-element.38.own, ...), custom_call_target="tpu_custom_call", output_to_operand_aliasing={{0}: (5, {}), {1}: (6, {})} | custom-call | tf_op jit(solution)/shard_map/outputs/pallas_call | solution.py:412
  84.5 0.0 copy-start
  84.5 1.9 %grads.1 = (bf16[4,128,512]{2,1,0:T(8,128)(2,1)S(1)}, bf16[4,128,512]{2,1,0:T(8,128)(2,1)S(1)}) custom-call(s32[11]{0:T(128)S(1)} %pad_add_fusion.meta, bf16[4,128,512]{2,1,0:T(8,128)(2,1)S(1)} %get-tuple-element.38.own, bf16[4,128,512]{2,1,0:T(8,128)(2,1)S(1)} %collective-permute-done.other, ...), custom_call_target="tpu_custom_call", output_to_operand_aliasing={{0}: (4, {}), {1}: (5, {})} | custom-call | tf_op jit(solution)/shard_map/grads/pallas_call | solution.py:422
  86.4 5.6 %collective-permute-start.3 = (bf16[4,128,512]{2,1,0:T(8,128)(2,1)S(1)}, bf16[4,128,512]{2,1,0:T(8,128)(2,1)S(1)}, u32[]{:S(2)}, u32[]{:S(2)}) collective-permute-start(bf16[4,128,512]{2,1,0:T(8,128)(2,1)S(1)} %get-tuple-element.57), channel_id=1, source_target_pairs={{0,4},{4,0},{1,5},{5,1},{2,6},{6,2},{3,7},{7,3},{8,12},{12,8},{9,1... | collective-permute-start | bytes 1572872 | tf_op jit(solution)/shard_map/ppermute | solution.py:431
  92.0 7.4 %all_to_all.25.logit_grad = bf16[8,32,128]{2,1,0:T(8,128)(2,1)S(1)} all-to-all(bf16[8,32,128]{2,1,0:T(8,128)(2,1)S(1)} %get-tuple-element.59), channel_id=1, replica_groups=mesh['y'=8,'z'=8,'core'=2,'head'=4] {'core','head'}, dimensions={0} | all-to-all | bytes 131072 | tf_op jit(solution)/shard_map/all_to_all | solution.py:320
  99.4 0.0 copy-done
  99.4 1.5 %first.1 = (bf16[128,1024]{1,0:T(8,128)(2,1)}, bf16[128,1024]{1,0:T(8,128)(2,1)}, bf16[128,1024]{1,0:T(8,128)(2,1)}, bf16[128,1024]{1,0:T(8,128)(2,1)}, bf16[128,512]{1,0:T(8,128)(2,1)}) custom-call(bf16[4,128,512]{2,1,0:T(8,128)(2,1)S(1)} %get-tuple-element.58.keep, bf16[8,32,128]{2,1,0:T(8,128)(2,1)S(1)} %all_to_all.25.logit_grad, bf16[512,256]{1,0:T(8,128)(2,1)S(1)} %copy-done), custom_call_target="tpu_custom_call" | custom-call | tf_op jit(solution)/shard_map/first/pallas_call | solution.py:433
  100.9 0.0 collective-permute-done.3.got
  101.0 0.8 second.1
  (1 shorter events, 0.0 us)
Async XLA Ops:
  0.6 2.1 %copy-start.2 = (bf16[128,1024]{1,0:T(8,128)(2,1)S(1)}, bf16[128,1024]{1,0:T(8,128)(2,1)}, u32[]{:S(2)}) copy-start(bf16[128,1024]{1,0:T(8,128)(2,1)} %k.1) | copy-start | bytes 786436
  0.6 2.1 %copy-start.1 = (bf16[128,1024]{1,0:T(8,128)(2,1)S(1)}, bf16[128,1024]{1,0:T(8,128)(2,1)}, u32[]{:S(2)}) copy-start(bf16[128,1024]{1,0:T(8,128)(2,1)} %q.1) | copy-start | bytes 786436
  2.7 1.0 copy-start.3
  3.8 12.8 %collective-permute-start = (bf16[4,128,512]{2,1,0:T(8,128)(2,1)S(1)}, bf16[4,128,512]{2,1,0:T(8,128)(2,1)S(1)}, u32[]{:S(2)}, u32[]{:S(2)}) collective-permute-start(bf16[4,128,512]{2,1,0:T(8,128)(2,1)S(1)} %get-tuple-element.39), channel_id=1, source_target_pairs={{0,4},{4,0},{1,5},{5,1},{2,6},{6,2},{3,7},{7,3},{8,12},{12,8},{9,1... | collective-permute-start | bytes 1572872 | tf_op jit(solution)/shard_map/ppermute | solution.py:347
  12.5 8.5 %all-to-all-start = ((f32[8,32,128]{2,1,0:T(8,128)}), f32[8,32,128]{2,1,0:T(8,128)S(1)}, u32[]{:S(2)}, u32[]{:S(2)}) async-start(f32[8,32,128]{2,1,0:T(8,128)} %get-tuple-element.40), calls=%async_computation | async-start | bytes 262144 | tf_op jit(solution)/shard_map/all_to_all | solution.py:320
  15.9 0.7 copy-start.4
  23.9 23.5 %all-to-all-start.1 = ((bf16[8,4,64,128]{3,2,1,0:T(8,128)(2,1)}), bf16[8,4,64,128]{3,2,1,0:T(8,128)(2,1)S(1)}, u32[]{:S(2)}, u32[]{:S(2)}) async-start(bf16[8,4,64,128]{3,2,1,0:T(8,128)(2,1)} %get-tuple-element.49), calls=%async_computation.1 | async-start | bytes 1048576 | tf_op jit(solution)/shard_map/all_to_all | solution.py:320
  29.7 25.8 %collective-permute-start.1 = (bf16[2,4,128,128]{3,2,1,0:T(8,128)(2,1)S(1)}, bf16[2,4,128,128]{3,2,1,0:T(8,128)(2,1)S(1)}, u32[]{:S(2)}, u32[]{:S(2)}) collective-permute-start(bf16[2,4,128,128]{3,2,1,0:T(8,128)(2,1)S(1)} %get-tuple-element.52.pair), channel_id=1, source_target_pairs={{0,8},{8,0},{16,24},{24,16},{32,40},{40,32},{48,56},{56,48},{1,9},... | collective-permute-start | bytes 786440 | tf_op jit(solution)/shard_map/ppermute | solution.py:323
  48.7 14.6 %all-to-all-start.2 = ((bf16[8,64,128]{2,1,0:T(8,128)(2,1)}), bf16[8,64,128]{2,1,0:T(8,128)(2,1)S(1)}, u32[]{:S(2)}, u32[]{:S(2)}) async-start(bf16[8,64,128]{2,1,0:T(8,128)(2,1)} %get-tuple-element.51), calls=%async_computation.2 | async-start | bytes 262144 | tf_op jit(solution)/shard_map/all_to_all | solution.py:320
  55.5 7.6 %collective-permute-start.2 = (bf16[4,128,128]{2,1,0:T(8,128)(2,1)S(1)}, bf16[4,128,128]{2,1,0:T(8,128)(2,1)S(1)}, u32[]{:S(2)}, u32[]{:S(2)}) collective-permute-start(bf16[4,128,128]{2,1,0:T(8,128)(2,1)S(1)} %pair.1), channel_id=1, source_target_pairs={{0,16},{8,24},{16,0},{24,8},{32,48},{40,56},{48,32},{56,40},{1,17}... | collective-permute-start | bytes 393224 | tf_op jit(solution)/shard_map/ppermute | solution.py:323
  64.7 18.2 %all-to-all-start.3 = ((bf16[8,4,64,128]{3,2,1,0:T(8,128)(2,1)}), bf16[8,4,64,128]{3,2,1,0:T(8,128)(2,1)S(1)}, u32[]{:S(2)}, u32[]{:S(2)}) async-start(bf16[8,4,64,128]{3,2,1,0:T(8,128)(2,1)} %get-tuple-element.54), calls=%async_computation.3 | async-start | bytes 1048576 | tf_op jit(solution)/shard_map/all_to_all | solution.py:320
  84.5 15.0 %copy-start = (bf16[512,256]{1,0:T(8,128)(2,1)S(1)}, bf16[512,256]{1,0:T(8,128)(2,1)}, u32[]{:S(2)}) copy-start(bf16[512,256]{1,0:T(8,128)(2,1)} %gate.3) | copy-start | bytes 786436
  86.4 14.6 %collective-permute-start.3 = (bf16[4,128,512]{2,1,0:T(8,128)(2,1)S(1)}, bf16[4,128,512]{2,1,0:T(8,128)(2,1)S(1)}, u32[]{:S(2)}, u32[]{:S(2)}) collective-permute-start(bf16[4,128,512]{2,1,0:T(8,128)(2,1)S(1)} %get-tuple-element.57), channel_id=1, source_target_pairs={{0,4},{4,0},{1,5},{5,1},{2,6},{6,2},{3,7},{7,3},{8,12},{12,8},{9,1... | collective-permute-start | bytes 1572872 | tf_op jit(solution)/shard_map/ppermute | solution.py:431

commit v7 on v6

--- a/solution.py
+++ b/solution.py
@@ -103,19 +103,19 @@
     padded = jnp.concatenate([weights, jnp.zeros((128 - 8 * HALF, 2 * SPAN), F32)], 0)
     for s in range(2):
         cols[s] = jnp.transpose(padded[:, s * SPAN : (s + 1) * SPAN])
-    both = jnp.concatenate([cols[0], cols[1]], 0)
+    both = jnp.concatenate([cols[0], cols[1]], 0).astype(BF)
     first = core == 0
     for h in range(HALF):
         lanes = slice(h * DK, (h + 1) * DK)
         q = jnp.concatenate([own[0, :, lanes], other[0, :, lanes]], 0)
-        g = jnp.concatenate([own[3, :, lanes], other[3, :, lanes]], 0).astype(F32)
+        g = jnp.concatenate([own[3, :, lanes], other[3, :, lanes]], 0)
         near = both[:, h * 8 + 1 : h * 8 + 2]
-        near_g = (near * g).astype(BF)
+        near_g = near * g
         grad_own = dot(q[:SPAN], near_g[:SPAN], 0, 0)
         grad_other = dot(q[SPAN:], near_g[SPAN:], 0, 0)
         near_grad[h] = (jnp.where(first, grad_other, grad_own) / SPAN).astype(BF)
         weighted = jnp.concatenate(
-            [(both[:, h * 8 + 2 + i : h * 8 + 3 + i] * g).astype(BF) for i in range(SLOTS)], 1
+            [both[:, h * 8 + 2 + i : h * 8 + 3 + i] * g for i in range(SLOTS)], 1
         )
         grads = dot(q, weighted, 0, 0)
         held = state[h]
@@ -255,13 +255,12 @@
 
 def grads_body(meta, own, other, cols, part_own, part_other, direct, got, keep, send):
     bits = level_bits(meta)
-    both = jnp.concatenate([cols[0], cols[1]], 0)
+    both = jnp.concatenate([cols[0], cols[1]], 0).astype(BF)
     for h in range(HALF):
         lanes = slice(h * DK, (h + 1) * DK)
         k, v, g = (
             jnp.concatenate([own[i, :, lanes], other[i, :, lanes]], 0) for i in range(1, 4)
         )
-        gf = g.astype(F32)
         levels, weighted = [], []
         back = jnp.zeros((DK, DK), F32)
         for i in range(SLOTS):
@@ -269,7 +268,7 @@
             zero = jnp.zeros_like(state)
             levels.append(jnp.where(bits[i] == 1, state, zero))
             back = back + jnp.where(bits[i] == 1, zero, state).astype(F32)
-            weighted.append((both[:, h * 8 + 2 + i : h * 8 + 3 + i] * gf).astype(BF))
+            weighted.append(both[:, h * 8 + 2 + i : h * 8 + 3 + i] * g)
         back = back.astype(BF)
         found = (
             dot(jnp.concatenate(weighted, 1), jnp.concatenate(levels, 1), 1, 1),

time: 102 us -> 102 us (level)
  no operation moved by 1% of the time
where the time goes in v7:
time: 102 us; the launch traced here: 101 us
  starting transfers between devices  39.1 us (38%)
  waiting for transfers between devices  36.2 us (35%)
  Pallas kernels  15.9 us (16%)
  blocking collectives  7.41 us (7%)
  local copies, waits for them, and re-layouts  1.61 us (2%)
    all_to_all x4, waiting for transfers between devices, exchange(): return lax.all_to_all(array, axis, 0, 0, tiled=True)  30.5 us
    all_to_all x4, starting transfers between devices, exchange(): return lax.all_to_all(array, axis, 0, 0, tiled=True)  19.4 us
    ppermute x1, starting transfers between devices, local(): other = lax.ppermute(send, 'core', swap)  8.75 us
    all_to_all x1, blocking collectives, exchange(): return lax.all_to_all(array, axis, 0, 0, tiled=True)  7.41 us
    ppermute x2, waiting for transfers between devices, flip(): return lax.ppermute(array, 'z', [(i, i ^ distance) for i in range(8)])  5.64 us
    ppermute x1, starting transfers between devices, local(): back = lax.ppermute(away, 'core', swap)  5.61 us
    ppermute x2, starting transfers between devices, flip(): return lax.ppermute(array, 'z', [(i, i ^ distance) for i in range(8)])  5.28 us
    pallas_call x1, Pallas kernels, local(): pl.pallas_call(local_body, out_shape=(shape(4, SPAN, LANES), shape(4, SPA...  2.79 us
  transfers between devices with their start and end apart: 8, of which 5 were waited for; matrix products, arithmetic and copies ran while one was open for 0% of the time, Pallas kernels for 6%

profile of v7, /device:TPU:1, one launch (start us, length us, event | category | flops | bytes accessed | tf_op | source)
XLA Modules:
  0.0 101.0 jit_solution(6791733175041780146)
XLA Ops:
  0.6 0.0 copy-start.2
  0.6 0.0 copy-start.1
  0.7 2.0 %logits.1 = (f32[8,32,128]{2,1,0:T(8,128)}, bf16[128,1024]{1,0:T(8,128)(2,1)S(1)}) custom-call(bf16[128,512]{1,0:T(8,128)(2,1)} %hidden.1, bf16[512,256]{1,0:T(8,128)(2,1)} %gate.3, bf16[128,1024]{1,0:T(8,128)(2,1)} %g.1), custom_call_target="tpu_custom_call" | custom-call | tf_op jit(solution)/shard_map/logits/pallas_call | solution.py:324
  2.7 0.0 copy-done.2
  2.7 0.0 copy-done.1
  2.7 0.0 copy-start.3
  2.7 0.9 copy-done.3
  3.7 0.1 pack.1
  3.8 8.7 %collective-permute-start = (bf16[4,128,512]{2,1,0:T(8,128)(2,1)S(1)}, bf16[4,128,512]{2,1,0:T(8,128)(2,1)S(1)}, u32[]{:S(2)}, u32[]{:S(2)}) collective-permute-start(bf16[4,128,512]{2,1,0:T(8,128)(2,1)S(1)} %get-tuple-element.39), channel_id=1, source_target_pairs={{0,4},{4,0},{1,5},{5,1},{2,6},{6,2},{3,7},{7,3},{8,12},{12,8},{9,1... | collective-permute-start | bytes 1572872 | tf_op jit(solution)/shard_map/ppermute | solution.py:346
  12.5 3.3 %all-to-all-start = ((f32[8,32,128]{2,1,0:T(8,128)}), f32[8,32,128]{2,1,0:T(8,128)S(1)}, u32[]{:S(2)}, u32[]{:S(2)}) async-start(f32[8,32,128]{2,1,0:T(8,128)} %get-tuple-element.40), calls=%async_computation | async-start | bytes 262144 | tf_op jit(solution)/shard_map/all_to_all | solution.py:319
  15.9 0.0 copy-start.4
  15.9 0.6 copy-done.4
  16.5 0.1 pad_add_fusion.meta
  16.6 0.0 collective-permute-done.other
  16.6 0.3 pre.1
  16.9 4.2 %all-to-all-done.parts = f32[8,32,128]{2,1,0:T(8,128)S(1)} async-done(((f32[8,32,128]{2,1,0:T(8,128)}), f32[8,32,128]{2,1,0:T(8,128)S(1)}, u32[]{:S(2)}, u32[]{:S(2)}) %all-to-all-start) | async-done | bytes 131104 | tf_op jit(solution)/shard_map/all_to_all | solution.py:319
  21.0 2.4 %states.1 = (bf16[8,4,64,128]{3,2,1,0:T(8,128)(2,1)}, bf16[2,4,128,128]{3,2,1,0:T(8,128)(2,1)S(1)}, f32[2,128,128]{2,1,0:T(8,128)S(1)}, f32[32,256]{1,0:T(8,128)S(1)}, bf16[4,128,128]{2,1,0:T(8,128)(2,1)S(1)}) custom-call(s32[11]{0:T(128)S(1)} %pad_add_fusion.meta, f32[8,32,128]{2,1,0:T(8,128)S(1)} %all-to-all-done.parts, ...), custom_call_target="tpu_custom_call" | custom-call | tf_op jit(solution)/shard_map/states/pallas_call | solution.py:355
  23.4 5.8 %all-to-all-start.1 = ((bf16[8,4,64,128]{3,2,1,0:T(8,128)(2,1)}), bf16[8,4,64,128]{3,2,1,0:T(8,128)(2,1)S(1)}, u32[]{:S(2)}, u32[]{:S(2)}) async-start(bf16[8,4,64,128]{3,2,1,0:T(8,128)(2,1)} %get-tuple-element.49), calls=%async_computation.1 | async-start | bytes 1048576 | tf_op jit(solution)/shard_map/all_to_all | solution.py:319
  29.2 3.4 %collective-permute-start.1 = (bf16[2,4,128,128]{3,2,1,0:T(8,128)(2,1)S(1)}, bf16[2,4,128,128]{3,2,1,0:T(8,128)(2,1)S(1)}, u32[]{:S(2)}, u32[]{:S(2)}) collective-permute-start(bf16[2,4,128,128]{3,2,1,0:T(8,128)(2,1)S(1)} %get-tuple-element.52.pair), channel_id=1, source_target_pairs={{0,8},{8,0},{16,24},{24,16},{32,40},{40,32},{48,56},{56,48},{1,9},... | collective-permute-start | bytes 786440 | tf_op jit(solution)/shard_map/ppermute | solution.py:322
  32.6 14.4 %all-to-all-done.1.got = bf16[8,4,64,128]{3,2,1,0:T(8,128)(2,1)S(1)} async-done(((bf16[8,4,64,128]{3,2,1,0:T(8,128)(2,1)}), bf16[8,4,64,128]{3,2,1,0:T(8,128)(2,1)S(1)}, u32[]{:S(2)}, u32[]{:S(2)}) %all-to-all-start.1) | async-done | bytes 524320 | tf_op jit(solution)/shard_map/all_to_all | solution.py:319
  47.0 1.3 %along_z.1 = (bf16[8,64,128]{2,1,0:T(8,128)(2,1)}, bf16[2,64,128]{2,1,0:T(8,128)(2,1)S(1)}) custom-call(s32[11]{0:T(128)S(1)} %pad_add_fusion.meta, bf16[8,4,64,128]{3,2,1,0:T(8,128)(2,1)S(1)} %all-to-all-done.1.got), custom_call_target="tpu_custom_call" | custom-call | tf_op jit(solution)/shard_map/along_z/pallas_call | solution.py:372
  48.2 6.8 %all-to-all-start.2 = ((bf16[8,64,128]{2,1,0:T(8,128)(2,1)}), bf16[8,64,128]{2,1,0:T(8,128)(2,1)S(1)}, u32[]{:S(2)}, u32[]{:S(2)}) async-start(bf16[8,64,128]{2,1,0:T(8,128)(2,1)} %get-tuple-element.51), calls=%async_computation.2 | async-start | bytes 262144 | tf_op jit(solution)/shard_map/all_to_all | solution.py:319
  55.0 0.0 collective-permute-done.1.pair_got
  55.1 1.9 %collective-permute-start.2 = (bf16[4,128,128]{2,1,0:T(8,128)(2,1)S(1)}, bf16[4,128,128]{2,1,0:T(8,128)(2,1)S(1)}, u32[]{:S(2)}, u32[]{:S(2)}) collective-permute-start(bf16[4,128,128]{2,1,0:T(8,128)(2,1)S(1)} %pair.1), channel_id=1, source_target_pairs={{0,16},{8,24},{16,0},{24,8},{32,48},{40,56},{48,32},{56,40},{1,17}... | collective-permute-start | bytes 393224 | tf_op jit(solution)/shard_map/ppermute | solution.py:322
  57.0 5.6 %collective-permute-done.2.quad_got = bf16[4,128,128]{2,1,0:T(8,128)(2,1)S(1)} collective-permute-done((bf16[4,128,128]{2,1,0:T(8,128)(2,1)S(1)}, bf16[4,128,128]{2,1,0:T(8,128)(2,1)S(1)}, u32[]{:S(2)}, u32[]{:S(2)}) %collective-permute-start.2) | collective-permute-done | bytes 131104 | tf_op jit(solution)/shard_map/ppermute | solution.py:322
  62.6 0.1 all-to-all-done.2.from_y
  62.8 1.4 %buckets.1 = (bf16[8,4,64,128]{3,2,1,0:T(8,128)(2,1)}, bf16[2,4,128,128]{3,2,1,0:T(8,128)(2,1)S(1)}) custom-call(s32[11]{0:T(128)S(1)} %pad_add_fusion.meta, bf16[2,64,128]{2,1,0:T(8,128)(2,1)S(1)} %get-tuple-element.50.halves, bf16[8,64,128]{2,1,0:T(8,128)(2,1)S(1)} %all-to-all-done.2.from_y, bf16[2,4,128,128]{3,2,1,0:T(8,128)(2,1)S(1)} %collective-permute-done.1.pair_got, ...), custom_call_target="tpu_custom_call" | custom-call | tf_op jit(solution)/shard_map/buckets/pallas_call | solution.py:402
  64.2 3.5 %all-to-all-start.3 = ((bf16[8,4,64,128]{3,2,1,0:T(8,128)(2,1)}), bf16[8,4,64,128]{3,2,1,0:T(8,128)(2,1)S(1)}, u32[]{:S(2)}, u32[]{:S(2)}) async-start(bf16[8,4,64,128]{3,2,1,0:T(8,128)(2,1)} %get-tuple-element.54), calls=%async_computation.3 | async-start | bytes 1048576 | tf_op jit(solution)/shard_map/all_to_all | solution.py:319
  67.7 2.8 %local.1 = (bf16[4,128,512]{2,1,0:T(8,128)(2,1)S(1)}, bf16[4,128,512]{2,1,0:T(8,128)(2,1)S(1)}, f32[32,256]{1,0:T(8,128)S(1)}) custom-call(s32[11]{0:T(128)S(1)} %pad_add_fusion.meta, bf16[4,128,512]{2,1,0:T(8,128)(2,1)S(1)} %get-tuple-element.38.own, bf16[4,128,512]{2,1,0:T(8,128)(2,1)S(1)} %collective-permute-done.other, ...), custom_call_target="tpu_custom_call" | custom-call | tf_op jit(solution)/shard_map/local/pallas_call | solution.py:390
  70.5 11.9 %all-to-all-done.3.got = bf16[8,4,64,128]{3,2,1,0:T(8,128)(2,1)S(1)} async-done(((bf16[8,4,64,128]{3,2,1,0:T(8,128)(2,1)}), bf16[8,4,64,128]{3,2,1,0:T(8,128)(2,1)S(1)}, u32[]{:S(2)}, u32[]{:S(2)}) %all-to-all-start.3) | async-done | bytes 524320 | tf_op jit(solution)/shard_map/all_to_all | solution.py:319
  82.4 1.6 %outputs.1 = (bf16[4,128,512]{2,1,0:T(8,128)(2,1)S(1)}, bf16[4,128,512]{2,1,0:T(8,128)(2,1)S(1)}, bf16[8,32,128]{2,1,0:T(8,128)(2,1)S(1)}) custom-call(s32[11]{0:T(128)S(1)} %pad_add_fusion.meta, bf16[4,128,512]{2,1,0:T(8,128)(2,1)S(1)} %get-tuple-element.38.own, ...), custom_call_target="tpu_custom_call", output_to_operand_aliasing={{0}: (5, {}), {1}: (6, {})} | custom-call | tf_op jit(solution)/shard_map/outputs/pallas_call | solution.py:411
  84.0 0.0 copy-start
  84.0 1.6 %grads.1 = (bf16[4,128,512]{2,1,0:T(8,128)(2,1)S(1)}, bf16[4,128,512]{2,1,0:T(8,128)(2,1)S(1)}) custom-call(s32[11]{0:T(128)S(1)} %pad_add_fusion.meta, bf16[4,128,512]{2,1,0:T(8,128)(2,1)S(1)} %get-tuple-element.38.own, bf16[4,128,512]{2,1,0:T(8,128)(2,1)S(1)} %collective-permute-done.other, ...), custom_call_target="tpu_custom_call", output_to_operand_aliasing={{0}: (4, {}), {1}: (5, {})} | custom-call | tf_op jit(solution)/shard_map/grads/pallas_call | solution.py:421
  85.6 5.6 %collective-permute-start.3 = (bf16[4,128,512]{2,1,0:T(8,128)(2,1)S(1)}, bf16[4,128,512]{2,1,0:T(8,128)(2,1)S(1)}, u32[]{:S(2)}, u32[]{:S(2)}) collective-permute-start(bf16[4,128,512]{2,1,0:T(8,128)(2,1)S(1)} %get-tuple-element.57), channel_id=1, source_target_pairs={{0,4},{4,0},{1,5},{5,1},{2,6},{6,2},{3,7},{7,3},{8,12},{12,8},{9,1... | collective-permute-start | bytes 1572872 | tf_op jit(solution)/shard_map/ppermute | solution.py:430
  91.2 7.4 %all_to_all.25.logit_grad = bf16[8,32,128]{2,1,0:T(8,128)(2,1)S(1)} all-to-all(bf16[8,32,128]{2,1,0:T(8,128)(2,1)S(1)} %get-tuple-element.59), channel_id=1, replica_groups=mesh['y'=8,'z'=8,'core'=2,'head'=4] {'core','head'}, dimensions={0} | all-to-all | bytes 131072 | tf_op jit(solution)/shard_map/all_to_all | solution.py:319
  98.6 0.0 copy-done
  98.6 1.5 %first.1 = (bf16[128,1024]{1,0:T(8,128)(2,1)}, bf16[128,1024]{1,0:T(8,128)(2,1)}, bf16[128,1024]{1,0:T(8,128)(2,1)}, bf16[128,1024]{1,0:T(8,128)(2,1)}, bf16[128,512]{1,0:T(8,128)(2,1)}) custom-call(bf16[4,128,512]{2,1,0:T(8,128)(2,1)S(1)} %get-tuple-element.58.keep, bf16[8,32,128]{2,1,0:T(8,128)(2,1)S(1)} %all_to_all.25.logit_grad, bf16[512,256]{1,0:T(8,128)(2,1)S(1)} %copy-done), custom_call_target="tpu_custom_call" | custom-call | tf_op jit(solution)/shard_map/first/pallas_call | solution.py:432
  100.2 0.0 collective-permute-done.3.got
  100.2 0.8 second.1
  (1 shorter events, 0.0 us)
Async XLA Ops:
  0.6 2.1 %copy-start.2 = (bf16[128,1024]{1,0:T(8,128)(2,1)S(1)}, bf16[128,1024]{1,0:T(8,128)(2,1)}, u32[]{:S(2)}) copy-start(bf16[128,1024]{1,0:T(8,128)(2,1)} %k.1) | copy-start | bytes 786436
  0.6 2.1 %copy-start.1 = (bf16[128,1024]{1,0:T(8,128)(2,1)S(1)}, bf16[128,1024]{1,0:T(8,128)(2,1)}, u32[]{:S(2)}) copy-start(bf16[128,1024]{1,0:T(8,128)(2,1)} %q.1) | copy-start | bytes 786436
  2.7 1.0 copy-start.3
  3.8 12.8 %collective-permute-start = (bf16[4,128,512]{2,1,0:T(8,128)(2,1)S(1)}, bf16[4,128,512]{2,1,0:T(8,128)(2,1)S(1)}, u32[]{:S(2)}, u32[]{:S(2)}) collective-permute-start(bf16[4,128,512]{2,1,0:T(8,128)(2,1)S(1)} %get-tuple-element.39), channel_id=1, source_target_pairs={{0,4},{4,0},{1,5},{5,1},{2,6},{6,2},{3,7},{7,3},{8,12},{12,8},{9,1... | collective-permute-start | bytes 1572872 | tf_op jit(solution)/shard_map/ppermute | solution.py:346
  12.5 8.5 %all-to-all-start = ((f32[8,32,128]{2,1,0:T(8,128)}), f32[8,32,128]{2,1,0:T(8,128)S(1)}, u32[]{:S(2)}, u32[]{:S(2)}) async-start(f32[8,32,128]{2,1,0:T(8,128)} %get-tuple-element.40), calls=%async_computation | async-start | bytes 262144 | tf_op jit(solution)/shard_map/all_to_all | solution.py:319
  15.9 0.7 copy-start.4
  23.4 23.5 %all-to-all-start.1 = ((bf16[8,4,64,128]{3,2,1,0:T(8,128)(2,1)}), bf16[8,4,64,128]{3,2,1,0:T(8,128)(2,1)S(1)}, u32[]{:S(2)}, u32[]{:S(2)}) async-start(bf16[8,4,64,128]{3,2,1,0:T(8,128)(2,1)} %get-tuple-element.49), calls=%async_computation.1 | async-start | bytes 1048576 | tf_op jit(solution)/shard_map/all_to_all | solution.py:319
  29.2 25.8 %collective-permute-start.1 = (bf16[2,4,128,128]{3,2,1,0:T(8,128)(2,1)S(1)}, bf16[2,4,128,128]{3,2,1,0:T(8,128)(2,1)S(1)}, u32[]{:S(2)}, u32[]{:S(2)}) collective-permute-start(bf16[2,4,128,128]{3,2,1,0:T(8,128)(2,1)S(1)} %get-tuple-element.52.pair), channel_id=1, source_target_pairs={{0,8},{8,0},{16,24},{24,16},{32,40},{40,32},{48,56},{56,48},{1,9},... | collective-permute-start | bytes 786440 | tf_op jit(solution)/shard_map/ppermute | solution.py:322
  48.2 14.6 %all-to-all-start.2 = ((bf16[8,64,128]{2,1,0:T(8,128)(2,1)}), bf16[8,64,128]{2,1,0:T(8,128)(2,1)S(1)}, u32[]{:S(2)}, u32[]{:S(2)}) async-start(bf16[8,64,128]{2,1,0:T(8,128)(2,1)} %get-tuple-element.51), calls=%async_computation.2 | async-start | bytes 262144 | tf_op jit(solution)/shard_map/all_to_all | solution.py:319
  55.1 7.6 %collective-permute-start.2 = (bf16[4,128,128]{2,1,0:T(8,128)(2,1)S(1)}, bf16[4,128,128]{2,1,0:T(8,128)(2,1)S(1)}, u32[]{:S(2)}, u32[]{:S(2)}) collective-permute-start(bf16[4,128,128]{2,1,0:T(8,128)(2,1)S(1)} %pair.1), channel_id=1, source_target_pairs={{0,16},{8,24},{16,0},{24,8},{32,48},{40,56},{48,32},{56,40},{1,17}... | collective-permute-start | bytes 393224 | tf_op jit(solution)/shard_map/ppermute | solution.py:322
  64.2 18.2 %all-to-all-start.3 = ((bf16[8,4,64,128]{3,2,1,0:T(8,128)(2,1)}), bf16[8,4,64,128]{3,2,1,0:T(8,128)(2,1)S(1)}, u32[]{:S(2)}, u32[]{:S(2)}) async-start(bf16[8,4,64,128]{3,2,1,0:T(8,128)(2,1)} %get-tuple-element.54), calls=%async_computation.3 | async-start | bytes 1048576 | tf_op jit(solution)/shard_map/all_to_all | solution.py:319
  84.0 14.7 %copy-start = (bf16[512,256]{1,0:T(8,128)(2,1)S(1)}, bf16[512,256]{1,0:T(8,128)(2,1)}, u32[]{:S(2)}) copy-start(bf16[512,256]{1,0:T(8,128)(2,1)} %gate.3) | copy-start | bytes 786436
  85.6 14.6 %collective-permute-start.3 = (bf16[4,128,512]{2,1,0:T(8,128)(2,1)S(1)}, bf16[4,128,512]{2,1,0:T(8,128)(2,1)S(1)}, u32[]{:S(2)}, u32[]{:S(2)}) collective-permute-start(bf16[4,128,512]{2,1,0:T(8,128)(2,1)S(1)} %get-tuple-element.57), channel_id=1, source_target_pairs={{0,4},{4,0},{1,5},{5,1},{2,6},{6,2},{3,7},{7,3},{8,12},{12,8},{9,1... | collective-permute-start | bytes 1572872 | tf_op jit(solution)/shard_map/ppermute | solution.py:430

commit v8 on v7

--- a/solution.py
+++ b/solution.py
@@ -224,7 +224,7 @@
 ):
     core = meta[0]
     bits = level_bits(meta)
-    both = jnp.concatenate([cols[0], cols[1]], 0)
+    both = jnp.concatenate([cols[0], cols[1]], 0).astype(BF)
     total = sums[...]
     for h in range(HALF):
         lanes = slice(h * DK, (h + 1) * DK)
@@ -239,7 +239,8 @@
         products = []
         for i in range(SLOTS):
             out = outs[:, i * DK : (i + 1) * DK]
-            mix = mix + both[:, h * 8 + 2 + i : h * 8 + 3 + i] * out
+            wide = jnp.broadcast_to(both[:, h * 8 + 2 + i : h * 8 + 3 + i], (2 * SPAN, DK))
+            mix = mix + wide.astype(F32) * out
             products.append((gf * out).astype(BF))
         total = total + dot(
             row_picker(meta, h, range(2, 8)), jnp.concatenate(products, 1), 1, 1

time: 102 us -> 102 us (level)
  no operation moved by 1% of the time
where the time goes in v8:
time: 102 us; the launch traced here: 101 us
  starting transfers between devices  39.1 us (38%)
  waiting for transfers between devices  36.2 us (35%)
  Pallas kernels  15.9 us (16%)
  blocking collectives  7.42 us (7%)
  local copies, waits for them, and re-layouts  1.61 us (2%)
    all_to_all x4, waiting for transfers between devices, exchange(): return lax.all_to_all(array, axis, 0, 0, tiled=True)  30.5 us
    all_to_all x4, starting transfers between devices, exchange(): return lax.all_to_all(array, axis, 0, 0, tiled=True)  19.4 us
    ppermute x1, starting transfers between devices, local(): other = lax.ppermute(send, 'core', swap)  8.75 us
    all_to_all x1, blocking collectives, exchange(): return lax.all_to_all(array, axis, 0, 0, tiled=True)  7.42 us
    ppermute x2, waiting for transfers between devices, flip(): return lax.ppermute(array, 'z', [(i, i ^ distance) for i in range(8)])  5.64 us
    ppermute x1, starting transfers between devices, local(): back = lax.ppermute(away, 'core', swap)  5.61 us
    ppermute x2, starting transfers between devices, flip(): return lax.ppermute(array, 'z', [(i, i ^ distance) for i in range(8)])  5.28 us
    pallas_call x1, Pallas kernels, local(): pl.pallas_call(local_body, out_shape=(shape(4, SPAN, LANES), shape(4, SPA...  2.79 us
  transfers between devices with their start and end apart: 8, of which 5 were waited for; matrix products, arithmetic and copies ran while one was open for 0% of the time, Pallas kernels for 6%

profile of v8, /device:TPU:1, one launch (start us, length us, event | category | flops | bytes accessed | tf_op | source)
XLA Modules:
  0.0 101.0 jit_solution(15677004498062630743)
XLA Ops:
  0.6 0.0 copy-start.2
  0.6 0.0 copy-start.1
  0.7 2.0 %logits.1 = (f32[8,32,128]{2,1,0:T(8,128)}, bf16[128,1024]{1,0:T(8,128)(2,1)S(1)}) custom-call(bf16[128,512]{1,0:T(8,128)(2,1)} %hidden.1, bf16[512,256]{1,0:T(8,128)(2,1)} %gate.3, bf16[128,1024]{1,0:T(8,128)(2,1)} %g.1), custom_call_target="tpu_custom_call" | custom-call | tf_op jit(solution)/shard_map/logits/pallas_call | solution.py:325
  2.7 0.0 copy-done.2
  2.7 0.0 copy-done.1
  2.7 0.0 copy-start.3
  2.7 0.9 copy-done.3
  3.7 0.1 pack.1
  3.8 8.7 %collective-permute-start = (bf16[4,128,512]{2,1,0:T(8,128)(2,1)S(1)}, bf16[4,128,512]{2,1,0:T(8,128)(2,1)S(1)}, u32[]{:S(2)}, u32[]{:S(2)}) collective-permute-start(bf16[4,128,512]{2,1,0:T(8,128)(2,1)S(1)} %get-tuple-element.39), channel_id=1, source_target_pairs={{0,4},{4,0},{1,5},{5,1},{2,6},{6,2},{3,7},{7,3},{8,12},{12,8},{9,1... | collective-permute-start | bytes 1572872 | tf_op jit(solution)/shard_map/ppermute | solution.py:347
  12.5 3.3 %all-to-all-start = ((f32[8,32,128]{2,1,0:T(8,128)}), f32[8,32,128]{2,1,0:T(8,128)S(1)}, u32[]{:S(2)}, u32[]{:S(2)}) async-start(f32[8,32,128]{2,1,0:T(8,128)} %get-tuple-element.40), calls=%async_computation | async-start | bytes 262144 | tf_op jit(solution)/shard_map/all_to_all | solution.py:320
  15.9 0.0 copy-start.4
  15.9 0.6 copy-done.4
  16.5 0.1 pad_add_fusion.meta
  16.6 0.0 collective-permute-done.other
  16.6 0.3 pre.1
  16.9 4.2 %all-to-all-done.parts = f32[8,32,128]{2,1,0:T(8,128)S(1)} async-done(((f32[8,32,128]{2,1,0:T(8,128)}), f32[8,32,128]{2,1,0:T(8,128)S(1)}, u32[]{:S(2)}, u32[]{:S(2)}) %all-to-all-start) | async-done | bytes 131104 | tf_op jit(solution)/shard_map/all_to_all | solution.py:320
  21.0 2.4 %states.1 = (bf16[8,4,64,128]{3,2,1,0:T(8,128)(2,1)}, bf16[2,4,128,128]{3,2,1,0:T(8,128)(2,1)S(1)}, f32[2,128,128]{2,1,0:T(8,128)S(1)}, f32[32,256]{1,0:T(8,128)S(1)}, bf16[4,128,128]{2,1,0:T(8,128)(2,1)S(1)}) custom-call(s32[11]{0:T(128)S(1)} %pad_add_fusion.meta, f32[8,32,128]{2,1,0:T(8,128)S(1)} %all-to-all-done.parts, ...), custom_call_target="tpu_custom_call" | custom-call | tf_op jit(solution)/shard_map/states/pallas_call | solution.py:356
  23.4 5.8 %all-to-all-start.1 = ((bf16[8,4,64,128]{3,2,1,0:T(8,128)(2,1)}), bf16[8,4,64,128]{3,2,1,0:T(8,128)(2,1)S(1)}, u32[]{:S(2)}, u32[]{:S(2)}) async-start(bf16[8,4,64,128]{3,2,1,0:T(8,128)(2,1)} %get-tuple-element.49), calls=%async_computation.1 | async-start | bytes 1048576 | tf_op jit(solution)/shard_map/all_to_all | solution.py:320
  29.2 3.4 %collective-permute-start.1 = (bf16[2,4,128,128]{3,2,1,0:T(8,128)(2,1)S(1)}, bf16[2,4,128,128]{3,2,1,0:T(8,128)(2,1)S(1)}, u32[]{:S(2)}, u32[]{:S(2)}) collective-permute-start(bf16[2,4,128,128]{3,2,1,0:T(8,128)(2,1)S(1)} %get-tuple-element.52.pair), channel_id=1, source_target_pairs={{0,8},{8,0},{16,24},{24,16},{32,40},{40,32},{48,56},{56,48},{1,9},... | collective-permute-start | bytes 786440 | tf_op jit(solution)/shard_map/ppermute | solution.py:323
  32.6 14.4 %all-to-all-done.1.got = bf16[8,4,64,128]{3,2,1,0:T(8,128)(2,1)S(1)} async-done(((bf16[8,4,64,128]{3,2,1,0:T(8,128)(2,1)}), bf16[8,4,64,128]{3,2,1,0:T(8,128)(2,1)S(1)}, u32[]{:S(2)}, u32[]{:S(2)}) %all-to-all-start.1) | async-done | bytes 524320 | tf_op jit(solution)/shard_map/all_to_all | solution.py:320
  47.0 1.3 %along_z.1 = (bf16[8,64,128]{2,1,0:T(8,128)(2,1)}, bf16[2,64,128]{2,1,0:T(8,128)(2,1)S(1)}) custom-call(s32[11]{0:T(128)S(1)} %pad_add_fusion.meta, bf16[8,4,64,128]{3,2,1,0:T(8,128)(2,1)S(1)} %all-to-all-done.1.got), custom_call_target="tpu_custom_call" | custom-call | tf_op jit(solution)/shard_map/along_z/pallas_call | solution.py:373
  48.2 6.8 %all-to-all-start.2 = ((bf16[8,64,128]{2,1,0:T(8,128)(2,1)}), bf16[8,64,128]{2,1,0:T(8,128)(2,1)S(1)}, u32[]{:S(2)}, u32[]{:S(2)}) async-start(bf16[8,64,128]{2,1,0:T(8,128)(2,1)} %get-tuple-element.51), calls=%async_computation.2 | async-start | bytes 262144 | tf_op jit(solution)/shard_map/all_to_all | solution.py:320
  55.0 0.0 collective-permute-done.1.pair_got
  55.1 1.9 %collective-permute-start.2 = (bf16[4,128,128]{2,1,0:T(8,128)(2,1)S(1)}, bf16[4,128,128]{2,1,0:T(8,128)(2,1)S(1)}, u32[]{:S(2)}, u32[]{:S(2)}) collective-permute-start(bf16[4,128,128]{2,1,0:T(8,128)(2,1)S(1)} %pair.1), channel_id=1, source_target_pairs={{0,16},{8,24},{16,0},{24,8},{32,48},{40,56},{48,32},{56,40},{1,17}... | collective-permute-start | bytes 393224 | tf_op jit(solution)/shard_map/ppermute | solution.py:323
  57.0 5.6 %collective-permute-done.2.quad_got = bf16[4,128,128]{2,1,0:T(8,128)(2,1)S(1)} collective-permute-done((bf16[4,128,128]{2,1,0:T(8,128)(2,1)S(1)}, bf16[4,128,128]{2,1,0:T(8,128)(2,1)S(1)}, u32[]{:S(2)}, u32[]{:S(2)}) %collective-permute-start.2) | collective-permute-done | bytes 131104 | tf_op jit(solution)/shard_map/ppermute | solution.py:323
  62.6 0.1 all-to-all-done.2.from_y
  62.8 1.4 %buckets.1 = (bf16[8,4,64,128]{3,2,1,0:T(8,128)(2,1)}, bf16[2,4,128,128]{3,2,1,0:T(8,128)(2,1)S(1)}) custom-call(s32[11]{0:T(128)S(1)} %pad_add_fusion.meta, bf16[2,64,128]{2,1,0:T(8,128)(2,1)S(1)} %get-tuple-element.50.halves, bf16[8,64,128]{2,1,0:T(8,128)(2,1)S(1)} %all-to-all-done.2.from_y, bf16[2,4,128,128]{3,2,1,0:T(8,128)(2,1)S(1)} %collective-permute-done.1.pair_got, ...), custom_call_target="tpu_custom_call" | custom-call | tf_op jit(solution)/shard_map/buckets/pallas_call | solution.py:403
  64.2 3.5 %all-to-all-start.3 = ((bf16[8,4,64,128]{3,2,1,0:T(8,128)(2,1)}), bf16[8,4,64,128]{3,2,1,0:T(8,128)(2,1)S(1)}, u32[]{:S(2)}, u32[]{:S(2)}) async-start(bf16[8,4,64,128]{3,2,1,0:T(8,128)(2,1)} %get-tuple-element.54), calls=%async_computation.3 | async-start | bytes 1048576 | tf_op jit(solution)/shard_map/all_to_all | solution.py:320
  67.7 2.8 %local.1 = (bf16[4,128,512]{2,1,0:T(8,128)(2,1)S(1)}, bf16[4,128,512]{2,1,0:T(8,128)(2,1)S(1)}, f32[32,256]{1,0:T(8,128)S(1)}) custom-call(s32[11]{0:T(128)S(1)} %pad_add_fusion.meta, bf16[4,128,512]{2,1,0:T(8,128)(2,1)S(1)} %get-tuple-element.38.own, bf16[4,128,512]{2,1,0:T(8,128)(2,1)S(1)} %collective-permute-done.other, ...), custom_call_target="tpu_custom_call" | custom-call | tf_op jit(solution)/shard_map/local/pallas_call | solution.py:391
  70.5 11.9 %all-to-all-done.3.got = bf16[8,4,64,128]{3,2,1,0:T(8,128)(2,1)S(1)} async-done(((bf16[8,4,64,128]{3,2,1,0:T(8,128)(2,1)}), bf16[8,4,64,128]{3,2,1,0:T(8,128)(2,1)S(1)}, u32[]{:S(2)}, u32[]{:S(2)}) %all-to-all-start.3) | async-done | bytes 524320 | tf_op jit(solution)/shard_map/all_to_all | solution.py:320
  82.4 1.6 %outputs.1 = (bf16[4,128,512]{2,1,0:T(8,128)(2,1)S(1)}, bf16[4,128,512]{2,1,0:T(8,128)(2,1)S(1)}, bf16[8,32,128]{2,1,0:T(8,128)(2,1)S(1)}) custom-call(s32[11]{0:T(128)S(1)} %pad_add_fusion.meta, bf16[4,128,512]{2,1,0:T(8,128)(2,1)S(1)} %get-tuple-element.38.own, ...), custom_call_target="tpu_custom_call", output_to_operand_aliasing={{0}: (5, {}), {1}: (6, {})} | custom-call | tf_op jit(solution)/shard_map/outputs/pallas_call | solution.py:412
  84.0 0.0 copy-start
  84.0 1.6 %grads.1 = (bf16[4,128,512]{2,1,0:T(8,128)(2,1)S(1)}, bf16[4,128,512]{2,1,0:T(8,128)(2,1)S(1)}) custom-call(s32[11]{0:T(128)S(1)} %pad_add_fusion.meta, bf16[4,128,512]{2,1,0:T(8,128)(2,1)S(1)} %get-tuple-element.38.own, bf16[4,128,512]{2,1,0:T(8,128)(2,1)S(1)} %collective-permute-done.other, ...), custom_call_target="tpu_custom_call", output_to_operand_aliasing={{0}: (4, {}), {1}: (5, {})} | custom-call | tf_op jit(solution)/shard_map/grads/pallas_call | solution.py:422
  85.6 5.6 %collective-permute-start.3 = (bf16[4,128,512]{2,1,0:T(8,128)(2,1)S(1)}, bf16[4,128,512]{2,1,0:T(8,128)(2,1)S(1)}, u32[]{:S(2)}, u32[]{:S(2)}) collective-permute-start(bf16[4,128,512]{2,1,0:T(8,128)(2,1)S(1)} %get-tuple-element.57), channel_id=1, source_target_pairs={{0,4},{4,0},{1,5},{5,1},{2,6},{6,2},{3,7},{7,3},{8,12},{12,8},{9,1... | collective-permute-start | bytes 1572872 | tf_op jit(solution)/shard_map/ppermute | solution.py:431
  91.2 7.4 %all_to_all.25.logit_grad = bf16[8,32,128]{2,1,0:T(8,128)(2,1)S(1)} all-to-all(bf16[8,32,128]{2,1,0:T(8,128)(2,1)S(1)} %get-tuple-element.59), channel_id=1, replica_groups=mesh['y'=8,'z'=8,'core'=2,'head'=4] {'core','head'}, dimensions={0} | all-to-all | bytes 131072 | tf_op jit(solution)/shard_map/all_to_all | solution.py:320
  98.6 0.0 copy-done
  98.7 1.5 %first.1 = (bf16[128,1024]{1,0:T(8,128)(2,1)}, bf16[128,1024]{1,0:T(8,128)(2,1)}, bf16[128,1024]{1,0:T(8,128)(2,1)}, bf16[128,1024]{1,0:T(8,128)(2,1)}, bf16[128,512]{1,0:T(8,128)(2,1)}) custom-call(bf16[4,128,512]{2,1,0:T(8,128)(2,1)S(1)} %get-tuple-element.58.keep, bf16[8,32,128]{2,1,0:T(8,128)(2,1)S(1)} %all_to_all.25.logit_grad, bf16[512,256]{1,0:T(8,128)(2,1)S(1)} %copy-done), custom_call_target="tpu_custom_call" | custom-call | tf_op jit(solution)/shard_map/first/pallas_call | solution.py:433
  100.2 0.0 collective-permute-done.3.got
  100.2 0.8 second.1
  (1 shorter events, 0.0 us)
Async XLA Ops:
  0.6 2.1 %copy-start.2 = (bf16[128,1024]{1,0:T(8,128)(2,1)S(1)}, bf16[128,1024]{1,0:T(8,128)(2,1)}, u32[]{:S(2)}) copy-start(bf16[128,1024]{1,0:T(8,128)(2,1)} %k.1) | copy-start | bytes 786436
  0.6 2.1 %copy-start.1 = (bf16[128,1024]{1,0:T(8,128)(2,1)S(1)}, bf16[128,1024]{1,0:T(8,128)(2,1)}, u32[]{:S(2)}) copy-start(bf16[128,1024]{1,0:T(8,128)(2,1)} %q.1) | copy-start | bytes 786436
  2.7 1.0 copy-start.3
  3.8 12.8 %collective-permute-start = (bf16[4,128,512]{2,1,0:T(8,128)(2,1)S(1)}, bf16[4,128,512]{2,1,0:T(8,128)(2,1)S(1)}, u32[]{:S(2)}, u32[]{:S(2)}) collective-permute-start(bf16[4,128,512]{2,1,0:T(8,128)(2,1)S(1)} %get-tuple-element.39), channel_id=1, source_target_pairs={{0,4},{4,0},{1,5},{5,1},{2,6},{6,2},{3,7},{7,3},{8,12},{12,8},{9,1... | collective-permute-start | bytes 1572872 | tf_op jit(solution)/shard_map/ppermute | solution.py:347
  12.5 8.5 %all-to-all-start = ((f32[8,32,128]{2,1,0:T(8,128)}), f32[8,32,128]{2,1,0:T(8,128)S(1)}, u32[]{:S(2)}, u32[]{:S(2)}) async-start(f32[8,32,128]{2,1,0:T(8,128)} %get-tuple-element.40), calls=%async_computation | async-start | bytes 262144 | tf_op jit(solution)/shard_map/all_to_all | solution.py:320
  15.9 0.7 copy-start.4
  23.4 23.5 %all-to-all-start.1 = ((bf16[8,4,64,128]{3,2,1,0:T(8,128)(2,1)}), bf16[8,4,64,128]{3,2,1,0:T(8,128)(2,1)S(1)}, u32[]{:S(2)}, u32[]{:S(2)}) async-start(bf16[8,4,64,128]{3,2,1,0:T(8,128)(2,1)} %get-tuple-element.49), calls=%async_computation.1 | async-start | bytes 1048576 | tf_op jit(solution)/shard_map/all_to_all | solution.py:320
  29.2 25.8 %collective-permute-start.1 = (bf16[2,4,128,128]{3,2,1,0:T(8,128)(2,1)S(1)}, bf16[2,4,128,128]{3,2,1,0:T(8,128)(2,1)S(1)}, u32[]{:S(2)}, u32[]{:S(2)}) collective-permute-start(bf16[2,4,128,128]{3,2,1,0:T(8,128)(2,1)S(1)} %get-tuple-element.52.pair), channel_id=1, source_target_pairs={{0,8},{8,0},{16,24},{24,16},{32,40},{40,32},{48,56},{56,48},{1,9},... | collective-permute-start | bytes 786440 | tf_op jit(solution)/shard_map/ppermute | solution.py:323
  48.2 14.6 %all-to-all-start.2 = ((bf16[8,64,128]{2,1,0:T(8,128)(2,1)}), bf16[8,64,128]{2,1,0:T(8,128)(2,1)S(1)}, u32[]{:S(2)}, u32[]{:S(2)}) async-start(bf16[8,64,128]{2,1,0:T(8,128)(2,1)} %get-tuple-element.51), calls=%async_computation.2 | async-start | bytes 262144 | tf_op jit(solution)/shard_map/all_to_all | solution.py:320
  55.1 7.6 %collective-permute-start.2 = (bf16[4,128,128]{2,1,0:T(8,128)(2,1)S(1)}, bf16[4,128,128]{2,1,0:T(8,128)(2,1)S(1)}, u32[]{:S(2)}, u32[]{:S(2)}) collective-permute-start(bf16[4,128,128]{2,1,0:T(8,128)(2,1)S(1)} %pair.1), channel_id=1, source_target_pairs={{0,16},{8,24},{16,0},{24,8},{32,48},{40,56},{48,32},{56,40},{1,17}... | collective-permute-start | bytes 393224 | tf_op jit(solution)/shard_map/ppermute | solution.py:323
  64.2 18.2 %all-to-all-start.3 = ((bf16[8,4,64,128]{3,2,1,0:T(8,128)(2,1)}), bf16[8,4,64,128]{3,2,1,0:T(8,128)(2,1)S(1)}, u32[]{:S(2)}, u32[]{:S(2)}) async-start(bf16[8,4,64,128]{3,2,1,0:T(8,128)(2,1)} %get-tuple-element.54), calls=%async_computation.3 | async-start | bytes 1048576 | tf_op jit(solution)/shard_map/all_to_all | solution.py:320
  84.0 14.7 %copy-start = (bf16[512,256]{1,0:T(8,128)(2,1)S(1)}, bf16[512,256]{1,0:T(8,128)(2,1)}, u32[]{:S(2)}) copy-start(bf16[512,256]{1,0:T(8,128)(2,1)} %gate.3) | copy-start | bytes 786436
  85.6 14.6 %collective-permute-start.3 = (bf16[4,128,512]{2,1,0:T(8,128)(2,1)S(1)}, bf16[4,128,512]{2,1,0:T(8,128)(2,1)S(1)}, u32[]{:S(2)}, u32[]{:S(2)}) collective-permute-start(bf16[4,128,512]{2,1,0:T(8,128)(2,1)S(1)} %get-tuple-element.57), channel_id=1, source_target_pairs={{0,4},{4,0},{1,5},{5,1},{2,6},{6,2},{3,7},{7,3},{8,12},{12,8},{9,1... | collective-permute-start | bytes 1572872 | tf_op jit(solution)/shard_map/ppermute | solution.py:431
